TPU v7x, 32 devices: a whole 2x2x4 slice. The times are simulated.
32 devices in a mesh: grp: 4 (over y, x), blk: 8 (over z, core).
Axes of the slice: x: 2, y: 2, z: 4, core: 2. Of those that a mesh axis runs over, the one named last changes fastest.
Arguments:
- queries: bfloat16 [4096, 1024], P(('grp', 'blk')), may hold values from -8 to 8
- key_rows: bfloat16 [4096, 128], P(('grp', 'blk')), may hold values from -8 to 8
- values: bfloat16 [4096, 128], P(('grp', 'blk')), may hold values from -6 to 6
- out_grad: bfloat16 [4096, 1024], P(('grp', 'blk')), may hold values from -6 to 6
- span_order: int32 [8], replicated, may hold values from 0 to 7, each once
Outputs:
- attended: bfloat16 [4096, 1024], P(('grp', 'blk'))
- grad_queries: bfloat16 [4096, 1024], P(('grp', 'blk'))
- grad_keys: bfloat16 [4096, 128], P(('grp', 'blk'))
- grad_values: bfloat16 [4096, 128], P(('grp', 'blk'))
Inputs may be any that keep to these rules, and one draw needn't show every extreme that they name: `span_order`: a permutation of 0 to 7.
All inputs are finite; a program needn't handle non-finite values.
Results may differ from a plain program's by a relative error of at most 0.015.
Values may be sent and summed in bfloat16 or wider, within the bound.
No kernel may reach another device: no remote copies, remote signals or barrier semaphores. Data moves between devices by JAX's collectives and lax.ppermute only.
A program may use at most 64 MiB of HBM per device.

v0:
```python
import functools
import math

import jax
import jax.numpy as jnp
from jax import lax
from jax.experimental import pallas as pl
from jax.experimental.pallas import tpu as pltpu
from jax.sharding import PartitionSpec as P

HEAD = 128
NEG_FILL = -1e30
F32 = jnp.float32
BF16 = jnp.bfloat16
NT = (((1,), (1,)), ((), ()))
FACTOR = 1.0 / math.sqrt(HEAD)
C2 = FACTOR * math.log2(math.e)
VMEM = pl.BlockSpec(memory_space=pltpu.VMEM)
SMEM = pl.BlockSpec(memory_space=pltpu.SMEM)


def dot(a, b):
    return jnp.dot(a, b, preferred_element_type=F32)


def dot_nt(a, b):
    return lax.dot_general(a, b, NT, preferred_element_type=F32)


def place(half, blk_count, span_ref):
    grp = lax.axis_index("grp")
    blk = lax.axis_index("blk")
    late = grp >= half
    even = lax.rem(blk, 2) == 0
    below = lax.rem(blk + blk_count - 1, blk_count)
    above = lax.rem(blk + 1, blk_count)
    mine = span_ref[blk]
    mate = span_ref[jnp.where(even, above, below)]
    off = span_ref[jnp.where(even, below, above)]
    return lax.rem(grp, half), late, late == (mate > mine), late == (off > mine)


def own_mask(keys, rows, idx):
    row = lax.broadcasted_iota(jnp.int32, (keys, 2 * rows), 0)
    col = lax.broadcasted_iota(jnp.int32, (keys, 2 * rows), 1)
    col = jnp.where(col >= rows, col - rows, col)
    return (row <= col) | ((row >= rows) & (row < (idx + 1) * rows))


def visit(see, run):
    if see is None:
        run()
    else:
        pl.when(see)(run)


def attend_group(units, sees, mask, qs, m_in, m_ref, w_ref, s_ref, finish):
    keys = units[0].shape[0]
    big = qs.shape[0]
    pair = min(big, 2 * HEAD)
    ones = jnp.ones((16, keys), BF16)
    for c in range(0, big, pair):
        cols = slice(c, c + pair)
        top = m_in[:, cols] if m_in is not None else jnp.full((1, pair), NEG_FILL, F32)
        for u, (kv, see) in enumerate(zip(units, sees)):
            s = dot_nt(kv[:, :HEAD], qs[cols, :]) * C2
            if u == 0 and mask is not None:
                s = jnp.where(mask, s, NEG_FILL)
            s_ref[u, :, cols] = s
            peak = jnp.max(s, axis=0, keepdims=True)
            top = jnp.maximum(top, peak if see is None else jnp.where(see, peak, NEG_FILL))
        m_ref[:, cols] = top
    vt = jnp.concatenate([jnp.concatenate([kv[:, HEAD:].T, ones], axis=0) for kv in units], axis=1)
    for c in range(0, big, pair):
        cols = slice(c, c + pair)
        top = m_ref[:, cols]
        for u, see in enumerate(sees):
            base = top if see is None else jnp.where(see, top, -NEG_FILL)
            w_ref[u * keys : (u + 1) * keys, cols] = jnp.exp2(s_ref[u, :, cols] - base).astype(BF16)
        summed = dot(vt, w_ref[:, cols])
        finish(cols, summed[:HEAD], summed[HEAD : HEAD + 1])


def near_kernel(
    half, blk_count, span_ref, q_ref, go_ref, so, sm, sf, o_ref, m_ref, l_ref, w_ref, qs, gs, s_ref
):
    idx, late, see_m, see_f = place(half, blk_count, span_ref)
    rows, width = q_ref.shape
    for h in range(width // HEAD):
        qs[h * rows : (h + 1) * rows, :] = q_ref[:, h * HEAD : (h + 1) * HEAD]
        gs[h * rows : (h + 1) * rows, :] = go_ref[:, h * HEAD : (h + 1) * HEAD]

    def finish(cols, summed, total):
        o_ref[:, cols] = summed
        l_ref[:, cols] = total

    mask = own_mask(so.shape[0], rows, idx)
    attend_group((so, sm, sf), (None, see_m, see_f), mask, qs, None, m_ref, w_ref, s_ref, finish)


def far_kernel(
    half, blk_count, span_ref, qs, gs, eo, em, ef, o_in, m_in, l_in,
    out_ref, w_ref, near_ref, far_ref, delta_ref, o_run, m_run, l_run, s_ref,
):
    idx, late, see_m, see_f = place(half, blk_count, span_ref)
    rows = out_ref.shape[0]
    big = qs.shape[0]
    pair = 2 * rows

    @pl.when(late)
    def _():
        def finish(cols, summed, total):
            alpha = jnp.exp2(m_in[:, cols] - m_run[:, cols])
            o_run[:, cols] = o_in[:, cols] * alpha + summed
            l_run[:, cols] = l_in[:, cols] * alpha + total

        attend_group((eo, em, ef), (None,) * 3, None, qs, m_in, m_run, w_ref, s_ref, finish)

    @pl.when(jnp.logical_not(late))
    def _():
        o_run[...] = o_in[...]
        m_run[...] = m_in[...]
        l_run[...] = l_in[...]

    ones = jnp.ones((8, HEAD), BF16)
    for p in range(big // pair):
        cols = slice(p * pair, (p + 1) * pair)
        inv = 1.0 / l_run[:, cols]
        far_ref[:, cols] = inv
        near_ref[:, cols] = inv * jnp.exp2(m_in[:, cols] - m_run[:, cols])
        o16 = (o_run[:, cols] * inv).astype(BF16).T
        out_ref[:, 2 * p * HEAD : (2 * p + 1) * HEAD] = o16[:rows]
        out_ref[:, (2 * p + 1) * HEAD : (2 * p + 2) * HEAD] = o16[rows:]
        prod = o16.astype(F32) * gs[cols, :].astype(F32)
        high = prod.astype(BF16)
        low = (prod - high.astype(F32)).astype(BF16)
        delta_ref[:, cols] = (dot_nt(ones, high) + dot_nt(ones, low))[:1]


def backward_unit(qs, gs, w_ref, slot, scale_ref, delta_ref, kv, gkv, gq_run, first, p_ref, d_ref):
    keys = kv.shape[0]
    big = qs.shape[0]
    pair = min(big, 2 * HEAD)
    kt = kv[:, :HEAD].T
    for c in range(0, big, pair):
        cols = slice(c, c + pair)
        prob = w_ref[slot * keys : (slot + 1) * keys, cols].astype(F32) * scale_ref[:, cols]
        dp = dot_nt(kv[:, HEAD:], gs[cols, :])
        p_ref[:, cols] = prob.astype(BF16)
        d_ref[:, cols] = (prob * (dp - delta_ref[:, cols])).astype(BF16)
    gkv[:, :HEAD] = (dot(d_ref[...], qs[...]) * FACTOR).astype(BF16)
    gkv[:, HEAD:] = dot(p_ref[...], gs[...]).astype(BF16)
    gq_run[...] = first[...] + dot(kt, d_ref[...])


def back_kernel(half, blk_count, which, span_ref, qs, gs, nw, fw, near_ref, far_ref, delta_ref, s_kv, e_kv, *refs):
    idx, late, see_m, see_f = place(half, blk_count, span_ref)
    if which == "off":
        gs_out, ge_out, gq_run, ps, ds, pe, de = refs
        slot, see = 2, see_f
        gq_run[...] = jnp.zeros_like(gq_run)
        first = gq_run
    elif which == "mate":
        first, gs_out, ge_out, gq_run, ps, ds, pe, de = refs
        slot, see = 1, see_m
    else:
        first, gs_out, ge_out, gq_ref, gq_run, ps, ds, pe, de = refs
        slot, see = 0, None
    if which == "mate":

        @pl.when(jnp.logical_not(see))
        def _():
            gq_run[...] = first[...]

    visit(
        see,
        functools.partial(
            backward_unit, qs, gs, nw, slot, near_ref, delta_ref, s_kv, gs_out, gq_run, first, ps, ds
        ),
    )
    visit(
        late,
        functools.partial(
            backward_unit, qs, gs, fw, slot, far_ref, delta_ref, e_kv, ge_out, gq_run, gq_run, pe, de
        ),
    )
    for gkv, shown in ((gs_out, see), (ge_out, late)):
        if shown is not None:

            @pl.when(jnp.logical_not(shown))
            def _(gkv=gkv):
                gkv[...] = jnp.zeros_like(gkv)

    if which == "own":
        rows = gq_ref.shape[0]
        for h in range(qs.shape[0] // rows):
            g16 = (gq_run[:, h * rows : (h + 1) * rows] * FACTOR).astype(BF16)
            gq_ref[:, h * HEAD : (h + 1) * HEAD] = g16.T


def like(shape, dtype):
    return jax.ShapeDtypeStruct(shape, dtype)


def call(kernel, name, outs, scratch, units, args):
    rows, width = args[1].shape
    keys = sum(u.shape[0] for u in units)
    work = 2 * keys * rows * width
    return pl.pallas_call(
        kernel,
        out_shape=outs,
        in_specs=[SMEM] + [VMEM] * (len(args) - 1),
        out_specs=[VMEM] * len(outs),
        scratch_shapes=scratch,
        cost_estimate=pl.CostEstimate(flops=4 * work, bytes_accessed=4 * rows * width, transcendentals=work // 256),
        compiler_params=pltpu.CompilerParams(vmem_limit_bytes=30 << 20),
        name=name,
    )(*args)


def body(queries, key_rows, values, out_grad, span_order):
    rows, width = queries.shape
    grp_count = lax.axis_size("grp")
    blk_count = lax.axis_size("blk")
    half = grp_count // 2
    unit = half * rows
    big = width // HEAD * rows
    wide, line = like((HEAD, big), F32), like((1, big), F32)
    tile = like((unit, 2 * HEAD), BF16)
    full = like((rows, width), BF16)
    wide_s, line_s = pltpu.VMEM((HEAD, big), F32), pltpu.VMEM((1, big), F32)

    def send(block, grp_to, blk_to):
        route = []
        for g in range(grp_count):
            for b in range(blk_count):
                to = grp_to(g)
                if to is not None:
                    route.append((g * blk_count + b, to * blk_count + blk_to(b) % blk_count))
        return lax.ppermute(block, ("grp", "blk"), route)

    same = lambda i: i
    on_chip = lambda block: send(block, same, lambda b: b ^ 1)
    off_chip = lambda block: send(block, same, lambda b: b + 1 if b % 2 else b - 1)
    ring_up = lambda block: send(block, lambda g: g // half * half + (g + 1) % half, same)
    ring_down = lambda block: send(block, lambda g: g // half * half + (g - 1) % half, same)
    to_late = lambda block: send(block, lambda g: g + half if g < half else None, same)
    to_early = lambda block: send(block, lambda g: g - half if g >= half else None, same)

    def gathered(block):
        parts = [block]
        for _ in range(half - 1):
            parts.append(ring_up(parts[-1]))
        return jnp.concatenate(parts, axis=0)

    def scattered(block):
        slots = [block[s * rows : (s + 1) * rows] for s in range(half)]
        total = slots[-1]
        for s in range(half - 2, -1, -1):
            total = add(ring_down(total), slots[s])
        return total

    add = lambda a, b: (a.astype(F32) + b.astype(F32)).astype(BF16)
    own = jnp.concatenate([key_rows, values], axis=1)
    off = off_chip(own)
    so = gathered(own)
    sf = gathered(off)
    sm = on_chip(so)
    eo = to_late(so)
    ef = to_late(sf)
    em = on_chip(eo)

    stack = like((big, HEAD), BF16)
    weights = like((3 * unit, big), BF16)
    scores = pltpu.VMEM((3, unit, big), F32)
    o_run, m_run, l_run, nw, qs, gs = call(
        functools.partial(near_kernel, half, blk_count), "near", [wide, line, line, weights, stack, stack], [scores],
        [so, sm, sf], [span_order, queries, out_grad, so, sm, sf],
    )
    out, fw, near, far, delta = call(
        functools.partial(far_kernel, half, blk_count), "far", [full, weights, line, line, line],
        [wide_s, line_s, line_s, scores],
        [eo, em, ef], [span_order, qs, gs, eo, em, ef, o_run, m_run, l_run],
    )

    state = [span_order, qs, gs, nw, fw, near, far, delta]
    back = lambda which: functools.partial(back_kernel, half, blk_count, which)
    temp = [pltpu.VMEM((unit, big), BF16)] * 4
    gsf, gef, gq = call(back("off"), "back_off", [tile, tile, wide], temp, [sf, ef], state + [sf, ef])
    gsm, gem, gq = call(back("mate"), "back_mate", [tile, tile, wide], temp, [sm, em], state + [sm, em, gq])
    gso, geo, gq = call(back("own"), "back_own", [tile, tile, full], [wide_s] + temp, [so, eo], state + [so, eo, gq])

    gsf = add(gsf, to_early(gef))
    total_f = scattered(gsf)
    ret_f = off_chip(total_f)
    mate = on_chip(jnp.concatenate([gsm, gem], axis=0))
    geo = add(geo, mate[unit:])
    gso = gso.astype(F32) + mate[:unit].astype(F32)
    gso = (gso + to_early(geo).astype(F32)).astype(BF16)
    final = add(scattered(gso), ret_f)
    return (out, gq, final[:, :HEAD], final[:, HEAD:])


def solution(mesh):
    spec = P(("grp", "blk"), None)
    return jax.shard_map(
        body,
        mesh=mesh,
        in_specs=(spec, spec, spec, spec, P()),
        out_specs=(spec, spec, spec, spec),
        check_vma=False,
    )
```

profile of v0, /device:TPU:0, one launch (start us, length us, event | category | flops | bytes accessed | tf_op | source)
XLA Modules:
  0.0 46.5 jit_solution(5364054588229293961)
XLA Ops:
  0.6 0.8 %constant_dynamic-update-slice_fusion.1 = bf16[128,256]{1,0:T(8,128)(2,1)S(1)} fusion(bf16[128,128]{1,0:T(8,128)(2,1)} %param.6), kind=kLoop, calls=%fused_computation.9 | loop fusion | bytes 65536
  1.4 0.8 %constant_dynamic-update-slice_fusion = bf16[128,256]{1,0:T(8,128)(2,1)S(1)} fusion(bf16[128,256]{1,0:T(8,128)(2,1)S(1)} %constant_dynamic-update-slice_fusion.1, bf16[128,128]{1,0:T(8,128)(2,1)} %param.7), kind=kLoop, calls=%fused_computation.8 | loop fusion | bytes 65536 | tf_op jit(solution)/shard_map/concatenate | solution.py:264
  2.2 3.0 %collective-permute-start = (bf16[128,256]{1,0:T(8,128)(2,1)S(1)}, bf16[128,256]{1,0:T(8,128)(2,1)S(1)}, u32[]{:S(2)}, u32[]{:S(2)}) collective-permute-start(bf16[128,256]{1,0:T(8,128)(2,1)S(1)} %constant_dynamic-update-slice_fusion), channel_id=1, source_target_pairs={{0,8},{1,9},{2,10},{3,11},{4,12},{5,13},{6,14},{7,15},{8,0},{9,1},... | collective-permute-start | bytes 196616 | tf_op jit(solution)/shard_map/ppermute | solution.py:240
  5.2 2.8 %collective-permute-start.2 = (bf16[128,256]{1,0:T(8,128)(2,1)S(1)}, bf16[128,256]{1,0:T(8,128)(2,1)S(1)}, u32[]{:S(2)}, u32[]{:S(2)}) collective-permute-start(bf16[128,256]{1,0:T(8,128)(2,1)S(1)} %constant_dynamic-update-slice_fusion), channel_id=1, source_target_pairs={{0,7},{1,2},{2,1},{3,4},{4,3},{5,6},{6,5},{7,0},{8,15},{9,10},{10,... | collective-permute-start | bytes 196616 | tf_op jit(solution)/shard_map/ppermute | solution.py:240
  8.0 3.4 %collective-permute-start.4 = (bf16[256,256]{1,0:T(8,128)(2,1)S(1)}, bf16[256,256]{1,0:T(8,128)(2,1)S(1)}, u32[]{:S(2)}, u32[]{:S(2)}) collective-permute-start(bf16[256,256]{1,0:T(8,128)(2,1)S(1)} %pad_maximum_fusion.1.so.s_kv), channel_id=1, source_target_pairs={{0,16},{1,17},{2,18},{3,19},{4,20},{5,21},{6,22},{7,23},{8,24},{9,... | collective-permute-start | bytes 393224 | tf_op jit(solution)/shard_map/ppermute | solution.py:240
  11.5 1.6 %collective-permute-start.3 = (bf16[128,256]{1,0:T(8,128)(2,1)S(1)}, bf16[128,256]{1,0:T(8,128)(2,1)S(1)}, u32[]{:S(2)}, u32[]{:S(2)}) collective-permute-start(bf16[128,256]{1,0:T(8,128)(2,1)S(1)} %collective-permute-done.2), channel_id=1, source_target_pairs={{0,8},{1,9},{2,10},{3,11},{4,12},{5,13},{6,14},{7,15},{8,0},{9,1},... | collective-permute-start | bytes 196616 | tf_op jit(solution)/shard_map/ppermute | solution.py:240
  13.1 2.9 %collective-permute-done.3 = bf16[128,256]{1,0:T(8,128)(2,1)S(1)} collective-permute-done((bf16[128,256]{1,0:T(8,128)(2,1)S(1)}, bf16[128,256]{1,0:T(8,128)(2,1)S(1)}, u32[]{:S(2)}, u32[]{:S(2)}) %collective-permute-start.3) | collective-permute-done | bytes 65568 | tf_op jit(solution)/shard_map/ppermute | solution.py:240
  16.0 2.7 %collective-permute-start.6 = (bf16[256,256]{1,0:T(8,128)(2,1)S(1)}, bf16[256,256]{1,0:T(8,128)(2,1)S(1)}, u32[]{:S(2)}, u32[]{:S(2)}) collective-permute-start(bf16[256,256]{1,0:T(8,128)(2,1)S(1)} %constant_dynamic-update-slice_fusion.2.sf.s_kv), channel_id=1, source_target_pairs={{0,16},{1,17},{2,18},{3,19},{4,20},{5,21},{6,22},{7,23},{8,24},{9,... | collective-permute-start | bytes 393224 | tf_op jit(solution)/shard_map/ppermute | solution.py:240
  18.8 0.6 %copy-done = s32[8]{0:T(128)S(1)} copy-done((s32[8]{0:T(128)S(1)}, s32[8]{0:T(128)}, u32[]{:S(2)}) %copy-start) | copy-done | bytes 56
  19.5 0.9 %copy-done.1 = bf16[128,1024]{1,0:T(8,128)(2,1)S(1)} copy-done((bf16[128,1024]{1,0:T(8,128)(2,1)S(1)}, bf16[128,1024]{1,0:T(8,128)(2,1)}, u32[]{:S(2)}) %copy-start.1) | copy-done | bytes 262168
  20.4 0.9 %copy-done.2 = bf16[128,1024]{1,0:T(8,128)(2,1)S(1)} copy-done((bf16[128,1024]{1,0:T(8,128)(2,1)S(1)}, bf16[128,1024]{1,0:T(8,128)(2,1)}, u32[]{:S(2)}) %copy-start.2) | copy-done | bytes 262168
  21.4 2.0 %near.1 = (f32[128,1024]{1,0:T(8,128)S(1)}, f32[1,1024]{1,0:T(1,128)S(1)}, f32[1,1024]{1,0:T(1,128)S(1)}, bf16[768,1024]{1,0:T(8,128)(2,1)S(1)}, bf16[1024,128]{...) custom-call(s32[8]{0:T(128)S(1)} %copy-done, bf16[128,1024]{1,0:T(8,128)(2,1)S(1)} %copy-done.1, ...), custom_call_target="tpu_custom_call" | custom-call | flops 805306368 | bytes 524288 | tf_op jit(solution)/shard_map/near/pallas_call | solution.py:209
  23.4 1.5 %far.1 = (bf16[128,1024]{1,0:T(8,128)(2,1)}, bf16[768,1024]{1,0:T(8,128)(2,1)S(1)}, f32[1,1024]{1,0:T(1,128)S(1)}, f32[1,1024]{1,0:T(1,128)S(1)}, f32[1,1024]{1,0:T(1,128)S(1)}) custom-call(s32[8]{0:T(128)S(1)} %copy-done, bf16[1024,128]{1,0:T(8,128)(2,1)S(1)} %get-tuple-element.24.qs, bf16[1024,128]{1,0:T(8,128)(2,1)S(1)} %get-tuple-element.25.gs, ...), custom_call_target="tpu_custom_call" | custom-call | flops 805306368 | bytes 524288 | tf_op jit(solution)/shard_map/far/pallas_call | solution.py:209
  24.9 1.3 %back_off.1 = (bf16[256,256]{1,0:T(8,128)(2,1)S(1)}, bf16[256,256]{1,0:T(8,128)(2,1)S(1)}, f32[128,1024]{1,0:T(8,128)S(1)}) custom-call(s32[8]{0:T(128)S(1)} %copy-done, bf16[1024,128]{1,0:T(8,128)(2,1)S(1)} %get-tuple-element.24.qs, bf16[1024,128]{1,0:T(8,128)(2,1)S(1)} %get-tuple-element.25.gs, bf16[768,1024]{1,0:T(8,128)(2,1)S(1)} %get-tuple-element.30.nw, ...), custom_call_target="tpu_custom_call" | custom-call | flops 536870912 | bytes 524288 | tf_op jit(solution)/shard_map/back_off/pallas_call | solution.py:209
  26.1 1.3 %collective-permute-start.10 = (bf16[256,256]{1,0:T(8,128)(2,1)S(1)}, bf16[256,256]{1,0:T(8,128)(2,1)S(1)}, u32[]{:S(2)}, u32[]{:S(2)}) collective-permute-start(bf16[256,256]{1,0:T(8,128)(2,1)S(1)} %get-tuple-element.43), channel_id=1, source_target_pairs={{16,0},{17,1},{18,2},{19,3},{20,4},{21,5},{22,6},{23,7},{24,8},{25... | collective-permute-start | bytes 393224 | tf_op jit(solution)/shard_map/ppermute | solution.py:240
  27.4 1.3 %back_mate.1 = (bf16[256,256]{1,0:T(8,128)(2,1)S(1)}, bf16[256,256]{1,0:T(8,128)(2,1)S(1)}, f32[128,1024]{1,0:T(8,128)S(1)}) custom-call(s32[8]{0:T(128)S(1)} %copy-done, bf16[1024,128]{1,0:T(8,128)(2,1)S(1)} %get-tuple-element.24.qs, bf16[1024,128]{1,0:T(8,128)(2,1)S(1)} %get-tuple-element.25.gs, bf16[768,1024]{1,0:T(8,128)(2,1)S(1)} %get-tuple-element.30.nw, ...), custom_call_target="tpu_custom_call" | custom-call | flops 536870912 | bytes 524288 | tf_op jit(solution)/shard_map/back_mate/pallas_call | solution.py:209
  28.8 2.0 %back_own.1 = (bf16[256,256]{1,0:T(8,128)(2,1)S(1)}, bf16[256,256]{1,0:T(8,128)(2,1)S(1)}, bf16[128,1024]{1,0:T(8,128)(2,1)}) custom-call(s32[8]{0:T(128)S(1)} %copy-done, bf16[1024,128]{1,0:T(8,128)(2,1)S(1)} %get-tuple-element.24.qs, bf16[1024,128]{1,0:T(8,128)(2,1)S(1)} %get-tuple-element.25.gs, bf16[768,1024]{1,0:T(8,128)(2,1)S(1)} %get-tuple-element.30.nw, ...), custom_call_target="tpu_custom_call" | custom-call | flops 536870912 | bytes 524288 | tf_op jit(solution)/shard_map/back_own/pallas_call | solution.py:209
  30.9 3.1 %collective-permute-done.10 = bf16[256,256]{1,0:T(8,128)(2,1)S(1)} collective-permute-done((bf16[256,256]{1,0:T(8,128)(2,1)S(1)}, bf16[256,256]{1,0:T(8,128)(2,1)S(1)}, u32[]{:S(2)}, u32[]{:S(2)}) %collective-permute-start.10) | collective-permute-done | bytes 131104 | tf_op jit(solution)/shard_map/ppermute | solution.py:240
  34.6 1.3 %collective-permute-start.8 = (bf16[256,256]{1,0:T(8,128)(2,1)S(1)}, bf16[256,256]{1,0:T(8,128)(2,1)S(1)}, u32[]{:S(2)}, u32[]{:S(2)}) collective-permute-start(bf16[256,256]{1,0:T(8,128)(2,1)S(1)} %add_convert_fusion.2), channel_id=1, source_target_pairs={{16,0},{17,1},{18,2},{19,3},{20,4},{21,5},{22,6},{23,7},{24,8},{25... | collective-permute-start | bytes 393224 | tf_op jit(solution)/shard_map/ppermute | solution.py:240
  35.9 2.4 %collective-permute-done.11 = bf16[128,256]{1,0:T(8,128)(2,1)S(1)} collective-permute-done((bf16[128,256]{1,0:T(8,128)(2,1)S(1)}, bf16[128,256]{1,0:T(8,128)(2,1)S(1)}, u32[]{:S(2)}, u32[]{:S(2)}) %collective-permute-start.11) | collective-permute-done | bytes 65568 | tf_op jit(solution)/shard_map/ppermute | solution.py:240
  38.4 3.1 %collective-permute-done.8 = bf16[256,256]{1,0:T(8,128)(2,1)S(1)} collective-permute-done((bf16[256,256]{1,0:T(8,128)(2,1)S(1)}, bf16[256,256]{1,0:T(8,128)(2,1)S(1)}, u32[]{:S(2)}, u32[]{:S(2)}) %collective-permute-start.8) | collective-permute-done | bytes 131104 | tf_op jit(solution)/shard_map/ppermute | solution.py:240
  41.6 1.6 %collective-permute-start.9 = (bf16[128,256]{1,0:T(8,128)(2,1)S(1)}, bf16[128,256]{1,0:T(8,128)(2,1)S(1)}, u32[]{:S(2)}, u32[]{:S(2)}) collective-permute-start(bf16[128,256]{1,0:T(8,128)(2,1)S(1)} %slice.34), channel_id=1, source_target_pairs={{0,8},{1,9},{2,10},{3,11},{4,12},{5,13},{6,14},{7,15},{8,0},{9,1},... | collective-permute-start | bytes 196616 | tf_op jit(solution)/shard_map/ppermute | solution.py:240
  43.1 0.8 %collective-permute-done.12 = bf16[128,256]{1,0:T(8,128)(2,1)S(1)} collective-permute-done((bf16[128,256]{1,0:T(8,128)(2,1)S(1)}, bf16[128,256]{1,0:T(8,128)(2,1)S(1)}, u32[]{:S(2)}, u32[]{:S(2)}) %collective-permute-start.12) | collective-permute-done | bytes 65568 | tf_op jit(solution)/shard_map/ppermute | solution.py:240
  43.9 2.0 %collective-permute-done.9 = bf16[128,256]{1,0:T(8,128)(2,1)S(1)} collective-permute-done((bf16[128,256]{1,0:T(8,128)(2,1)S(1)}, bf16[128,256]{1,0:T(8,128)(2,1)S(1)}, u32[]{:S(2)}, u32[]{:S(2)}) %collective-permute-start.9) | collective-permute-done | bytes 65568 | tf_op jit(solution)/shard_map/ppermute | solution.py:240
  (27 shorter events, 1.8 us)
Async XLA Ops:
  2.2 5.8 %collective-permute-start = (bf16[128,256]{1,0:T(8,128)(2,1)S(1)}, bf16[128,256]{1,0:T(8,128)(2,1)S(1)}, u32[]{:S(2)}, u32[]{:S(2)}) collective-permute-start(bf16[128,256]{1,0:T(8,128)(2,1)S(1)} %constant_dynamic-update-slice_fusion), channel_id=1, source_target_pairs={{0,8},{1,9},{2,10},{3,11},{4,12},{5,13},{6,14},{7,15},{8,0},{9,1},... | collective-permute-start | bytes 196616 | tf_op jit(solution)/shard_map/ppermute | solution.py:240
  5.2 6.3 %collective-permute-start.2 = (bf16[128,256]{1,0:T(8,128)(2,1)S(1)}, bf16[128,256]{1,0:T(8,128)(2,1)S(1)}, u32[]{:S(2)}, u32[]{:S(2)}) collective-permute-start(bf16[128,256]{1,0:T(8,128)(2,1)S(1)} %constant_dynamic-update-slice_fusion), channel_id=1, source_target_pairs={{0,7},{1,2},{2,1},{3,4},{4,3},{5,6},{6,5},{7,0},{8,15},{9,10},{10,... | collective-permute-start | bytes 196616 | tf_op jit(solution)/shard_map/ppermute | solution.py:240
  8.0 10.8 %collective-permute-start.4 = (bf16[256,256]{1,0:T(8,128)(2,1)S(1)}, bf16[256,256]{1,0:T(8,128)(2,1)S(1)}, u32[]{:S(2)}, u32[]{:S(2)}) collective-permute-start(bf16[256,256]{1,0:T(8,128)(2,1)S(1)} %pad_maximum_fusion.1.so.s_kv), channel_id=1, source_target_pairs={{0,16},{1,17},{2,18},{3,19},{4,20},{5,21},{6,22},{7,23},{8,24},{9,... | collective-permute-start | bytes 393224 | tf_op jit(solution)/shard_map/ppermute | solution.py:240
  11.4 7.4 %collective-permute-start.1 = (bf16[256,256]{1,0:T(8,128)(2,1)S(1)}, bf16[256,256]{1,0:T(8,128)(2,1)S(1)}, u32[]{:S(2)}, u32[]{:S(2)}) collective-permute-start(bf16[256,256]{1,0:T(8,128)(2,1)S(1)} %pad_maximum_fusion.1.so.s_kv), channel_id=1, source_target_pairs={{0,1},{1,0},{2,3},{3,2},{4,5},{5,4},{6,7},{7,6},{8,9},{9,8},{10,11... | collective-permute-start | bytes 393224 | tf_op jit(solution)/shard_map/ppermute | solution.py:240
  11.5 4.5 %collective-permute-start.3 = (bf16[128,256]{1,0:T(8,128)(2,1)S(1)}, bf16[128,256]{1,0:T(8,128)(2,1)S(1)}, u32[]{:S(2)}, u32[]{:S(2)}) collective-permute-start(bf16[128,256]{1,0:T(8,128)(2,1)S(1)} %collective-permute-done.2), channel_id=1, source_target_pairs={{0,8},{1,9},{2,10},{3,11},{4,12},{5,13},{6,14},{7,15},{8,0},{9,1},... | collective-permute-start | bytes 196616 | tf_op jit(solution)/shard_map/ppermute | solution.py:240
  16.0 7.4 %collective-permute-start.6 = (bf16[256,256]{1,0:T(8,128)(2,1)S(1)}, bf16[256,256]{1,0:T(8,128)(2,1)S(1)}, u32[]{:S(2)}, u32[]{:S(2)}) collective-permute-start(bf16[256,256]{1,0:T(8,128)(2,1)S(1)} %constant_dynamic-update-slice_fusion.2.sf.s_kv), channel_id=1, source_target_pairs={{0,16},{1,17},{2,18},{3,19},{4,20},{5,21},{6,22},{7,23},{8,24},{9,... | collective-permute-start | bytes 393224 | tf_op jit(solution)/shard_map/ppermute | solution.py:240
  18.7 4.7 %collective-permute-start.5 = (bf16[256,256]{1,0:T(8,128)(2,1)S(1)}, bf16[256,256]{1,0:T(8,128)(2,1)S(1)}, u32[]{:S(2)}, u32[]{:S(2)}) collective-permute-start(bf16[256,256]{1,0:T(8,128)(2,1)S(1)} %collective-permute-done.4.eo.e_kv), channel_id=1, source_target_pairs={{0,1},{1,0},{2,3},{3,2},{4,5},{5,4},{6,7},{7,6},{8,9},{9,8},{10,11... | collective-permute-start | bytes 393224 | tf_op jit(solution)/shard_map/ppermute | solution.py:240
  18.8 0.7 %copy-start = (s32[8]{0:T(128)S(1)}, s32[8]{0:T(128)}, u32[]{:S(2)}) copy-start(s32[8]{0:T(128)} %span_ref.9) | copy-start | bytes 100
  19.5 0.9 %copy-start.1 = (bf16[128,1024]{1,0:T(8,128)(2,1)S(1)}, bf16[128,1024]{1,0:T(8,128)(2,1)}, u32[]{:S(2)}) copy-start(bf16[128,1024]{1,0:T(8,128)(2,1)} %q_ref.1) | copy-start | bytes 786436
  20.4 0.9 %copy-start.2 = (bf16[128,1024]{1,0:T(8,128)(2,1)S(1)}, bf16[128,1024]{1,0:T(8,128)(2,1)}, u32[]{:S(2)}) copy-start(bf16[128,1024]{1,0:T(8,128)(2,1)} %go_ref.1) | copy-start | bytes 786436
  26.1 7.8 %collective-permute-start.10 = (bf16[256,256]{1,0:T(8,128)(2,1)S(1)}, bf16[256,256]{1,0:T(8,128)(2,1)S(1)}, u32[]{:S(2)}, u32[]{:S(2)}) collective-permute-start(bf16[256,256]{1,0:T(8,128)(2,1)S(1)} %get-tuple-element.43), channel_id=1, source_target_pairs={{16,0},{17,1},{18,2},{19,3},{20,4},{21,5},{22,6},{23,7},{24,8},{25... | collective-permute-start | bytes 393224 | tf_op jit(solution)/shard_map/ppermute | solution.py:240
  28.7 5.9 %collective-permute-start.7 = (bf16[512,256]{1,0:T(8,128)(2,1)S(1)}, bf16[512,256]{1,0:T(8,128)(2,1)S(1)}, u32[]{:S(2)}, u32[]{:S(2)}) collective-permute-start(bf16[512,256]{1,0:T(8,128)(2,1)S(1)} %pad_maximum_fusion), channel_id=1, source_target_pairs={{0,1},{1,0},{2,3},{3,2},{4,5},{5,4},{6,7},{7,6},{8,9},{9,8},{10,11... | collective-permute-start | bytes 786440 | tf_op jit(solution)/shard_map/ppermute | solution.py:240
  34.0 4.3 %collective-permute-start.11 = (bf16[128,256]{1,0:T(8,128)(2,1)S(1)}, bf16[128,256]{1,0:T(8,128)(2,1)S(1)}, u32[]{:S(2)}, u32[]{:S(2)}) collective-permute-start(bf16[128,256]{1,0:T(8,128)(2,1)S(1)} %slice.36), channel_id=1, source_target_pairs={{0,8},{1,9},{2,10},{3,11},{4,12},{5,13},{6,14},{7,15},{8,0},{9,1},... | collective-permute-start | bytes 196616 | tf_op jit(solution)/shard_map/ppermute | solution.py:240
  34.6 6.9 %collective-permute-start.8 = (bf16[256,256]{1,0:T(8,128)(2,1)S(1)}, bf16[256,256]{1,0:T(8,128)(2,1)S(1)}, u32[]{:S(2)}, u32[]{:S(2)}) collective-permute-start(bf16[256,256]{1,0:T(8,128)(2,1)S(1)} %add_convert_fusion.2), channel_id=1, source_target_pairs={{16,0},{17,1},{18,2},{19,3},{20,4},{21,5},{22,6},{23,7},{24,8},{25... | collective-permute-start | bytes 393224 | tf_op jit(solution)/shard_map/ppermute | solution.py:240
  38.3 5.6 %collective-permute-start.12 = (bf16[128,256]{1,0:T(8,128)(2,1)S(1)}, bf16[128,256]{1,0:T(8,128)(2,1)S(1)}, u32[]{:S(2)}, u32[]{:S(2)}) collective-permute-start(bf16[128,256]{1,0:T(8,128)(2,1)S(1)} %add_convert_fusion.4), channel_id=1, source_target_pairs={{0,7},{1,2},{2,1},{3,4},{4,3},{5,6},{6,5},{7,0},{8,15},{9,10},{10,... | collective-permute-start | bytes 196616 | tf_op jit(solution)/shard_map/ppermute | solution.py:240
  41.6 4.3 %collective-permute-start.9 = (bf16[128,256]{1,0:T(8,128)(2,1)S(1)}, bf16[128,256]{1,0:T(8,128)(2,1)S(1)}, u32[]{:S(2)}, u32[]{:S(2)}) collective-permute-start(bf16[128,256]{1,0:T(8,128)(2,1)S(1)} %slice.34), channel_id=1, source_target_pairs={{0,8},{1,9},{2,10},{3,11},{4,12},{5,13},{6,14},{7,15},{8,0},{9,1},... | collective-permute-start | bytes 196616 | tf_op jit(solution)/shard_map/ppermute | solution.py:240
where the time goes:
time: 46.6 us; the launch traced here: 46.5 us
  starting transfers between devices  18.5 us (40%)
  waiting for transfers between devices  14.2 us (30%)
  Pallas kernels  8.02 us (17%)
  local copies, waits for them, and re-layouts  4.74 us (10%)
  between operations  0.82 us (2%)
    ppermute x13, starting transfers between devices, send(): return lax.ppermute(block, ('grp', 'blk'), route)  18.5 us
    ppermute x13, waiting for transfers between devices, send(): return lax.ppermute(block, ('grp', 'blk'), route)  14.2 us
    pallas_call x5, Pallas kernels, call(): pl.pallas_call(kernel, out_shape=outs, in_specs=[SMEM] + [VMEM] * (len(ar...  8.02 us
    unnamed x8, local copies, waits for them, and re-layouts  3.32 us
  transfers between devices with their start and end apart: 13, of which 6 were waited for; matrix products, arithmetic and copies ran while one was open for 0% of the time, Pallas kernels for 11%

commit v1 on v0

--- a/solution.py
+++ b/solution.py
@@ -7,6 +7,7 @@
 from jax.experimental import pallas as pl
 from jax.experimental.pallas import tpu as pltpu
 from jax.sharding import PartitionSpec as P
+
 
 HEAD = 128
 NEG_FILL = -1e30
@@ -84,7 +85,7 @@
 def near_kernel(
     half, blk_count, span_ref, q_ref, go_ref, so, sm, sf, o_ref, m_ref, l_ref, w_ref, qs, gs, s_ref
 ):
-    idx, late, see_m, see_f = place(half, blk_count, span_ref)
+    idx, _, see_m, see_f = place(half, blk_count, span_ref)
     rows, width = q_ref.shape
     for h in range(width // HEAD):
         qs[h * rows : (h + 1) * rows, :] = q_ref[:, h * HEAD : (h + 1) * HEAD]
@@ -102,7 +103,7 @@
     half, blk_count, span_ref, qs, gs, eo, em, ef, o_in, m_in, l_in,
     out_ref, w_ref, near_ref, far_ref, delta_ref, o_run, m_run, l_run, s_ref,
 ):
-    idx, late, see_m, see_f = place(half, blk_count, span_ref)
+    _, late, _, _ = place(half, blk_count, span_ref)
     rows = out_ref.shape[0]
     big = qs.shape[0]
     pair = 2 * rows
@@ -154,7 +155,7 @@
 
 
 def back_kernel(half, blk_count, which, span_ref, qs, gs, nw, fw, near_ref, far_ref, delta_ref, s_kv, e_kv, *refs):
-    idx, late, see_m, see_f = place(half, blk_count, span_ref)
+    _, late, see_m, see_f = place(half, blk_count, span_ref)
     if which == "off":
         gs_out, ge_out, gq_run, ps, ds, pe, de = refs
         slot, see = 2, see_f
@@ -202,7 +203,7 @@
     return jax.ShapeDtypeStruct(shape, dtype)
 
 
-def call(kernel, name, outs, scratch, units, args):
+def call(kernel, outs, scratch, units, args):
     rows, width = args[1].shape
     keys = sum(u.shape[0] for u in units)
     work = 2 * keys * rows * width
@@ -214,11 +215,10 @@
         scratch_shapes=scratch,
         cost_estimate=pl.CostEstimate(flops=4 * work, bytes_accessed=4 * rows * width, transcendentals=work // 256),
         compiler_params=pltpu.CompilerParams(vmem_limit_bytes=30 << 20),
-        name=name,
     )(*args)
 
 
-def body(queries, key_rows, values, out_grad, span_order):
+def step(queries, key_rows, values, out_grad, span_order):
     rows, width = queries.shape
     grp_count = lax.axis_size("grp")
     blk_count = lax.axis_size("blk")
@@ -257,11 +257,12 @@
         slots = [block[s * rows : (s + 1) * rows] for s in range(half)]
         total = slots[-1]
         for s in range(half - 2, -1, -1):
-            total = add(ring_down(total), slots[s])
+            moved = ring_down(total)
+            total = add(moved, slots[s])
         return total
 
     add = lambda a, b: (a.astype(F32) + b.astype(F32)).astype(BF16)
-    own = jnp.concatenate([key_rows, values], axis=1)
+    own = lax.optimization_barrier(jnp.concatenate([key_rows, values], axis=1))
     off = off_chip(own)
     so = gathered(own)
     sf = gathered(off)
@@ -274,11 +275,11 @@
     weights = like((3 * unit, big), BF16)
     scores = pltpu.VMEM((3, unit, big), F32)
     o_run, m_run, l_run, nw, qs, gs = call(
-        functools.partial(near_kernel, half, blk_count), "near", [wide, line, line, weights, stack, stack], [scores],
+        functools.partial(near_kernel, half, blk_count), [wide, line, line, weights, stack, stack], [scores],
         [so, sm, sf], [span_order, queries, out_grad, so, sm, sf],
     )
     out, fw, near, far, delta = call(
-        functools.partial(far_kernel, half, blk_count), "far", [full, weights, line, line, line],
+        functools.partial(far_kernel, half, blk_count), [full, weights, line, line, line],
         [wide_s, line_s, line_s, scores],
         [eo, em, ef], [span_order, qs, gs, eo, em, ef, o_run, m_run, l_run],
     )
@@ -286,17 +287,19 @@
     state = [span_order, qs, gs, nw, fw, near, far, delta]
     back = lambda which: functools.partial(back_kernel, half, blk_count, which)
     temp = [pltpu.VMEM((unit, big), BF16)] * 4
-    gsf, gef, gq = call(back("off"), "back_off", [tile, tile, wide], temp, [sf, ef], state + [sf, ef])
-    gsm, gem, gq = call(back("mate"), "back_mate", [tile, tile, wide], temp, [sm, em], state + [sm, em, gq])
-    gso, geo, gq = call(back("own"), "back_own", [tile, tile, full], [wide_s] + temp, [so, eo], state + [so, eo, gq])
-
-    gsf = add(gsf, to_early(gef))
+    gsf, gef, gq = call(back("off"), [tile, tile, wide], temp, [sf, ef], state + [sf, ef])
+    gsm, gem, gq = call(back("mate"), [tile, tile, wide], temp, [sm, em], state + [sm, em, gq])
+    gso, geo, gq = call(back("own"), [tile, tile, full], [wide_s] + temp, [so, eo], state + [so, eo, gq])
+
+    back_f = to_early(gef)
+    gsf = add(gsf, back_f)
     total_f = scattered(gsf)
     ret_f = off_chip(total_f)
     mate = on_chip(jnp.concatenate([gsm, gem], axis=0))
     geo = add(geo, mate[unit:])
+    back_o = to_early(geo)
     gso = gso.astype(F32) + mate[:unit].astype(F32)
-    gso = (gso + to_early(geo).astype(F32)).astype(BF16)
+    gso = (gso + back_o.astype(F32)).astype(BF16)
     final = add(scattered(gso), ret_f)
     return (out, gq, final[:, :HEAD], final[:, HEAD:])
 
@@ -304,7 +307,7 @@
 def solution(mesh):
     spec = P(("grp", "blk"), None)
     return jax.shard_map(
-        body,
+        step,
         mesh=mesh,
         in_specs=(spec, spec, spec, spec, P()),
         out_specs=(spec, spec, spec, spec),

time: 46.6 us -> 45.5 us (0.976)
  starting transfers between devices: 18.5 us -> 20.9 us
  waiting for transfers between devices: 14.2 us -> 12.6 us
  local copies, waits for them, and re-layouts: 4.74 us -> 3.2 us
  Pallas kernels: 8.02 us -> 6.73 us
  other arithmetic: 0.2 us -> 0.98 us
    ppermute x13, starting transfers between devices: 18.5 us -> 20.9 us  [send(): return lax.ppermute(block, ('grp', 'blk'), route)]
    ppermute x13, waiting for transfers between devices: 14.2 us -> 12.6 us  [send(): return lax.ppermute(block, ('grp', 'blk'), route)]
    pallas_call x5, Pallas kernels: 8.02 us -> 6.73 us  [call(): pl.pallas_call(kernel, out_shape=outs, in_specs=[SMEM] + [VMEM] * (len(ar...]
    concatenate x1 -> x2, other arithmetic: 0.02 us -> 0.8 us  [the longest x1 0.78 us: step(): own = lax.optimization_barrier(jnp.concatenate([key_rows, values], axis=1))]
    concatenate x1 -> x0, local copies, waits for them, and re-layouts: 0.77 us -> none  [body(): own = jnp.concatenate([key_rows, values], axis=1)]
    unnamed x8 -> x7, local copies, waits for them, and re-layouts: 3.32 us -> 2.55 us
  transfers between devices with their start and end apart: 13 -> 13, of which waited for: 6 -> 6; matrix products, arithmetic and copies ran while one was open for 0% -> 0% of each run, Pallas kernels for 11% -> 10%
where the time goes in v1:
time: 45.5 us; the launch traced here: 45.1 us
  starting transfers between devices  20.9 us (46%)
  waiting for transfers between devices  12.6 us (28%)
  Pallas kernels  6.73 us (15%)
  local copies, waits for them, and re-layouts  3.2 us (7%)
  other arithmetic  0.98 us (2%)
  between operations  0.81 us (2%)
    ppermute x13, starting transfers between devices, send(): return lax.ppermute(block, ('grp', 'blk'), route)  20.9 us
    ppermute x13, waiting for transfers between devices, send(): return lax.ppermute(block, ('grp', 'blk'), route)  12.6 us
    pallas_call x5, Pallas kernels, call(): pl.pallas_call(kernel, out_shape=outs, in_specs=[SMEM] + [VMEM] * (len(ar...  6.73 us
    unnamed x7, local copies, waits for them, and re-layouts  2.55 us
  transfers between devices with their start and end apart: 13, of which 6 were waited for; matrix products, arithmetic and copies ran while one was open for 0% of the time, Pallas kernels for 10%

profile of v1, /device:TPU:0, one launch (start us, length us, event | category | flops | bytes accessed | tf_op | source)
XLA Modules:
  0.0 45.1 jit_solution(13422703818594458481)
XLA Ops:
  0.6 0.8 %pad_maximum_fusion.2 = bf16[128,256]{1,0:T(8,128)(2,1)S(1)} fusion(bf16[128,128]{1,0:T(8,128)(2,1)} %param.7, bf16[128,128]{1,0:T(8,128)(2,1)} %param.6), kind=kLoop, calls=%fused_computation.8 | loop fusion | flops 131072 | bytes 131072 | tf_op jit(solution)/shard_map/concatenate | solution.py:265
  1.4 3.0 %collective-permute-start = (bf16[128,256]{1,0:T(8,128)(2,1)S(1)}, bf16[128,256]{1,0:T(8,128)(2,1)S(1)}, u32[]{:S(2)}, u32[]{:S(2)}) collective-permute-start(bf16[128,256]{1,0:T(8,128)(2,1)S(1)} %pad_maximum_fusion.2), channel_id=1, source_target_pairs={{0,8},{1,9},{2,10},{3,11},{4,12},{5,13},{6,14},{7,15},{8,0},{9,1},... | collective-permute-start | bytes 196616 | tf_op jit(solution)/shard_map/ppermute | solution.py:240
  4.4 2.8 %collective-permute-start.2 = (bf16[128,256]{1,0:T(8,128)(2,1)S(1)}, bf16[128,256]{1,0:T(8,128)(2,1)S(1)}, u32[]{:S(2)}, u32[]{:S(2)}) collective-permute-start(bf16[128,256]{1,0:T(8,128)(2,1)S(1)} %pad_maximum_fusion.2), channel_id=1, source_target_pairs={{0,7},{1,2},{2,1},{3,4},{4,3},{5,6},{6,5},{7,0},{8,15},{9,10},{10,... | collective-permute-start | bytes 196616 | tf_op jit(solution)/shard_map/ppermute | solution.py:240
  7.2 3.4 %collective-permute-start.4 = (bf16[256,256]{1,0:T(8,128)(2,1)S(1)}, bf16[256,256]{1,0:T(8,128)(2,1)S(1)}, u32[]{:S(2)}, u32[]{:S(2)}) collective-permute-start(bf16[256,256]{1,0:T(8,128)(2,1)S(1)} %pad_maximum_fusion.1.so.s_kv), channel_id=1, source_target_pairs={{0,16},{1,17},{2,18},{3,19},{4,20},{5,21},{6,22},{7,23},{8,24},{9,... | collective-permute-start | bytes 393224 | tf_op jit(solution)/shard_map/ppermute | solution.py:240
  10.8 1.6 %collective-permute-start.3 = (bf16[128,256]{1,0:T(8,128)(2,1)S(1)}, bf16[128,256]{1,0:T(8,128)(2,1)S(1)}, u32[]{:S(2)}, u32[]{:S(2)}) collective-permute-start(bf16[128,256]{1,0:T(8,128)(2,1)S(1)} %collective-permute-done.2), channel_id=1, source_target_pairs={{0,8},{1,9},{2,10},{3,11},{4,12},{5,13},{6,14},{7,15},{8,0},{9,1},... | collective-permute-start | bytes 196616 | tf_op jit(solution)/shard_map/ppermute | solution.py:240
  12.3 2.9 %collective-permute-done.3 = bf16[128,256]{1,0:T(8,128)(2,1)S(1)} collective-permute-done((bf16[128,256]{1,0:T(8,128)(2,1)S(1)}, bf16[128,256]{1,0:T(8,128)(2,1)S(1)}, u32[]{:S(2)}, u32[]{:S(2)}) %collective-permute-start.3) | collective-permute-done | bytes 65568 | tf_op jit(solution)/shard_map/ppermute | solution.py:240
  15.3 2.7 %collective-permute-start.6 = (bf16[256,256]{1,0:T(8,128)(2,1)S(1)}, bf16[256,256]{1,0:T(8,128)(2,1)S(1)}, u32[]{:S(2)}, u32[]{:S(2)}) collective-permute-start(bf16[256,256]{1,0:T(8,128)(2,1)S(1)} %constant_dynamic-update-slice_fusion.sf.s_kv), channel_id=1, source_target_pairs={{0,16},{1,17},{2,18},{3,19},{4,20},{5,21},{6,22},{7,23},{8,24},{9,... | collective-permute-start | bytes 393224 | tf_op jit(solution)/shard_map/ppermute | solution.py:240
  18.1 0.6 %copy-done = s32[8]{0:T(128)S(1)} copy-done((s32[8]{0:T(128)S(1)}, s32[8]{0:T(128)}, u32[]{:S(2)}) %copy-start) | copy-done | bytes 56
  18.7 0.9 %copy-done.1 = bf16[128,1024]{1,0:T(8,128)(2,1)S(1)} copy-done((bf16[128,1024]{1,0:T(8,128)(2,1)S(1)}, bf16[128,1024]{1,0:T(8,128)(2,1)}, u32[]{:S(2)}) %copy-start.1) | copy-done | bytes 262168
  19.7 0.9 %copy-done.2 = bf16[128,1024]{1,0:T(8,128)(2,1)S(1)} copy-done((bf16[128,1024]{1,0:T(8,128)(2,1)S(1)}, bf16[128,1024]{1,0:T(8,128)(2,1)}, u32[]{:S(2)}) %copy-start.2) | copy-done | bytes 262168
  20.6 2.0 %shard_map.84 = (f32[128,1024]{1,0:T(8,128)S(1)}, f32[1,1024]{1,0:T(1,128)S(1)}, f32[1,1024]{1,0:T(1,128)S(1)}, bf16[768,1024]{1,0:T(8,128)(2,1)S(1)}, bf16[1024...) custom-call(s32[8]{0:T(128)S(1)} %copy-done, bf16[128,1024]{1,0:T(8,128)(2,1)S(1)} %copy-done.1, ...), custom_call_target="tpu_custom_call" | custom-call | flops 805306368 | bytes 524288 | tf_op jit(solution)/shard_map/pallas_call | solution.py:210
  22.7 1.5 %shard_map.85 = (bf16[128,1024]{1,0:T(8,128)(2,1)}, bf16[768,1024]{1,0:T(8,128)(2,1)S(1)}, f32[1,1024]{1,0:T(1,128)S(1)}, f32[1,1024]{1,0:T(1,128)S(1)}, f32[1,1024]{1,0:T(1,128)S(1)}) custom-call(s32[8]{0:T(128)S(1)} %copy-done, bf16[1024,128]{1,0:T(8,128)(2,1)S(1)} %get-tuple-element.24.qs, bf16[1024,128]{1,0:T(8,128)(2,1)S(1)} %get-tuple-element.25.gs, ...), custom_call_target="tpu_custom_call" | custom-call | flops 805306368 | bytes 524288 | tf_op jit(solution)/shard_map/pallas_call | solution.py:210
  24.7 1.3 %collective-permute-start.10 = (bf16[256,256]{1,0:T(8,128)(2,1)S(1)}, bf16[256,256]{1,0:T(8,128)(2,1)S(1)}, u32[]{:S(2)}, u32[]{:S(2)}) collective-permute-start(bf16[256,256]{1,0:T(8,128)(2,1)S(1)} %get-tuple-element.43), channel_id=1, source_target_pairs={{16,0},{17,1},{18,2},{19,3},{20,4},{21,5},{22,6},{23,7},{24,8},{25... | collective-permute-start | bytes 393224 | tf_op jit(solution)/shard_map/ppermute | solution.py:240
  26.7 1.2 %collective-permute-start.7 = (bf16[512,256]{1,0:T(8,128)(2,1)S(1)}, bf16[512,256]{1,0:T(8,128)(2,1)S(1)}, u32[]{:S(2)}, u32[]{:S(2)}) collective-permute-start(bf16[512,256]{1,0:T(8,128)(2,1)S(1)} %pad_maximum_fusion), channel_id=1, source_target_pairs={{0,1},{1,0},{2,3},{3,2},{4,5},{5,4},{6,7},{7,6},{8,9},{9,8},{10,11... | collective-permute-start | bytes 786440 | tf_op jit(solution)/shard_map/ppermute | solution.py:240
  27.9 2.0 %shard_map.88 = (bf16[256,256]{1,0:T(8,128)(2,1)S(1)}, bf16[256,256]{1,0:T(8,128)(2,1)S(1)}, bf16[128,1024]{1,0:T(8,128)(2,1)}) custom-call(s32[8]{0:T(128)S(1)} %copy-done, bf16[1024,128]{1,0:T(8,128)(2,1)S(1)} %get-tuple-element.24.qs, bf16[1024,128]{1,0:T(8,128)(2,1)S(1)} %get-tuple-element.25.gs, bf16[768,1024]{1,0:T(8,128)(2,1)S(1)} %get-tuple-element.30.nw, ...), custom_call_target="tpu_custom_call" | custom-call | flops 536870912 | bytes 524288 | tf_op jit(solution)/shard_map/pallas_call | solution.py:210
  29.9 2.6 %collective-permute-done.10 = bf16[256,256]{1,0:T(8,128)(2,1)S(1)} collective-permute-done((bf16[256,256]{1,0:T(8,128)(2,1)S(1)}, bf16[256,256]{1,0:T(8,128)(2,1)S(1)}, u32[]{:S(2)}, u32[]{:S(2)}) %collective-permute-start.10) | collective-permute-done | bytes 131104 | tf_op jit(solution)/shard_map/ppermute | solution.py:240
  33.2 1.3 %collective-permute-start.8 = (bf16[256,256]{1,0:T(8,128)(2,1)S(1)}, bf16[256,256]{1,0:T(8,128)(2,1)S(1)}, u32[]{:S(2)}, u32[]{:S(2)}) collective-permute-start(bf16[256,256]{1,0:T(8,128)(2,1)S(1)} %add_convert_fusion.2), channel_id=1, source_target_pairs={{16,0},{17,1},{18,2},{19,3},{20,4},{21,5},{22,6},{23,7},{24,8},{25... | collective-permute-start | bytes 393224 | tf_op jit(solution)/shard_map/ppermute | solution.py:240
  34.5 2.4 %collective-permute-done.11 = bf16[128,256]{1,0:T(8,128)(2,1)S(1)} collective-permute-done((bf16[128,256]{1,0:T(8,128)(2,1)S(1)}, bf16[128,256]{1,0:T(8,128)(2,1)S(1)}, u32[]{:S(2)}, u32[]{:S(2)}) %collective-permute-start.11) | collective-permute-done | bytes 65568 | tf_op jit(solution)/shard_map/ppermute | solution.py:240
  36.9 1.3 %collective-permute-start.12 = (bf16[128,256]{1,0:T(8,128)(2,1)S(1)}, bf16[128,256]{1,0:T(8,128)(2,1)S(1)}, u32[]{:S(2)}, u32[]{:S(2)}) collective-permute-start(bf16[128,256]{1,0:T(8,128)(2,1)S(1)} %add_convert_fusion.4), channel_id=1, source_target_pairs={{0,7},{1,2},{2,1},{3,4},{4,3},{5,6},{6,5},{7,0},{8,15},{9,10},{10,... | collective-permute-start | bytes 196616 | tf_op jit(solution)/shard_map/ppermute | solution.py:240
  38.2 1.9 %collective-permute-done.8 = bf16[256,256]{1,0:T(8,128)(2,1)S(1)} collective-permute-done((bf16[256,256]{1,0:T(8,128)(2,1)S(1)}, bf16[256,256]{1,0:T(8,128)(2,1)S(1)}, u32[]{:S(2)}, u32[]{:S(2)}) %collective-permute-start.8) | collective-permute-done | bytes 131104 | tf_op jit(solution)/shard_map/ppermute | solution.py:240
  40.1 1.6 %collective-permute-start.9 = (bf16[128,256]{1,0:T(8,128)(2,1)S(1)}, bf16[128,256]{1,0:T(8,128)(2,1)S(1)}, u32[]{:S(2)}, u32[]{:S(2)}) collective-permute-start(bf16[128,256]{1,0:T(8,128)(2,1)S(1)} %slice.34), channel_id=1, source_target_pairs={{0,8},{1,9},{2,10},{3,11},{4,12},{5,13},{6,14},{7,15},{8,0},{9,1},... | collective-permute-start | bytes 196616 | tf_op jit(solution)/shard_map/ppermute | solution.py:240
  41.7 1.4 %collective-permute-done.12 = bf16[128,256]{1,0:T(8,128)(2,1)S(1)} collective-permute-done((bf16[128,256]{1,0:T(8,128)(2,1)S(1)}, bf16[128,256]{1,0:T(8,128)(2,1)S(1)}, u32[]{:S(2)}, u32[]{:S(2)}) %collective-permute-start.12) | collective-permute-done | bytes 65568 | tf_op jit(solution)/shard_map/ppermute | solution.py:240
  43.1 1.3 %collective-permute-done.9 = bf16[128,256]{1,0:T(8,128)(2,1)S(1)} collective-permute-done((bf16[128,256]{1,0:T(8,128)(2,1)S(1)}, bf16[128,256]{1,0:T(8,128)(2,1)S(1)}, u32[]{:S(2)}, u32[]{:S(2)}) %collective-permute-start.9) | collective-permute-done | bytes 65568 | tf_op jit(solution)/shard_map/ppermute | solution.py:240
  44.5 0.6 %fusion = (bf16[128,128]{1,0:T(8,128)(2,1)}, bf16[128,128]{1,0:T(8,128)(2,1)}) fusion(bf16[128,256]{1,0:T(8,128)(2,1)S(1)} %add_convert_fusion.3), kind=kLoop, calls=%fused_computation.11 | loop fusion | bytes 131072 | tf_op jit(solution)/shard_map/slice | solution.py:304
  (26 shorter events, 2.2 us)
Async XLA Ops:
  1.4 5.8 %collective-permute-start = (bf16[128,256]{1,0:T(8,128)(2,1)S(1)}, bf16[128,256]{1,0:T(8,128)(2,1)S(1)}, u32[]{:S(2)}, u32[]{:S(2)}) collective-permute-start(bf16[128,256]{1,0:T(8,128)(2,1)S(1)} %pad_maximum_fusion.2), channel_id=1, source_target_pairs={{0,8},{1,9},{2,10},{3,11},{4,12},{5,13},{6,14},{7,15},{8,0},{9,1},... | collective-permute-start | bytes 196616 | tf_op jit(solution)/shard_map/ppermute | solution.py:240
  4.4 6.3 %collective-permute-start.2 = (bf16[128,256]{1,0:T(8,128)(2,1)S(1)}, bf16[128,256]{1,0:T(8,128)(2,1)S(1)}, u32[]{:S(2)}, u32[]{:S(2)}) collective-permute-start(bf16[128,256]{1,0:T(8,128)(2,1)S(1)} %pad_maximum_fusion.2), channel_id=1, source_target_pairs={{0,7},{1,2},{2,1},{3,4},{4,3},{5,6},{6,5},{7,0},{8,15},{9,10},{10,... | collective-permute-start | bytes 196616 | tf_op jit(solution)/shard_map/ppermute | solution.py:240
  7.2 10.8 %collective-permute-start.4 = (bf16[256,256]{1,0:T(8,128)(2,1)S(1)}, bf16[256,256]{1,0:T(8,128)(2,1)S(1)}, u32[]{:S(2)}, u32[]{:S(2)}) collective-permute-start(bf16[256,256]{1,0:T(8,128)(2,1)S(1)} %pad_maximum_fusion.1.so.s_kv), channel_id=1, source_target_pairs={{0,16},{1,17},{2,18},{3,19},{4,20},{5,21},{6,22},{7,23},{8,24},{9,... | collective-permute-start | bytes 393224 | tf_op jit(solution)/shard_map/ppermute | solution.py:240
  10.7 7.4 %collective-permute-start.1 = (bf16[256,256]{1,0:T(8,128)(2,1)S(1)}, bf16[256,256]{1,0:T(8,128)(2,1)S(1)}, u32[]{:S(2)}, u32[]{:S(2)}) collective-permute-start(bf16[256,256]{1,0:T(8,128)(2,1)S(1)} %pad_maximum_fusion.1.so.s_kv), channel_id=1, source_target_pairs={{0,1},{1,0},{2,3},{3,2},{4,5},{5,4},{6,7},{7,6},{8,9},{9,8},{10,11... | collective-permute-start | bytes 393224 | tf_op jit(solution)/shard_map/ppermute | solution.py:240
  10.8 4.5 %collective-permute-start.3 = (bf16[128,256]{1,0:T(8,128)(2,1)S(1)}, bf16[128,256]{1,0:T(8,128)(2,1)S(1)}, u32[]{:S(2)}, u32[]{:S(2)}) collective-permute-start(bf16[128,256]{1,0:T(8,128)(2,1)S(1)} %collective-permute-done.2), channel_id=1, source_target_pairs={{0,8},{1,9},{2,10},{3,11},{4,12},{5,13},{6,14},{7,15},{8,0},{9,1},... | collective-permute-start | bytes 196616 | tf_op jit(solution)/shard_map/ppermute | solution.py:240
  15.3 7.4 %collective-permute-start.6 = (bf16[256,256]{1,0:T(8,128)(2,1)S(1)}, bf16[256,256]{1,0:T(8,128)(2,1)S(1)}, u32[]{:S(2)}, u32[]{:S(2)}) collective-permute-start(bf16[256,256]{1,0:T(8,128)(2,1)S(1)} %constant_dynamic-update-slice_fusion.sf.s_kv), channel_id=1, source_target_pairs={{0,16},{1,17},{2,18},{3,19},{4,20},{5,21},{6,22},{7,23},{8,24},{9,... | collective-permute-start | bytes 393224 | tf_op jit(solution)/shard_map/ppermute | solution.py:240
  18.0 4.7 %collective-permute-start.5 = (bf16[256,256]{1,0:T(8,128)(2,1)S(1)}, bf16[256,256]{1,0:T(8,128)(2,1)S(1)}, u32[]{:S(2)}, u32[]{:S(2)}) collective-permute-start(bf16[256,256]{1,0:T(8,128)(2,1)S(1)} %collective-permute-done.4.eo.e_kv), channel_id=1, source_target_pairs={{0,1},{1,0},{2,3},{3,2},{4,5},{5,4},{6,7},{7,6},{8,9},{9,8},{10,11... | collective-permute-start | bytes 393224 | tf_op jit(solution)/shard_map/ppermute | solution.py:240
  18.1 0.7 %copy-start = (s32[8]{0:T(128)S(1)}, s32[8]{0:T(128)}, u32[]{:S(2)}) copy-start(s32[8]{0:T(128)} %span_ref.9) | copy-start | bytes 100
  18.7 0.9 %copy-start.1 = (bf16[128,1024]{1,0:T(8,128)(2,1)S(1)}, bf16[128,1024]{1,0:T(8,128)(2,1)}, u32[]{:S(2)}) copy-start(bf16[128,1024]{1,0:T(8,128)(2,1)} %q_ref.1) | copy-start | bytes 786436
  19.7 0.9 %copy-start.2 = (bf16[128,1024]{1,0:T(8,128)(2,1)S(1)}, bf16[128,1024]{1,0:T(8,128)(2,1)}, u32[]{:S(2)}) copy-start(bf16[128,1024]{1,0:T(8,128)(2,1)} %go_ref.1) | copy-start | bytes 786436
  24.7 7.8 %collective-permute-start.10 = (bf16[256,256]{1,0:T(8,128)(2,1)S(1)}, bf16[256,256]{1,0:T(8,128)(2,1)S(1)}, u32[]{:S(2)}, u32[]{:S(2)}) collective-permute-start(bf16[256,256]{1,0:T(8,128)(2,1)S(1)} %get-tuple-element.43), channel_id=1, source_target_pairs={{16,0},{17,1},{18,2},{19,3},{20,4},{21,5},{22,6},{23,7},{24,8},{25... | collective-permute-start | bytes 393224 | tf_op jit(solution)/shard_map/ppermute | solution.py:240
  26.7 6.5 %collective-permute-start.7 = (bf16[512,256]{1,0:T(8,128)(2,1)S(1)}, bf16[512,256]{1,0:T(8,128)(2,1)S(1)}, u32[]{:S(2)}, u32[]{:S(2)}) collective-permute-start(bf16[512,256]{1,0:T(8,128)(2,1)S(1)} %pad_maximum_fusion), channel_id=1, source_target_pairs={{0,1},{1,0},{2,3},{3,2},{4,5},{5,4},{6,7},{7,6},{8,9},{9,8},{10,11... | collective-permute-start | bytes 786440 | tf_op jit(solution)/shard_map/ppermute | solution.py:240
  32.6 4.3 %collective-permute-start.11 = (bf16[128,256]{1,0:T(8,128)(2,1)S(1)}, bf16[128,256]{1,0:T(8,128)(2,1)S(1)}, u32[]{:S(2)}, u32[]{:S(2)}) collective-permute-start(bf16[128,256]{1,0:T(8,128)(2,1)S(1)} %slice.36), channel_id=1, source_target_pairs={{0,8},{1,9},{2,10},{3,11},{4,12},{5,13},{6,14},{7,15},{8,0},{9,1},... | collective-permute-start | bytes 196616 | tf_op jit(solution)/shard_map/ppermute | solution.py:240
  33.2 6.9 %collective-permute-start.8 = (bf16[256,256]{1,0:T(8,128)(2,1)S(1)}, bf16[256,256]{1,0:T(8,128)(2,1)S(1)}, u32[]{:S(2)}, u32[]{:S(2)}) collective-permute-start(bf16[256,256]{1,0:T(8,128)(2,1)S(1)} %add_convert_fusion.2), channel_id=1, source_target_pairs={{16,0},{17,1},{18,2},{19,3},{20,4},{21,5},{22,6},{23,7},{24,8},{25... | collective-permute-start | bytes 393224 | tf_op jit(solution)/shard_map/ppermute | solution.py:240
  36.9 6.2 %collective-permute-start.12 = (bf16[128,256]{1,0:T(8,128)(2,1)S(1)}, bf16[128,256]{1,0:T(8,128)(2,1)S(1)}, u32[]{:S(2)}, u32[]{:S(2)}) collective-permute-start(bf16[128,256]{1,0:T(8,128)(2,1)S(1)} %add_convert_fusion.4), channel_id=1, source_target_pairs={{0,7},{1,2},{2,1},{3,4},{4,3},{5,6},{6,5},{7,0},{8,15},{9,10},{10,... | collective-permute-start | bytes 196616 | tf_op jit(solution)/shard_map/ppermute | solution.py:240
  40.1 4.3 %collective-permute-start.9 = (bf16[128,256]{1,0:T(8,128)(2,1)S(1)}, bf16[128,256]{1,0:T(8,128)(2,1)S(1)}, u32[]{:S(2)}, u32[]{:S(2)}) collective-permute-start(bf16[128,256]{1,0:T(8,128)(2,1)S(1)} %slice.34), channel_id=1, source_target_pairs={{0,8},{1,9},{2,10},{3,11},{4,12},{5,13},{6,14},{7,15},{8,0},{9,1},... | collective-permute-start | bytes 196616 | tf_op jit(solution)/shard_map/ppermute | solution.py:240

commit v2 on v1

v2 whole, which is shorter than its diff:
```python
import functools
import math

import jax
import jax.numpy as jnp
from jax import lax
from jax.experimental import pallas as pl
from jax.experimental.pallas import tpu as pltpu
from jax.sharding import PartitionSpec as P


HEAD = 128
NEG_FILL = -1e30
F32 = jnp.float32
BF16 = jnp.bfloat16
NT = (((1,), (1,)), ((), ()))
FACTOR = 1.0 / math.sqrt(HEAD)
C2 = FACTOR * math.log2(math.e)
VMEM = pl.BlockSpec(memory_space=pltpu.VMEM)


def dot(a, b):
    return jnp.dot(a, b, preferred_element_type=F32)


def dot_nt(a, b):
    return lax.dot_general(a, b, NT, preferred_element_type=F32)


def biases(half, blk_count, span_ref):
    blk = lax.axis_index("blk")
    late = lax.axis_index("grp") >= half
    step = jnp.where(lax.rem(blk, 2) == 0, 1, -1)
    span = span_ref[...]
    ids = lax.broadcasted_iota(jnp.int32, span.shape, 1)
    pick = lambda b: jnp.sum(jnp.where(ids == lax.rem(b + blk_count, blk_count), span, 0), axis=1, keepdims=True)
    mine = pick(blk)
    sign = jnp.where(late, 1, -1)
    hidden = lambda other: jnp.where((pick(other) - mine) * sign > 0, 0.0, NEG_FILL)
    return hidden(blk + step), hidden(blk - step)


def is_late(half):
    return lax.axis_index("grp") >= half


def own_mask(keys, rows, idx):
    row = lax.broadcasted_iota(jnp.int32, (keys, 2 * rows), 0)
    col = lax.broadcasted_iota(jnp.int32, (keys, 2 * rows), 1)
    col = jnp.where(col >= rows, col - rows, col)
    return (row <= col) | ((row >= rows) & (row < (idx + 1) * rows))


def attend_group(units, bias, mask, qs, m_in, m_ref, w_ref, s_ref, finish):
    keys = units[0].shape[0]
    big = qs.shape[0]
    pair = min(big, 2 * HEAD)
    ones = jnp.ones((16, keys), BF16)
    for c in range(0, big, pair):
        cols = slice(c, c + pair)
        top = m_in[:, cols] if m_in is not None else jnp.full((1, pair), NEG_FILL, F32)
        for u, kv in enumerate(units):
            s = dot_nt(kv[:, :HEAD], qs[cols, :]) * C2
            if u == 0 and mask is not None:
                s = jnp.where(mask, s, NEG_FILL)
            s_ref[u, :, cols] = s
            peak = jnp.max(s, axis=0, keepdims=True)
            if u > 0 and bias is not None:
                peak = jnp.where(bias[u - 1] < 0.0, NEG_FILL, peak)
            top = jnp.maximum(top, peak)
        m_ref[:, cols] = top
    vt = jnp.concatenate([jnp.concatenate([kv[:, HEAD:].T, ones], axis=0) for kv in units], axis=1)
    for c in range(0, big, pair):
        cols = slice(c, c + pair)
        for u in range(len(units)):
            base = m_ref[:, cols]
            if u > 0 and bias is not None:
                base = jnp.where(bias[u - 1] < 0.0, -NEG_FILL, base)
            w_ref[u * keys : (u + 1) * keys, cols] = jnp.exp2(s_ref[u, :, cols] - base).astype(BF16)
        summed = dot(vt, w_ref[:, cols])
        finish(cols, summed[:HEAD], summed[HEAD : HEAD + 1])


def near_kernel(rows, half, blk_count, span_ref, qs, so, sm, sf, o_ref, m_ref, l_ref, w_ref, s_ref):
    idx = lax.rem(lax.axis_index("grp"), half)

    def finish(cols, summed, total):
        o_ref[:, cols] = summed
        l_ref[:, cols] = total

    mask = own_mask(so.shape[0], rows, idx)
    bias = biases(half, blk_count, span_ref)
    attend_group((so, sm, sf), bias, mask, qs, None, m_ref, w_ref, s_ref, finish)


def far_kernel(
    half, qs, gs, eo, em, ef, o_in, m_in, l_in,
    out_ref, w_ref, near_ref, far_ref, delta_ref, o_run, m_run, l_run, s_ref,
):
    late = is_late(half)
    rows = out_ref.shape[0]
    big = qs.shape[0]
    pair = 2 * rows

    @pl.when(late)
    def _():
        def finish(cols, summed, total):
            alpha = jnp.exp2(m_in[:, cols] - m_run[:, cols])
            o_run[:, cols] = o_in[:, cols] * alpha + summed
            l_run[:, cols] = l_in[:, cols] * alpha + total

        attend_group((eo, em, ef), None, None, qs, m_in, m_run, w_ref, s_ref, finish)

    @pl.when(jnp.logical_not(late))
    def _():
        o_run[...] = o_in[...]
        m_run[...] = m_in[...]
        l_run[...] = l_in[...]

    ones = jnp.ones((8, HEAD), BF16)
    for p in range(big // pair):
        cols = slice(p * pair, (p + 1) * pair)
        inv = 1.0 / l_run[:, cols]
        far_ref[:, cols] = inv
        near_ref[:, cols] = inv * jnp.exp2(m_in[:, cols] - m_run[:, cols])
        o16 = (o_run[:, cols] * inv).astype(BF16).T
        out_ref[:, 2 * p * HEAD : (2 * p + 1) * HEAD] = o16[:rows]
        out_ref[:, (2 * p + 1) * HEAD : (2 * p + 2) * HEAD] = o16[rows:]
        prod = o16.astype(F32) * gs[cols, :].astype(F32)
        high = prod.astype(BF16)
        low = (prod - high.astype(F32)).astype(BF16)
        delta_ref[:, cols] = (dot_nt(ones, high) + dot_nt(ones, low))[:1]


def backward_unit(qs, gs, w_ref, slot, scale_ref, delta_ref, kv, gkv, gq_run, first, p_ref, d_ref):
    keys = kv.shape[0]
    big = qs.shape[0]
    pair = min(big, 2 * HEAD)
    kt = kv[:, :HEAD].T
    for c in range(0, big, pair):
        cols = slice(c, c + pair)
        prob = w_ref[slot * keys : (slot + 1) * keys, cols].astype(F32) * scale_ref[:, cols]
        dp = dot_nt(kv[:, HEAD:], gs[cols, :])
        p_ref[:, cols] = prob.astype(BF16)
        d_ref[:, cols] = (prob * (dp - delta_ref[:, cols])).astype(BF16)
    gkv[:, :HEAD] = (dot(d_ref[...], qs[...]) * FACTOR).astype(BF16)
    gkv[:, HEAD:] = dot(p_ref[...], gs[...]).astype(BF16)
    more = dot(kt, d_ref[...])
    gq_run[...] = more if first is None else first[...] + more


def back_kernel(half, parts, has_first, last, qs, gs, delta_ref, *refs):
    late = is_late(half)
    refs = list(refs)
    take = lambda n: [refs.pop(0) for _ in range(n)]
    ins = [take(3) for _ in parts]
    first = take(1)[0] if has_first else None
    outs = take(1 + max(p[2] for p in parts))
    gq_ref = take(1)[0] if last else None
    gq_run = take(1)[0]
    keys = ins[0][2].shape[0]
    for i, ((far, slot, out, row), (w_ref, scale_ref, kv)) in enumerate(zip(parts, ins)):
        gkv = outs[out].at[row * keys : (row + 1) * keys, :]
        p_ref, d_ref = refs[2 * i], refs[2 * i + 1]
        base = first if i == 0 else gq_run
        run = functools.partial(
            backward_unit, qs, gs, w_ref, slot, scale_ref, delta_ref, kv, gkv, gq_run, base, p_ref, d_ref
        )
        if far:
            pl.when(late)(run)

            @pl.when(jnp.logical_not(late))
            def _(gkv=gkv, base=base):
                gkv[...] = jnp.zeros_like(gkv)
                if base is not gq_run:
                    gq_run[...] = jnp.zeros_like(gq_run) if base is None else base[...]
        else:
            run()
    if last:
        rows = gq_ref.shape[0]
        for h in range(qs.shape[0] // rows):
            g16 = (gq_run[:, h * rows : (h + 1) * rows] * FACTOR).astype(BF16)
            gq_ref[:, h * HEAD : (h + 1) * HEAD] = g16.T


def like(shape, dtype):
    return jax.ShapeDtypeStruct(shape, dtype)


def call(kernel, outs, scratch, keys, args, spec=VMEM):
    work = 2 * keys * HEAD * HEAD * 8
    return pl.pallas_call(
        kernel,
        out_shape=outs,
        in_specs=[spec] * len(args),
        out_specs=[VMEM] * len(outs),
        scratch_shapes=scratch,
        cost_estimate=pl.CostEstimate(flops=4 * work, bytes_accessed=1 << 20, transcendentals=work // 256),
        compiler_params=pltpu.CompilerParams(vmem_limit_bytes=30 << 20),
    )(*args)


def step(queries, key_rows, values, out_grad, span_order):
    rows, width = queries.shape
    grp_count = lax.axis_size("grp")
    blk_count = lax.axis_size("blk")
    half = grp_count // 2
    unit = half * rows
    big = width // HEAD * rows
    wide, line = like((HEAD, big), F32), like((1, big), F32)
    full = like((rows, width), BF16)
    wide_s, line_s = pltpu.VMEM((HEAD, big), F32), pltpu.VMEM((1, big), F32)

    def send(block, grp_to, blk_to):
        route = []
        for g in range(grp_count):
            for b in range(blk_count):
                to = grp_to(g)
                if to is not None:
                    route.append((g * blk_count + b, to * blk_count + blk_to(b) % blk_count))
        return lax.ppermute(block, ("grp", "blk"), route)

    same = lambda i: i
    on_chip = lambda block: send(block, same, lambda b: b ^ 1)
    off_chip = lambda block: send(block, same, lambda b: b + 1 if b % 2 else b - 1)
    ring_up = lambda block: send(block, lambda g: g // half * half + (g + 1) % half, same)
    ring_down = lambda block: send(block, lambda g: g // half * half + (g - 1) % half, same)
    across = lambda block: send(block, lambda g: (g + half) % grp_count, same)

    def gathered(block):
        parts = [block]
        for _ in range(half - 1):
            parts.append(ring_up(parts[-1]))
        return jnp.concatenate(parts, axis=0)

    def scattered(block):
        slots = [block[s * rows : (s + 1) * rows] for s in range(half)]
        total = slots[-1]
        for s in range(half - 2, -1, -1):
            moved = ring_down(total)
            total = add(moved, slots[s])
        return total

    add = lambda a, b: (a.astype(F32) + b.astype(F32)).astype(BF16)
    own = lax.optimization_barrier(jnp.concatenate([key_rows, values], axis=1))

    def stacked(x):
        x = jnp.transpose(x.reshape(rows, width // HEAD, HEAD), (1, 0, 2))
        return lax.optimization_barrier(x.reshape(big, HEAD))

    qs, gs = stacked(queries), stacked(out_grad)

    off = off_chip(own)
    so = gathered(own)
    sf = gathered(off)
    sm = on_chip(so)
    eo = across(so)
    ef = across(sf)
    em = on_chip(eo)

    weights = like((3 * unit, big), BF16)
    scores = pltpu.VMEM((3, unit, big), F32)
    o_run, m_run, l_run, nw = call(
        functools.partial(near_kernel, rows, half, blk_count), [wide, line, line, weights], [scores],
        3 * unit, [span_order.reshape(1, blk_count), qs, so, sm, sf],
    )
    out, fw, near, far, delta = call(
        functools.partial(far_kernel, half), [full, weights, line, line, line], [wide_s, line_s, line_s, scores],
        3 * unit, [qs, gs, eo, em, ef, o_run, m_run, l_run],
    )

    def back(parts, first, last=False):
        args = [qs, gs, delta]
        for far_part, slot, out_index, row, kv in parts:
            args += [fw, far, kv] if far_part else [nw, near, kv]
        if first is not None:
            args.append(first)
        shape = tuple(p[:4] for p in parts)
        sizes = [sum(p[2] == i for p in shape) for i in range(1 + max(p[2] for p in shape))]
        outs = [like((n * unit, 2 * HEAD), BF16) for n in sizes] + [full if last else wide]
        temp = ([wide_s] if last else []) + [pltpu.VMEM((unit, big), BF16)] * (2 * len(parts))
        kernel = functools.partial(back_kernel, half, shape, first is not None, last)
        return call(kernel, outs, temp, unit * len(parts), args)

    gef, gq = back([(True, 2, 0, 0, ef)], None)
    gm, gq = back([(True, 1, 0, 1, em), (False, 1, 0, 0, sm)], gq)
    geo, gsf, gq = back([(True, 0, 0, 0, eo), (False, 2, 1, 0, sf)], gq)
    gso, gq = back([(False, 0, 0, 0, so)], gq, last=True)

    back_f = across(gef)
    gsf = add(gsf, back_f)
    total_f = scattered(gsf)
    ret_f = off_chip(total_f)
    mate = on_chip(gm)
    geo = add(geo, mate[unit:])
    back_o = across(geo)
    gso = gso.astype(F32) + mate[:unit].astype(F32)
    gso = (gso + back_o.astype(F32)).astype(BF16)
    final = add(scattered(gso), ret_f)
    return (out, gq, final[:, :HEAD], final[:, HEAD:])


def solution(mesh):
    spec = P(("grp", "blk"), None)
    return jax.shard_map(
        step,
        mesh=mesh,
        in_specs=(spec, spec, spec, spec, P()),
        out_specs=(spec, spec, spec, spec),
        check_vma=False,
    )
```

time: 45.5 us -> 40.4 us (0.89)
  starting transfers between devices: 20.9 us -> 16.5 us
  waiting for transfers between devices: 12.6 us -> 15 us
  local copies, waits for them, and re-layouts: 3.2 us -> 1.71 us
  Pallas kernels: 6.73 us -> 5.28 us
    ppermute x13, starting transfers between devices: 20.9 us -> 16.5 us  [send(): return lax.ppermute(block, ('grp', 'blk'), route)]
    unnamed x7 -> x5, local copies, waits for them, and re-layouts: 2.55 us -> 0.02 us
    ppermute x13, waiting for transfers between devices: 12.6 us -> 15 us  [send(): return lax.ppermute(block, ('grp', 'blk'), route)]
    pallas_call x5 -> x6, Pallas kernels: 6.73 us -> 5.28 us  [call(): pl.pallas_call(kernel, out_shape=outs, in_specs=[spec] * len(args), out_s...]
    reshape x0 -> x2, local copies, waits for them, and re-layouts: none -> 1.04 us  [stacked(): x = jnp.transpose(x.reshape(rows, width // HEAD, HEAD), (1, 0, 2))]
  transfers between devices with their start and end apart: 13 -> 13, of which waited for: 6 -> 8; matrix products, arithmetic and copies ran while one was open for 0% -> 3% of each run, Pallas kernels for 10% -> 11%
where the time goes in v2:
time: 40.4 us; the launch traced here: 40.2 us
  starting transfers between devices  16.5 us (41%)
  waiting for transfers between devices  15 us (37%)
  Pallas kernels  5.28 us (13%)
  local copies, waits for them, and re-layouts  1.71 us (4%)
  other arithmetic  1 us (2%)
  between operations  0.77 us (2%)
    ppermute x13, starting transfers between devices, send(): return lax.ppermute(block, ('grp', 'blk'), route)  16.5 us
    ppermute x13, waiting for transfers between devices, send(): return lax.ppermute(block, ('grp', 'blk'), route)  15 us
    pallas_call x6, Pallas kernels, call(): pl.pallas_call(kernel, out_shape=outs, in_specs=[spec] * len(args), out_s...  5.28 us
    reshape x2, local copies, waits for them, and re-layouts, stacked(): x = jnp.transpose(x.reshape(rows, width // HEAD, HEAD), (1, 0, 2))  1.04 us
    concatenate x1, other arithmetic, step(): own = lax.optimization_barrier(jnp.concatenate([key_rows, values], axis=1))  0.82 us
  transfers between devices with their start and end apart: 13, of which 8 were waited for; matrix products, arithmetic and copies ran while one was open for 3% of the time, Pallas kernels for 11%

profile of v2, /device:TPU:0, one launch (start us, length us, event | category | flops | bytes accessed | tf_op | source)
XLA Modules:
  0.0 40.2 jit_solution(9800044151401226850)
XLA Ops:
  0.7 0.8 %pad_maximum_fusion.1 = bf16[128,256]{1,0:T(8,128)(2,1)S(1)} fusion(bf16[128,128]{1,0:T(8,128)(2,1)} %param.7, bf16[128,128]{1,0:T(8,128)(2,1)} %param.6), kind=kLoop, calls=%fused_computation.9 | loop fusion | flops 131072 | bytes 131072 | tf_op jit(solution)/shard_map/concatenate | solution.py:245
  1.5 4.6 %collective-permute-start.3 = (bf16[128,256]{1,0:T(8,128)(2,1)S(1)}, bf16[128,256]{1,0:T(8,128)(2,1)S(1)}, u32[]{:S(2)}, u32[]{:S(2)}) collective-permute-start(bf16[128,256]{1,0:T(8,128)(2,1)S(1)} %pad_maximum_fusion.1), channel_id=1, source_target_pairs={{0,7},{1,2},{2,1},{3,4},{4,3},{5,6},{6,5},{7,0},{8,15},{9,10},{10,... | collective-permute-start | bytes 196616 | tf_op jit(solution)/shard_map/ppermute | solution.py:221
  6.1 1.5 %collective-permute-start = (bf16[128,256]{1,0:T(8,128)(2,1)S(1)}, bf16[128,256]{1,0:T(8,128)(2,1)S(1)}, u32[]{:S(2)}, u32[]{:S(2)}) collective-permute-start(bf16[128,256]{1,0:T(8,128)(2,1)S(1)} %pad_maximum_fusion.1), channel_id=1, source_target_pairs={{0,8},{1,9},{2,10},{3,11},{4,12},{5,13},{6,14},{7,15},{8,0},{9,1},... | collective-permute-start | bytes 196616 | tf_op jit(solution)/shard_map/ppermute | solution.py:221
  7.6 2.7 %collective-permute-done = bf16[128,256]{1,0:T(8,128)(2,1)S(1)} collective-permute-done((bf16[128,256]{1,0:T(8,128)(2,1)S(1)}, bf16[128,256]{1,0:T(8,128)(2,1)S(1)}, u32[]{:S(2)}, u32[]{:S(2)}) %collective-permute-start) | collective-permute-done | bytes 65568 | tf_op jit(solution)/shard_map/ppermute | solution.py:221
  10.4 1.6 %collective-permute-start.1 = (bf16[256,256]{1,0:T(8,128)(2,1)S(1)}, bf16[256,256]{1,0:T(8,128)(2,1)S(1)}, u32[]{:S(2)}, u32[]{:S(2)}) collective-permute-start(bf16[256,256]{1,0:T(8,128)(2,1)S(1)} %pad_maximum_fusion.so.refs_2_), channel_id=1, source_target_pairs={{0,16},{1,17},{2,18},{3,19},{4,20},{5,21},{6,22},{7,23},{8,24},{9,... | collective-permute-start | bytes 393224 | tf_op jit(solution)/shard_map/ppermute | solution.py:221
  12.0 1.5 %collective-permute-start.4 = (bf16[128,256]{1,0:T(8,128)(2,1)S(1)}, bf16[128,256]{1,0:T(8,128)(2,1)S(1)}, u32[]{:S(2)}, u32[]{:S(2)}) collective-permute-start(bf16[128,256]{1,0:T(8,128)(2,1)S(1)} %collective-permute-done.3), channel_id=1, source_target_pairs={{0,8},{1,9},{2,10},{3,11},{4,12},{5,13},{6,14},{7,15},{8,0},{9,1},... | collective-permute-start | bytes 196616 | tf_op jit(solution)/shard_map/ppermute | solution.py:221
  13.5 2.8 %collective-permute-done.4 = bf16[128,256]{1,0:T(8,128)(2,1)S(1)} collective-permute-done((bf16[128,256]{1,0:T(8,128)(2,1)S(1)}, bf16[128,256]{1,0:T(8,128)(2,1)S(1)}, u32[]{:S(2)}, u32[]{:S(2)}) %collective-permute-start.4) | collective-permute-done | bytes 65568 | tf_op jit(solution)/shard_map/ppermute | solution.py:221
  16.3 0.5 %collective-permute-start.5 = (bf16[256,256]{1,0:T(8,128)(2,1)S(1)}, bf16[256,256]{1,0:T(8,128)(2,1)S(1)}, u32[]{:S(2)}, u32[]{:S(2)}) collective-permute-start(bf16[256,256]{1,0:T(8,128)(2,1)S(1)} %constant_dynamic-update-slice_fusion.sf.refs_5_), channel_id=1, source_target_pairs={{0,16},{1,17},{2,18},{3,19},{4,20},{5,21},{6,22},{7,23},{8,24},{9,... | collective-permute-start | bytes 393224 | tf_op jit(solution)/shard_map/ppermute | solution.py:221
  16.8 1.0 %copy_bitcast_fusion = bf16[128,8,128]{2,0,1:T(8,128)(2,1)S(1)} fusion(bf16[128,1024]{1,0:T(8,128)(2,1)} %param.8), kind=kLoop, calls=%fused_computation | loop fusion | bytes 524288 | tf_op jit(solution)/shard_map/reshape | solution.py:248
  17.8 1.4 %shard_map.84 = (f32[128,1024]{1,0:T(8,128)S(1)}, f32[1,1024]{1,0:T(1,128)S(1)}, f32[1,1024]{1,0:T(1,128)S(1)}, bf16[768,1024]{1,0:T(8,128)(2,1)S(1)}) custom-call(s32[1,8]{1,0:T(1,128)S(1)} %bitcast.28, bf16[1024,128]{1,0:T(8,128)(2,1)S(1)} %bitcast.17, bf16[256,256]{1,0:T(8,128)(2,1)S(1)} %pad_maximum_fusion.so.refs_2_, ...), custom_call_target="tpu_custom_call" | custom-call | flops 805306368 | bytes 1048576 | tf_op jit(solution)/shard_map/pallas_call | solution.py:192
  19.2 2.0 %collective-permute-done.5.ef.refs_2_ = bf16[256,256]{1,0:T(8,128)(2,1)S(1)} collective-permute-done((bf16[256,256]{1,0:T(8,128)(2,1)S(1)}, bf16[256,256]{1,0:T(8,128)(2,1)S(1)}, u32[]{:S(2)}, u32[]{:S(2)}) %collective-permute-start.5) | collective-permute-done | bytes 131104 | tf_op jit(solution)/shard_map/ppermute | solution.py:221
  21.2 0.9 %shard_map.85 = (bf16[128,1024]{1,0:T(8,128)(2,1)}, bf16[768,1024]{1,0:T(8,128)(2,1)S(1)}, f32[1,1024]{1,0:T(1,128)S(1)}, f32[1,1024]{1,0:T(1,128)S(1)}, f32[1,1024]{1,0:T(1,128)S(1)}) custom-call(bf16[1024,128]{1,0:T(8,128)(2,1)S(1)} %bitcast.18, bf16[1024,128]{1,0:T(8,128)(2,1)S(1)} %bitcast.23, bf16[256,256]{1,0:T(8,128)(2,1)S(1)} %collective-permute-done.1.eo.refs_2_, ...), custom_call_target="tpu_custom_call" | custom-call | flops 805306368 | bytes 1048576 | tf_op jit(solution)/shard_map/pallas_call | solution.py:192
  22.2 2.6 %collective-permute-start.10 = (bf16[256,256]{1,0:T(8,128)(2,1)S(1)}, bf16[256,256]{1,0:T(8,128)(2,1)S(1)}, u32[]{:S(2)}, u32[]{:S(2)}) collective-permute-start(bf16[256,256]{1,0:T(8,128)(2,1)S(1)} %get-tuple-element.39), channel_id=1, source_target_pairs={{0,16},{1,17},{2,18},{3,19},{4,20},{5,21},{6,22},{7,23},{8,24},{9,... | collective-permute-start | bytes 393224 | tf_op jit(solution)/shard_map/ppermute | solution.py:221
  24.9 0.7 %shard_map.87 = (bf16[512,256]{1,0:T(8,128)(2,1)S(1)}, f32[128,1024]{1,0:T(8,128)S(1)}) custom-call(bf16[1024,128]{1,0:T(8,128)(2,1)S(1)} %bitcast.20, bf16[1024,128]{1,0:T(8,128)(2,1)S(1)} %bitcast.25, f32[1,1024]{1,0:T(1,128)S(1)} %get-tuple-element.26.delta_ref, bf16[768,1024]{1,0:T(8,128)(2,1)S(1)} %get-tuple-element.29.refs_0_, ...), custom_call_target="tpu_custom_call" | custom-call | flops 536870912 | bytes 1048576 | tf_op jit(solution)/shard_map/pallas_call | solution.py:192
  25.7 0.7 %shard_map.88 = (bf16[256,256]{1,0:T(8,128)(2,1)S(1)}, bf16[256,256]{1,0:T(8,128)(2,1)S(1)}, f32[128,1024]{1,0:T(8,128)S(1)}) custom-call(bf16[1024,128]{1,0:T(8,128)(2,1)S(1)} %bitcast.21, bf16[1024,128]{1,0:T(8,128)(2,1)S(1)} %bitcast.26, f32[1,1024]{1,0:T(1,128)S(1)} %get-tuple-element.26.delta_ref, bf16[768,1024]{1,0:T(8,128)(2,1)S(1)} %get-tuple-element.29.refs_0_, ...), custom_call_target="tpu_custom_call" | custom-call | flops 536870912 | bytes 1048576 | tf_op jit(solution)/shard_map/pallas_call | solution.py:192
  26.4 1.5 %shard_map.89 = (bf16[256,256]{1,0:T(8,128)(2,1)S(1)}, bf16[128,1024]{1,0:T(8,128)(2,1)}) custom-call(bf16[1024,128]{1,0:T(8,128)(2,1)S(1)} %bitcast.22, bf16[1024,128]{1,0:T(8,128)(2,1)S(1)} %bitcast.27, f32[1,1024]{1,0:T(1,128)S(1)} %get-tuple-element.26.delta_ref, bf16[768,1024]{1,0:T(8,128)(2,1)S(1)} %get-tuple-element.27.refs_3_.refs_0_, ...), custom_call_target="tpu_custom_call" | custom-call | flops 268435456 | bytes 1048576 | tf_op jit(solution)/shard_map/pallas_call | solution.py:192
  28.1 1.6 %collective-permute-start.11 = (bf16[128,256]{1,0:T(8,128)(2,1)S(1)}, bf16[128,256]{1,0:T(8,128)(2,1)S(1)}, u32[]{:S(2)}, u32[]{:S(2)}) collective-permute-start(bf16[128,256]{1,0:T(8,128)(2,1)S(1)} %slice.36), channel_id=1, source_target_pairs={{0,8},{1,9},{2,10},{3,11},{4,12},{5,13},{6,14},{7,15},{8,0},{9,1},... | collective-permute-start | bytes 196616 | tf_op jit(solution)/shard_map/ppermute | solution.py:221
  29.7 1.8 %collective-permute-start.8 = (bf16[256,256]{1,0:T(8,128)(2,1)S(1)}, bf16[256,256]{1,0:T(8,128)(2,1)S(1)}, u32[]{:S(2)}, u32[]{:S(2)}) collective-permute-start(bf16[256,256]{1,0:T(8,128)(2,1)S(1)} %add_convert_fusion.2), channel_id=1, source_target_pairs={{0,16},{1,17},{2,18},{3,19},{4,20},{5,21},{6,22},{7,23},{8,24},{9,... | collective-permute-start | bytes 393224 | tf_op jit(solution)/shard_map/ppermute | solution.py:221
  31.5 0.9 %collective-permute-done.11 = bf16[128,256]{1,0:T(8,128)(2,1)S(1)} collective-permute-done((bf16[128,256]{1,0:T(8,128)(2,1)S(1)}, bf16[128,256]{1,0:T(8,128)(2,1)S(1)}, u32[]{:S(2)}, u32[]{:S(2)}) %collective-permute-start.11) | collective-permute-done | bytes 65568 | tf_op jit(solution)/shard_map/ppermute | solution.py:221
  32.6 2.6 %collective-permute-done.8 = bf16[256,256]{1,0:T(8,128)(2,1)S(1)} collective-permute-done((bf16[256,256]{1,0:T(8,128)(2,1)S(1)}, bf16[256,256]{1,0:T(8,128)(2,1)S(1)}, u32[]{:S(2)}, u32[]{:S(2)}) %collective-permute-start.8) | collective-permute-done | bytes 131104 | tf_op jit(solution)/shard_map/ppermute | solution.py:221
  35.2 0.6 %collective-permute-start.9 = (bf16[128,256]{1,0:T(8,128)(2,1)S(1)}, bf16[128,256]{1,0:T(8,128)(2,1)S(1)}, u32[]{:S(2)}, u32[]{:S(2)}) collective-permute-start(bf16[128,256]{1,0:T(8,128)(2,1)S(1)} %slice.34), channel_id=1, source_target_pairs={{0,8},{1,9},{2,10},{3,11},{4,12},{5,13},{6,14},{7,15},{8,0},{9,1},... | collective-permute-start | bytes 196616 | tf_op jit(solution)/shard_map/ppermute | solution.py:221
  35.8 2.2 %collective-permute-done.12 = bf16[128,256]{1,0:T(8,128)(2,1)S(1)} collective-permute-done((bf16[128,256]{1,0:T(8,128)(2,1)S(1)}, bf16[128,256]{1,0:T(8,128)(2,1)S(1)}, u32[]{:S(2)}, u32[]{:S(2)}) %collective-permute-start.12) | collective-permute-done | bytes 65568 | tf_op jit(solution)/shard_map/ppermute | solution.py:221
  38.0 1.5 %collective-permute-done.9 = bf16[128,256]{1,0:T(8,128)(2,1)S(1)} collective-permute-done((bf16[128,256]{1,0:T(8,128)(2,1)S(1)}, bf16[128,256]{1,0:T(8,128)(2,1)S(1)}, u32[]{:S(2)}, u32[]{:S(2)}) %collective-permute-start.9) | collective-permute-done | bytes 65568 | tf_op jit(solution)/shard_map/ppermute | solution.py:221
  39.6 0.6 %fusion = (bf16[128,128]{1,0:T(8,128)(2,1)}, bf16[128,128]{1,0:T(8,128)(2,1)}) fusion(bf16[128,256]{1,0:T(8,128)(2,1)S(1)} %add_convert_fusion.3), kind=kLoop, calls=%fused_computation.12 | loop fusion | bytes 131072 | tf_op jit(solution)/shard_map/slice | solution.py:300
  (26 shorter events, 0.8 us)
Async XLA Ops:
  0.6 6.9 %copy-start = (bf16[128,1024]{1,0:T(8,128)(2,1)S(1)}, bf16[128,1024]{1,0:T(8,128)(2,1)}, u32[]{:S(2)}) copy-start(bf16[128,1024]{1,0:T(8,128)(2,1)} %param.5) | copy-start | bytes 786436
  0.6 17.2 %copy-start.1 = (s32[8]{0:T(128)S(1)}, s32[8]{0:T(128)}, u32[]{:S(2)}) copy-start(s32[8]{0:T(128)} %param.9) | copy-start | bytes 100
  1.5 10.5 %collective-permute-start.3 = (bf16[128,256]{1,0:T(8,128)(2,1)S(1)}, bf16[128,256]{1,0:T(8,128)(2,1)S(1)}, u32[]{:S(2)}, u32[]{:S(2)}) collective-permute-start(bf16[128,256]{1,0:T(8,128)(2,1)S(1)} %pad_maximum_fusion.1), channel_id=1, source_target_pairs={{0,7},{1,2},{2,1},{3,4},{4,3},{5,6},{6,5},{7,0},{8,15},{9,10},{10,... | collective-permute-start | bytes 196616 | tf_op jit(solution)/shard_map/ppermute | solution.py:221
  6.1 4.3 %collective-permute-start = (bf16[128,256]{1,0:T(8,128)(2,1)S(1)}, bf16[128,256]{1,0:T(8,128)(2,1)S(1)}, u32[]{:S(2)}, u32[]{:S(2)}) collective-permute-start(bf16[128,256]{1,0:T(8,128)(2,1)S(1)} %pad_maximum_fusion.1), channel_id=1, source_target_pairs={{0,8},{1,9},{2,10},{3,11},{4,12},{5,13},{6,14},{7,15},{8,0},{9,1},... | collective-permute-start | bytes 196616 | tf_op jit(solution)/shard_map/ppermute | solution.py:221
  10.3 7.5 %collective-permute-start.6 = (bf16[256,256]{1,0:T(8,128)(2,1)S(1)}, bf16[256,256]{1,0:T(8,128)(2,1)S(1)}, u32[]{:S(2)}, u32[]{:S(2)}) collective-permute-start(bf16[256,256]{1,0:T(8,128)(2,1)S(1)} %pad_maximum_fusion.so.refs_2_), channel_id=1, source_target_pairs={{0,1},{1,0},{2,3},{3,2},{4,5},{5,4},{6,7},{7,6},{8,9},{9,8},{10,11... | collective-permute-start | bytes 393224 | tf_op jit(solution)/shard_map/ppermute | solution.py:221
  10.4 6.4 %collective-permute-start.1 = (bf16[256,256]{1,0:T(8,128)(2,1)S(1)}, bf16[256,256]{1,0:T(8,128)(2,1)S(1)}, u32[]{:S(2)}, u32[]{:S(2)}) collective-permute-start(bf16[256,256]{1,0:T(8,128)(2,1)S(1)} %pad_maximum_fusion.so.refs_2_), channel_id=1, source_target_pairs={{0,16},{1,17},{2,18},{3,19},{4,20},{5,21},{6,22},{7,23},{8,24},{9,... | collective-permute-start | bytes 393224 | tf_op jit(solution)/shard_map/ppermute | solution.py:221
  12.0 4.3 %collective-permute-start.4 = (bf16[128,256]{1,0:T(8,128)(2,1)S(1)}, bf16[128,256]{1,0:T(8,128)(2,1)S(1)}, u32[]{:S(2)}, u32[]{:S(2)}) collective-permute-start(bf16[128,256]{1,0:T(8,128)(2,1)S(1)} %collective-permute-done.3), channel_id=1, source_target_pairs={{0,8},{1,9},{2,10},{3,11},{4,12},{5,13},{6,14},{7,15},{8,0},{9,1},... | collective-permute-start | bytes 196616 | tf_op jit(solution)/shard_map/ppermute | solution.py:221
  16.3 5.0 %collective-permute-start.5 = (bf16[256,256]{1,0:T(8,128)(2,1)S(1)}, bf16[256,256]{1,0:T(8,128)(2,1)S(1)}, u32[]{:S(2)}, u32[]{:S(2)}) collective-permute-start(bf16[256,256]{1,0:T(8,128)(2,1)S(1)} %constant_dynamic-update-slice_fusion.sf.refs_5_), channel_id=1, source_target_pairs={{0,16},{1,17},{2,18},{3,19},{4,20},{5,21},{6,22},{7,23},{8,24},{9,... | collective-permute-start | bytes 393224 | tf_op jit(solution)/shard_map/ppermute | solution.py:221
  16.8 4.5 %collective-permute-start.2 = (bf16[256,256]{1,0:T(8,128)(2,1)S(1)}, bf16[256,256]{1,0:T(8,128)(2,1)S(1)}, u32[]{:S(2)}, u32[]{:S(2)}) collective-permute-start(bf16[256,256]{1,0:T(8,128)(2,1)S(1)} %collective-permute-done.1.eo.refs_2_), channel_id=1, source_target_pairs={{0,1},{1,0},{2,3},{3,2},{4,5},{5,4},{6,7},{7,6},{8,9},{9,8},{10,11... | collective-permute-start | bytes 393224 | tf_op jit(solution)/shard_map/ppermute | solution.py:221
  22.2 5.8 %collective-permute-start.10 = (bf16[256,256]{1,0:T(8,128)(2,1)S(1)}, bf16[256,256]{1,0:T(8,128)(2,1)S(1)}, u32[]{:S(2)}, u32[]{:S(2)}) collective-permute-start(bf16[256,256]{1,0:T(8,128)(2,1)S(1)} %get-tuple-element.39), channel_id=1, source_target_pairs={{0,16},{1,17},{2,18},{3,19},{4,20},{5,21},{6,22},{7,23},{8,24},{9,... | collective-permute-start | bytes 393224 | tf_op jit(solution)/shard_map/ppermute | solution.py:221
  25.6 4.1 %collective-permute-start.7 = (bf16[512,256]{1,0:T(8,128)(2,1)S(1)}, bf16[512,256]{1,0:T(8,128)(2,1)S(1)}, u32[]{:S(2)}, u32[]{:S(2)}) collective-permute-start(bf16[512,256]{1,0:T(8,128)(2,1)S(1)} %get-tuple-element.36), channel_id=1, source_target_pairs={{0,1},{1,0},{2,3},{3,2},{4,5},{5,4},{6,7},{7,6},{8,9},{9,8},{10,11... | collective-permute-start | bytes 786440 | tf_op jit(solution)/shard_map/ppermute | solution.py:221
  28.1 4.3 %collective-permute-start.11 = (bf16[128,256]{1,0:T(8,128)(2,1)S(1)}, bf16[128,256]{1,0:T(8,128)(2,1)S(1)}, u32[]{:S(2)}, u32[]{:S(2)}) collective-permute-start(bf16[128,256]{1,0:T(8,128)(2,1)S(1)} %slice.36), channel_id=1, source_target_pairs={{0,8},{1,9},{2,10},{3,11},{4,12},{5,13},{6,14},{7,15},{8,0},{9,1},... | collective-permute-start | bytes 196616 | tf_op jit(solution)/shard_map/ppermute | solution.py:221
  29.7 5.4 %collective-permute-start.8 = (bf16[256,256]{1,0:T(8,128)(2,1)S(1)}, bf16[256,256]{1,0:T(8,128)(2,1)S(1)}, u32[]{:S(2)}, u32[]{:S(2)}) collective-permute-start(bf16[256,256]{1,0:T(8,128)(2,1)S(1)} %add_convert_fusion.2), channel_id=1, source_target_pairs={{0,16},{1,17},{2,18},{3,19},{4,20},{5,21},{6,22},{7,23},{8,24},{9,... | collective-permute-start | bytes 393224 | tf_op jit(solution)/shard_map/ppermute | solution.py:221
  32.5 5.6 %collective-permute-start.12 = (bf16[128,256]{1,0:T(8,128)(2,1)S(1)}, bf16[128,256]{1,0:T(8,128)(2,1)S(1)}, u32[]{:S(2)}, u32[]{:S(2)}) collective-permute-start(bf16[128,256]{1,0:T(8,128)(2,1)S(1)} %add_convert_fusion.4), channel_id=1, source_target_pairs={{0,7},{1,2},{2,1},{3,4},{4,3},{5,6},{6,5},{7,0},{8,15},{9,10},{10,... | collective-permute-start | bytes 196616 | tf_op jit(solution)/shard_map/ppermute | solution.py:221
  35.2 4.3 %collective-permute-start.9 = (bf16[128,256]{1,0:T(8,128)(2,1)S(1)}, bf16[128,256]{1,0:T(8,128)(2,1)S(1)}, u32[]{:S(2)}, u32[]{:S(2)}) collective-permute-start(bf16[128,256]{1,0:T(8,128)(2,1)S(1)} %slice.34), channel_id=1, source_target_pairs={{0,8},{1,9},{2,10},{3,11},{4,12},{5,13},{6,14},{7,15},{8,0},{9,1},... | collective-permute-start | bytes 196616 | tf_op jit(solution)/shard_map/ppermute | solution.py:221

commit v3 on v2

--- a/solution.py
+++ b/solution.py
@@ -149,52 +149,63 @@
     gq_run[...] = more if first is None else first[...] + more
 
 
-def back_kernel(half, parts, has_first, last, qs, gs, delta_ref, *refs):
+def back_kernel(half, parts, blanks, carried, new, last, qs, gs, delta_ref, *refs):
     late = is_late(half)
     refs = list(refs)
     take = lambda n: [refs.pop(0) for _ in range(n)]
     ins = [take(3) for _ in parts]
-    first = take(1)[0] if has_first else None
-    outs = take(1 + max(p[2] for p in parts))
-    gq_ref = take(1)[0] if last else None
+    kept = take(1)[0] if last else None
+    first = take(carried)[-1] if carried else None
+    outs = take(new)
+    gq_ref, out_ref = take(2) if last else (None, None)
     gq_run = take(1)[0]
+    if last:
+        copy = pltpu.make_async_copy(kept, out_ref, refs.pop())
+        copy.start()
     keys = ins[0][2].shape[0]
-    for i, ((far, slot, out, row), (w_ref, scale_ref, kv)) in enumerate(zip(parts, ins)):
-        gkv = outs[out].at[row * keys : (row + 1) * keys, :]
-        p_ref, d_ref = refs[2 * i], refs[2 * i + 1]
-        base = first if i == 0 else gq_run
-        run = functools.partial(
-            backward_unit, qs, gs, w_ref, slot, scale_ref, delta_ref, kv, gkv, gq_run, base, p_ref, d_ref
-        )
-        if far:
-            pl.when(late)(run)
-
-            @pl.when(jnp.logical_not(late))
-            def _(gkv=gkv, base=base):
-                gkv[...] = jnp.zeros_like(gkv)
-                if base is not gq_run:
-                    gq_run[...] = jnp.zeros_like(gq_run) if base is None else base[...]
+    block = lambda out, row: outs[out].at[row * keys : (row + 1) * keys, :]
+    for when in ("late", "early", "all"):
+        chosen = [i for i, p in enumerate(parts) if p[0] == when]
+        empty = [block(out, row) for w, out, row in blanks if w == when]
+        if not chosen and not empty:
+            continue
+
+        def run(chosen=chosen, empty=empty):
+            for ref in empty:
+                ref[...] = jnp.zeros_like(ref)
+            for n, i in enumerate(chosen):
+                _, slot, out, row = parts[i][1:]
+                w_ref, scale_ref, kv = ins[i]
+                backward_unit(
+                    qs, gs, w_ref, slot, scale_ref, delta_ref, kv, block(out, row), gq_run,
+                    first if n == 0 else gq_run, refs[2 * n], refs[2 * n + 1],
+                )
+
+        if when == "all":
+            run()
         else:
-            run()
+            pl.when(late if when == "late" else jnp.logical_not(late))(run)
     if last:
         rows = gq_ref.shape[0]
         for h in range(qs.shape[0] // rows):
             g16 = (gq_run[:, h * rows : (h + 1) * rows] * FACTOR).astype(BF16)
             gq_ref[:, h * HEAD : (h + 1) * HEAD] = g16.T
+        copy.wait()
 
 
 def like(shape, dtype):
     return jax.ShapeDtypeStruct(shape, dtype)
 
 
-def call(kernel, outs, scratch, keys, args, spec=VMEM):
+def call(kernel, outs, scratch, keys, args, out_specs=None, aliases={}):
     work = 2 * keys * HEAD * HEAD * 8
     return pl.pallas_call(
         kernel,
         out_shape=outs,
-        in_specs=[spec] * len(args),
-        out_specs=[VMEM] * len(outs),
+        in_specs=[VMEM] * len(args),
+        out_specs=out_specs or [VMEM] * len(outs),
         scratch_shapes=scratch,
+        input_output_aliases=aliases,
         cost_estimate=pl.CostEstimate(flops=4 * work, bytes_accessed=1 << 20, transcendentals=work // 256),
         compiler_params=pltpu.CompilerParams(vmem_limit_bytes=30 << 20),
     )(*args)
@@ -264,28 +275,46 @@
         functools.partial(near_kernel, rows, half, blk_count), [wide, line, line, weights], [scores],
         3 * unit, [span_order.reshape(1, blk_count), qs, so, sm, sf],
     )
-    out, fw, near, far, delta = call(
+    kept, fw, near, far, delta = call(
         functools.partial(far_kernel, half), [full, weights, line, line, line], [wide_s, line_s, line_s, scores],
         3 * unit, [qs, gs, eo, em, ef, o_run, m_run, l_run],
     )
 
-    def back(parts, first, last=False):
+    def back(parts, blanks, carry, sizes, gq, last=False):
         args = [qs, gs, delta]
-        for far_part, slot, out_index, row, kv in parts:
+        for _, far_part, slot, _, _, kv in parts:
             args += [fw, far, kv] if far_part else [nw, near, kv]
-        if first is not None:
-            args.append(first)
-        shape = tuple(p[:4] for p in parts)
-        sizes = [sum(p[2] == i for p in shape) for i in range(1 + max(p[2] for p in shape))]
-        outs = [like((n * unit, 2 * HEAD), BF16) for n in sizes] + [full if last else wide]
-        temp = ([wide_s] if last else []) + [pltpu.VMEM((unit, big), BF16)] * (2 * len(parts))
-        kernel = functools.partial(back_kernel, half, shape, first is not None, last)
-        return call(kernel, outs, temp, unit * len(parts), args)
-
-    gef, gq = back([(True, 2, 0, 0, ef)], None)
-    gm, gq = back([(True, 1, 0, 1, em), (False, 1, 0, 0, sm)], gq)
-    geo, gsf, gq = back([(True, 0, 0, 0, eo), (False, 2, 1, 0, sf)], gq)
-    gso, gq = back([(False, 0, 0, 0, so)], gq, last=True)
+        if last:
+            args.append(kept)
+        carried = list(carry) + ([] if gq is None else [gq])
+        base = len(args)
+        args += carried
+        outs = [like(a.shape, a.dtype) for a in carry] + [like((n, 2 * HEAD), BF16) for n in sizes]
+        aliases = {base + i: i for i in range(len(carry))}
+        new = len(outs)
+        temp = [pltpu.VMEM((unit, big), BF16)] * (2 * len(parts))
+        specs = None
+        if last:
+            outs += [full, full]
+            specs = [VMEM] * (len(outs) - 1) + [pl.BlockSpec(memory_space=pl.ANY)]
+            temp = [wide_s] + temp + [pltpu.SemaphoreType.DMA]
+        else:
+            outs.append(wide)
+            if gq is not None:
+                aliases[base + len(carry)] = len(outs) - 1
+        shape = tuple(p[:5] for p in parts)
+        kernel = functools.partial(back_kernel, half, shape, blanks, len(carried), new, last)
+        return call(kernel, outs, temp, unit * len(parts), args, specs, aliases)
+
+    gef, gsf, gm, gq = back(
+        [("late", True, 2, 0, 0, ef), ("early", False, 2, 1, 0, sf), ("early", False, 1, 2, 0, sm)],
+        (("early", 0, 0), ("early", 2, 1)), [], [unit, unit, 2 * unit], None,
+    )
+    gm, gq = back([("late", True, 1, 0, 1, em), ("late", False, 1, 0, 0, sm)], (), [gm], [], gq)
+    gsf, geo, gq = back(
+        [("late", True, 0, 1, 0, eo), ("late", False, 2, 0, 0, sf)], (("early", 1, 0),), [gsf], [unit], gq
+    )
+    gso, gq, out = back([("all", False, 0, 0, 0, so)], (), [], [unit], gq, last=True)
 
     back_f = across(gef)
     gsf = add(gsf, back_f)

time: 40.4 us -> 39.8 us (0.985)
  waiting for transfers between devices: 15 us -> 16.6 us
  starting transfers between devices: 16.5 us -> 15 us
  Pallas kernels: 5.28 us -> 4.57 us
    ppermute x13, waiting for transfers between devices: 15 us -> 16.6 us  [send(): return lax.ppermute(block, ('grp', 'blk'), route)]
    ppermute x13, starting transfers between devices: 16.5 us -> 15 us  [send(): return lax.ppermute(block, ('grp', 'blk'), route)]
    pallas_call x6, Pallas kernels: 5.28 us -> 4.57 us  [call(): pl.pallas_call(kernel, out_shape=outs, in_specs=[VMEM] * len(args), out_s...]
  transfers between devices with their start and end apart: 13 -> 13, of which waited for: 8 -> 8; matrix products, arithmetic and copies ran while one was open for 3% -> 3% of each run, Pallas kernels for 11% -> 8%
where the time goes in v3:
time: 39.8 us; the launch traced here: 39.6 us
  waiting for transfers between devices  16.6 us (42%)
  starting transfers between devices  15 us (38%)
  Pallas kernels  4.57 us (11%)
  local copies, waits for them, and re-layouts  1.71 us (4%)
  other arithmetic  1 us (3%)
  between operations  0.77 us (2%)
    ppermute x13, waiting for transfers between devices, send(): return lax.ppermute(block, ('grp', 'blk'), route)  16.6 us
    ppermute x13, starting transfers between devices, send(): return lax.ppermute(block, ('grp', 'blk'), route)  15 us
    pallas_call x6, Pallas kernels, call(): pl.pallas_call(kernel, out_shape=outs, in_specs=[VMEM] * len(args), out_s...  4.57 us
    reshape x2, local copies, waits for them, and re-layouts, stacked(): x = jnp.transpose(x.reshape(rows, width // HEAD, HEAD), (1, 0, 2))  1.04 us
    concatenate x1, other arithmetic, step(): own = lax.optimization_barrier(jnp.concatenate([key_rows, values], axis=1))  0.82 us
  transfers between devices with their start and end apart: 13, of which 8 were waited for; matrix products, arithmetic and copies ran while one was open for 3% of the time, Pallas kernels for 8%

profile of v3, /device:TPU:0, one launch (start us, length us, event | category | flops | bytes accessed | tf_op | source)
XLA Modules:
  0.0 39.6 jit_solution(13387543876566713886)
XLA Ops:
  0.7 0.8 %pad_maximum_fusion.1 = bf16[128,256]{1,0:T(8,128)(2,1)S(1)} fusion(bf16[128,128]{1,0:T(8,128)(2,1)} %param.7, bf16[128,128]{1,0:T(8,128)(2,1)} %param.6), kind=kLoop, calls=%fused_computation.9 | loop fusion | flops 131072 | bytes 131072 | tf_op jit(solution)/shard_map/concatenate | solution.py:256
  1.5 4.6 %collective-permute-start.3 = (bf16[128,256]{1,0:T(8,128)(2,1)S(1)}, bf16[128,256]{1,0:T(8,128)(2,1)S(1)}, u32[]{:S(2)}, u32[]{:S(2)}) collective-permute-start(bf16[128,256]{1,0:T(8,128)(2,1)S(1)} %pad_maximum_fusion.1), channel_id=1, source_target_pairs={{0,7},{1,2},{2,1},{3,4},{4,3},{5,6},{6,5},{7,0},{8,15},{9,10},{10,... | collective-permute-start | bytes 196616 | tf_op jit(solution)/shard_map/ppermute | solution.py:232
  6.1 1.5 %collective-permute-start = (bf16[128,256]{1,0:T(8,128)(2,1)S(1)}, bf16[128,256]{1,0:T(8,128)(2,1)S(1)}, u32[]{:S(2)}, u32[]{:S(2)}) collective-permute-start(bf16[128,256]{1,0:T(8,128)(2,1)S(1)} %pad_maximum_fusion.1), channel_id=1, source_target_pairs={{0,8},{1,9},{2,10},{3,11},{4,12},{5,13},{6,14},{7,15},{8,0},{9,1},... | collective-permute-start | bytes 196616 | tf_op jit(solution)/shard_map/ppermute | solution.py:232
  7.6 2.7 %collective-permute-done = bf16[128,256]{1,0:T(8,128)(2,1)S(1)} collective-permute-done((bf16[128,256]{1,0:T(8,128)(2,1)S(1)}, bf16[128,256]{1,0:T(8,128)(2,1)S(1)}, u32[]{:S(2)}, u32[]{:S(2)}) %collective-permute-start) | collective-permute-done | bytes 65568 | tf_op jit(solution)/shard_map/ppermute | solution.py:232
  10.4 1.6 %collective-permute-start.1 = (bf16[256,256]{1,0:T(8,128)(2,1)S(1)}, bf16[256,256]{1,0:T(8,128)(2,1)S(1)}, u32[]{:S(2)}, u32[]{:S(2)}) collective-permute-start(bf16[256,256]{1,0:T(8,128)(2,1)S(1)} %pad_maximum_fusion.so.refs_2_), channel_id=1, source_target_pairs={{0,16},{1,17},{2,18},{3,19},{4,20},{5,21},{6,22},{7,23},{8,24},{9,... | collective-permute-start | bytes 393224 | tf_op jit(solution)/shard_map/ppermute | solution.py:232
  12.0 1.5 %collective-permute-start.4 = (bf16[128,256]{1,0:T(8,128)(2,1)S(1)}, bf16[128,256]{1,0:T(8,128)(2,1)S(1)}, u32[]{:S(2)}, u32[]{:S(2)}) collective-permute-start(bf16[128,256]{1,0:T(8,128)(2,1)S(1)} %collective-permute-done.3), channel_id=1, source_target_pairs={{0,8},{1,9},{2,10},{3,11},{4,12},{5,13},{6,14},{7,15},{8,0},{9,1},... | collective-permute-start | bytes 196616 | tf_op jit(solution)/shard_map/ppermute | solution.py:232
  13.5 2.8 %collective-permute-done.4 = bf16[128,256]{1,0:T(8,128)(2,1)S(1)} collective-permute-done((bf16[128,256]{1,0:T(8,128)(2,1)S(1)}, bf16[128,256]{1,0:T(8,128)(2,1)S(1)}, u32[]{:S(2)}, u32[]{:S(2)}) %collective-permute-start.4) | collective-permute-done | bytes 65568 | tf_op jit(solution)/shard_map/ppermute | solution.py:232
  16.3 0.5 %collective-permute-start.5 = (bf16[256,256]{1,0:T(8,128)(2,1)S(1)}, bf16[256,256]{1,0:T(8,128)(2,1)S(1)}, u32[]{:S(2)}, u32[]{:S(2)}) collective-permute-start(bf16[256,256]{1,0:T(8,128)(2,1)S(1)} %constant_dynamic-update-slice_fusion.sf.refs_5_), channel_id=1, source_target_pairs={{0,16},{1,17},{2,18},{3,19},{4,20},{5,21},{6,22},{7,23},{8,24},{9,... | collective-permute-start | bytes 393224 | tf_op jit(solution)/shard_map/ppermute | solution.py:232
  16.8 1.0 %copy_bitcast_fusion = bf16[128,8,128]{2,0,1:T(8,128)(2,1)S(1)} fusion(bf16[128,1024]{1,0:T(8,128)(2,1)} %param.8), kind=kLoop, calls=%fused_computation | loop fusion | bytes 524288 | tf_op jit(solution)/shard_map/reshape | solution.py:259
  17.8 1.4 %shard_map.84 = (f32[128,1024]{1,0:T(8,128)S(1)}, f32[1,1024]{1,0:T(1,128)S(1)}, f32[1,1024]{1,0:T(1,128)S(1)}, bf16[768,1024]{1,0:T(8,128)(2,1)S(1)}) custom-call(s32[1,8]{1,0:T(1,128)S(1)} %bitcast.28, bf16[1024,128]{1,0:T(8,128)(2,1)S(1)} %bitcast.17, bf16[256,256]{1,0:T(8,128)(2,1)S(1)} %pad_maximum_fusion.so.refs_2_, ...), custom_call_target="tpu_custom_call" | custom-call | flops 805306368 | bytes 1048576 | tf_op jit(solution)/shard_map/pallas_call | solution.py:202
  19.2 2.0 %collective-permute-done.5.ef.refs_2_ = bf16[256,256]{1,0:T(8,128)(2,1)S(1)} collective-permute-done((bf16[256,256]{1,0:T(8,128)(2,1)S(1)}, bf16[256,256]{1,0:T(8,128)(2,1)S(1)}, u32[]{:S(2)}, u32[]{:S(2)}) %collective-permute-start.5) | collective-permute-done | bytes 131104 | tf_op jit(solution)/shard_map/ppermute | solution.py:232
  21.2 0.4 shard_map.85
  21.6 1.2 %shard_map.86 = (bf16[256,256]{1,0:T(8,128)(2,1)S(1)}, bf16[256,256]{1,0:T(8,128)(2,1)S(1)}, bf16[512,256]{1,0:T(8,128)(2,1)S(1)}, f32[128,1024]{1,0:T(8,128)S(1)}) custom-call(bf16[1024,128]{1,0:T(8,128)(2,1)S(1)} %bitcast.19, bf16[1024,128]{1,0:T(8,128)(2,1)S(1)} %bitcast.24, f32[1,1024]{1,0:T(1,128)S(1)} %get-tuple-element.28.delta_ref, ...), custom_call_target="tpu_custom_call" | custom-call | flops 805306368 | bytes 1048576 | tf_op jit(solution)/shard_map/pallas_call | solution.py:202
  22.9 1.5 %collective-permute-start.10 = (bf16[256,256]{1,0:T(8,128)(2,1)S(1)}, bf16[256,256]{1,0:T(8,128)(2,1)S(1)}, u32[]{:S(2)}, u32[]{:S(2)}) collective-permute-start(bf16[256,256]{1,0:T(8,128)(2,1)S(1)} %get-tuple-element.45), channel_id=1, source_target_pairs={{0,16},{1,17},{2,18},{3,19},{4,20},{5,21},{6,22},{7,23},{8,24},{9,... | collective-permute-start | bytes 393224 | tf_op jit(solution)/shard_map/ppermute | solution.py:232
  24.4 1.5 %shard_map.89 = (bf16[256,256]{1,0:T(8,128)(2,1)S(1)}, bf16[128,1024]{1,0:T(8,128)(2,1)}, bf16[128,1024]{1,0:T(8,128)(2,1)}) custom-call(bf16[1024,128]{1,0:T(8,128)(2,1)S(1)} %bitcast.22, bf16[1024,128]{1,0:T(8,128)(2,1)S(1)} %bitcast.27, f32[1,1024]{1,0:T(1,128)S(1)} %get-tuple-element.28.delta_ref, ...), custom_call_target="tpu_custom_call" | custom-call | flops 268435456 | bytes 1048576 | tf_op jit(solution)/shard_map/pallas_call | solution.py:202
  25.9 1.9 %collective-permute-done.10 = bf16[256,256]{1,0:T(8,128)(2,1)S(1)} collective-permute-done((bf16[256,256]{1,0:T(8,128)(2,1)S(1)}, bf16[256,256]{1,0:T(8,128)(2,1)S(1)}, u32[]{:S(2)}, u32[]{:S(2)}) %collective-permute-start.10) | collective-permute-done | bytes 131104 | tf_op jit(solution)/shard_map/ppermute | solution.py:232
  27.9 1.6 %collective-permute-start.11 = (bf16[128,256]{1,0:T(8,128)(2,1)S(1)}, bf16[128,256]{1,0:T(8,128)(2,1)S(1)}, u32[]{:S(2)}, u32[]{:S(2)}) collective-permute-start(bf16[128,256]{1,0:T(8,128)(2,1)S(1)} %slice.36), channel_id=1, source_target_pairs={{0,8},{1,9},{2,10},{3,11},{4,12},{5,13},{6,14},{7,15},{8,0},{9,1},... | collective-permute-start | bytes 196616 | tf_op jit(solution)/shard_map/ppermute | solution.py:232
  29.5 1.5 %collective-permute-start.8 = (bf16[256,256]{1,0:T(8,128)(2,1)S(1)}, bf16[256,256]{1,0:T(8,128)(2,1)S(1)}, u32[]{:S(2)}, u32[]{:S(2)}) collective-permute-start(bf16[256,256]{1,0:T(8,128)(2,1)S(1)} %add_convert_fusion.2), channel_id=1, source_target_pairs={{0,16},{1,17},{2,18},{3,19},{4,20},{5,21},{6,22},{7,23},{8,24},{9,... | collective-permute-start | bytes 393224 | tf_op jit(solution)/shard_map/ppermute | solution.py:232
  31.1 1.2 %collective-permute-done.11 = bf16[128,256]{1,0:T(8,128)(2,1)S(1)} collective-permute-done((bf16[128,256]{1,0:T(8,128)(2,1)S(1)}, bf16[128,256]{1,0:T(8,128)(2,1)S(1)}, u32[]{:S(2)}, u32[]{:S(2)}) %collective-permute-start.11) | collective-permute-done | bytes 65568 | tf_op jit(solution)/shard_map/ppermute | solution.py:232
  32.4 2.2 %collective-permute-done.8 = bf16[256,256]{1,0:T(8,128)(2,1)S(1)} collective-permute-done((bf16[256,256]{1,0:T(8,128)(2,1)S(1)}, bf16[256,256]{1,0:T(8,128)(2,1)S(1)}, u32[]{:S(2)}, u32[]{:S(2)}) %collective-permute-start.8) | collective-permute-done | bytes 131104 | tf_op jit(solution)/shard_map/ppermute | solution.py:232
  34.6 0.6 %collective-permute-start.9 = (bf16[128,256]{1,0:T(8,128)(2,1)S(1)}, bf16[128,256]{1,0:T(8,128)(2,1)S(1)}, u32[]{:S(2)}, u32[]{:S(2)}) collective-permute-start(bf16[128,256]{1,0:T(8,128)(2,1)S(1)} %slice.34), channel_id=1, source_target_pairs={{0,8},{1,9},{2,10},{3,11},{4,12},{5,13},{6,14},{7,15},{8,0},{9,1},... | collective-permute-start | bytes 196616 | tf_op jit(solution)/shard_map/ppermute | solution.py:232
  35.2 2.6 %collective-permute-done.12 = bf16[128,256]{1,0:T(8,128)(2,1)S(1)} collective-permute-done((bf16[128,256]{1,0:T(8,128)(2,1)S(1)}, bf16[128,256]{1,0:T(8,128)(2,1)S(1)}, u32[]{:S(2)}, u32[]{:S(2)}) %collective-permute-start.12) | collective-permute-done | bytes 65568 | tf_op jit(solution)/shard_map/ppermute | solution.py:232
  37.8 1.1 %collective-permute-done.9 = bf16[128,256]{1,0:T(8,128)(2,1)S(1)} collective-permute-done((bf16[128,256]{1,0:T(8,128)(2,1)S(1)}, bf16[128,256]{1,0:T(8,128)(2,1)S(1)}, u32[]{:S(2)}, u32[]{:S(2)}) %collective-permute-start.9) | collective-permute-done | bytes 65568 | tf_op jit(solution)/shard_map/ppermute | solution.py:232
  39.0 0.6 %fusion = (bf16[128,128]{1,0:T(8,128)(2,1)}, bf16[128,128]{1,0:T(8,128)(2,1)}) fusion(bf16[128,256]{1,0:T(8,128)(2,1)S(1)} %add_convert_fusion.3), kind=kLoop, calls=%fused_computation.12 | loop fusion | bytes 131072 | tf_op jit(solution)/shard_map/slice | solution.py:329
  (26 shorter events, 0.4 us)
Async XLA Ops:
  0.6 6.9 %copy-start = (bf16[128,1024]{1,0:T(8,128)(2,1)S(1)}, bf16[128,1024]{1,0:T(8,128)(2,1)}, u32[]{:S(2)}) copy-start(bf16[128,1024]{1,0:T(8,128)(2,1)} %param.5) | copy-start | bytes 786436
  0.6 17.2 %copy-start.1 = (s32[8]{0:T(128)S(1)}, s32[8]{0:T(128)}, u32[]{:S(2)}) copy-start(s32[8]{0:T(128)} %param.9) | copy-start | bytes 100
  1.5 10.5 %collective-permute-start.3 = (bf16[128,256]{1,0:T(8,128)(2,1)S(1)}, bf16[128,256]{1,0:T(8,128)(2,1)S(1)}, u32[]{:S(2)}, u32[]{:S(2)}) collective-permute-start(bf16[128,256]{1,0:T(8,128)(2,1)S(1)} %pad_maximum_fusion.1), channel_id=1, source_target_pairs={{0,7},{1,2},{2,1},{3,4},{4,3},{5,6},{6,5},{7,0},{8,15},{9,10},{10,... | collective-permute-start | bytes 196616 | tf_op jit(solution)/shard_map/ppermute | solution.py:232
  6.1 4.3 %collective-permute-start = (bf16[128,256]{1,0:T(8,128)(2,1)S(1)}, bf16[128,256]{1,0:T(8,128)(2,1)S(1)}, u32[]{:S(2)}, u32[]{:S(2)}) collective-permute-start(bf16[128,256]{1,0:T(8,128)(2,1)S(1)} %pad_maximum_fusion.1), channel_id=1, source_target_pairs={{0,8},{1,9},{2,10},{3,11},{4,12},{5,13},{6,14},{7,15},{8,0},{9,1},... | collective-permute-start | bytes 196616 | tf_op jit(solution)/shard_map/ppermute | solution.py:232
  10.3 7.5 %collective-permute-start.6 = (bf16[256,256]{1,0:T(8,128)(2,1)S(1)}, bf16[256,256]{1,0:T(8,128)(2,1)S(1)}, u32[]{:S(2)}, u32[]{:S(2)}) collective-permute-start(bf16[256,256]{1,0:T(8,128)(2,1)S(1)} %pad_maximum_fusion.so.refs_2_), channel_id=1, source_target_pairs={{0,1},{1,0},{2,3},{3,2},{4,5},{5,4},{6,7},{7,6},{8,9},{9,8},{10,11... | collective-permute-start | bytes 393224 | tf_op jit(solution)/shard_map/ppermute | solution.py:232
  10.4 6.4 %collective-permute-start.1 = (bf16[256,256]{1,0:T(8,128)(2,1)S(1)}, bf16[256,256]{1,0:T(8,128)(2,1)S(1)}, u32[]{:S(2)}, u32[]{:S(2)}) collective-permute-start(bf16[256,256]{1,0:T(8,128)(2,1)S(1)} %pad_maximum_fusion.so.refs_2_), channel_id=1, source_target_pairs={{0,16},{1,17},{2,18},{3,19},{4,20},{5,21},{6,22},{7,23},{8,24},{9,... | collective-permute-start | bytes 393224 | tf_op jit(solution)/shard_map/ppermute | solution.py:232
  12.0 4.3 %collective-permute-start.4 = (bf16[128,256]{1,0:T(8,128)(2,1)S(1)}, bf16[128,256]{1,0:T(8,128)(2,1)S(1)}, u32[]{:S(2)}, u32[]{:S(2)}) collective-permute-start(bf16[128,256]{1,0:T(8,128)(2,1)S(1)} %collective-permute-done.3), channel_id=1, source_target_pairs={{0,8},{1,9},{2,10},{3,11},{4,12},{5,13},{6,14},{7,15},{8,0},{9,1},... | collective-permute-start | bytes 196616 | tf_op jit(solution)/shard_map/ppermute | solution.py:232
  16.3 5.0 %collective-permute-start.5 = (bf16[256,256]{1,0:T(8,128)(2,1)S(1)}, bf16[256,256]{1,0:T(8,128)(2,1)S(1)}, u32[]{:S(2)}, u32[]{:S(2)}) collective-permute-start(bf16[256,256]{1,0:T(8,128)(2,1)S(1)} %constant_dynamic-update-slice_fusion.sf.refs_5_), channel_id=1, source_target_pairs={{0,16},{1,17},{2,18},{3,19},{4,20},{5,21},{6,22},{7,23},{8,24},{9,... | collective-permute-start | bytes 393224 | tf_op jit(solution)/shard_map/ppermute | solution.py:232
  16.8 4.5 %collective-permute-start.2 = (bf16[256,256]{1,0:T(8,128)(2,1)S(1)}, bf16[256,256]{1,0:T(8,128)(2,1)S(1)}, u32[]{:S(2)}, u32[]{:S(2)}) collective-permute-start(bf16[256,256]{1,0:T(8,128)(2,1)S(1)} %collective-permute-done.1.eo.refs_2_), channel_id=1, source_target_pairs={{0,1},{1,0},{2,3},{3,2},{4,5},{5,4},{6,7},{7,6},{8,9},{9,8},{10,11... | collective-permute-start | bytes 393224 | tf_op jit(solution)/shard_map/ppermute | solution.py:232
  22.9 5.0 %collective-permute-start.10 = (bf16[256,256]{1,0:T(8,128)(2,1)S(1)}, bf16[256,256]{1,0:T(8,128)(2,1)S(1)}, u32[]{:S(2)}, u32[]{:S(2)}) collective-permute-start(bf16[256,256]{1,0:T(8,128)(2,1)S(1)} %get-tuple-element.45), channel_id=1, source_target_pairs={{0,16},{1,17},{2,18},{3,19},{4,20},{5,21},{6,22},{7,23},{8,24},{9,... | collective-permute-start | bytes 393224 | tf_op jit(solution)/shard_map/ppermute | solution.py:232
  24.4 5.1 %collective-permute-start.7 = (bf16[512,256]{1,0:T(8,128)(2,1)S(1)}, bf16[512,256]{1,0:T(8,128)(2,1)S(1)}, u32[]{:S(2)}, u32[]{:S(2)}) collective-permute-start(bf16[512,256]{1,0:T(8,128)(2,1)S(1)} %get-tuple-element.42), channel_id=1, source_target_pairs={{0,1},{1,0},{2,3},{3,2},{4,5},{5,4},{6,7},{7,6},{8,9},{9,8},{10,11... | collective-permute-start | bytes 786440 | tf_op jit(solution)/shard_map/ppermute | solution.py:232
  27.9 4.3 %collective-permute-start.11 = (bf16[128,256]{1,0:T(8,128)(2,1)S(1)}, bf16[128,256]{1,0:T(8,128)(2,1)S(1)}, u32[]{:S(2)}, u32[]{:S(2)}) collective-permute-start(bf16[128,256]{1,0:T(8,128)(2,1)S(1)} %slice.36), channel_id=1, source_target_pairs={{0,8},{1,9},{2,10},{3,11},{4,12},{5,13},{6,14},{7,15},{8,0},{9,1},... | collective-permute-start | bytes 196616 | tf_op jit(solution)/shard_map/ppermute | solution.py:232
  29.5 5.0 %collective-permute-start.8 = (bf16[256,256]{1,0:T(8,128)(2,1)S(1)}, bf16[256,256]{1,0:T(8,128)(2,1)S(1)}, u32[]{:S(2)}, u32[]{:S(2)}) collective-permute-start(bf16[256,256]{1,0:T(8,128)(2,1)S(1)} %add_convert_fusion.2), channel_id=1, source_target_pairs={{0,16},{1,17},{2,18},{3,19},{4,20},{5,21},{6,22},{7,23},{8,24},{9,... | collective-permute-start | bytes 393224 | tf_op jit(solution)/shard_map/ppermute | solution.py:232
  32.3 5.6 %collective-permute-start.12 = (bf16[128,256]{1,0:T(8,128)(2,1)S(1)}, bf16[128,256]{1,0:T(8,128)(2,1)S(1)}, u32[]{:S(2)}, u32[]{:S(2)}) collective-permute-start(bf16[128,256]{1,0:T(8,128)(2,1)S(1)} %add_convert_fusion.4), channel_id=1, source_target_pairs={{0,7},{1,2},{2,1},{3,4},{4,3},{5,6},{6,5},{7,0},{8,15},{9,10},{10,... | collective-permute-start | bytes 196616 | tf_op jit(solution)/shard_map/ppermute | solution.py:232
  34.6 4.3 %collective-permute-start.9 = (bf16[128,256]{1,0:T(8,128)(2,1)S(1)}, bf16[128,256]{1,0:T(8,128)(2,1)S(1)}, u32[]{:S(2)}, u32[]{:S(2)}) collective-permute-start(bf16[128,256]{1,0:T(8,128)(2,1)S(1)} %slice.34), channel_id=1, source_target_pairs={{0,8},{1,9},{2,10},{3,11},{4,12},{5,13},{6,14},{7,15},{8,0},{9,1},... | collective-permute-start | bytes 196616 | tf_op jit(solution)/shard_map/ppermute | solution.py:232

commit v4 on v3

--- a/solution.py
+++ b/solution.py
@@ -51,78 +51,93 @@
     return (row <= col) | ((row >= rows) & (row < (idx + 1) * rows))
 
 
-def attend_group(units, bias, mask, qs, m_in, m_ref, w_ref, s_ref, finish):
-    keys = units[0].shape[0]
+def load(refs, rows, far, column):
+    tiles = []
+    for ref in refs:
+        for r in range(far * rows, ref.shape[0], 2 * rows):
+            tiles.append(ref[r : r + rows, column : column + HEAD])
+    return jnp.concatenate(tiles, axis=0) if len(tiles) > 1 else tiles[0]
+
+
+def attend_group(refs, rows, count, hidden, mask, qs, m_in, m_ref, w_ref, s_ref, finish):
     big = qs.shape[0]
     pair = min(big, 2 * HEAD)
+    ks = [load(refs, rows, u, 0) for u in range(count)]
+    keys = ks[0].shape[0]
     ones = jnp.ones((16, keys), BF16)
     for c in range(0, big, pair):
         cols = slice(c, c + pair)
         top = m_in[:, cols] if m_in is not None else jnp.full((1, pair), NEG_FILL, F32)
-        for u, kv in enumerate(units):
-            s = dot_nt(kv[:, :HEAD], qs[cols, :]) * C2
+        for u, k in enumerate(ks):
+            s = dot_nt(k, qs[cols, :]) * C2
             if u == 0 and mask is not None:
                 s = jnp.where(mask, s, NEG_FILL)
             s_ref[u, :, cols] = s
             peak = jnp.max(s, axis=0, keepdims=True)
-            if u > 0 and bias is not None:
-                peak = jnp.where(bias[u - 1] < 0.0, NEG_FILL, peak)
+            if u == 0 and hidden is not None:
+                peak = jnp.where(hidden < 0.0, NEG_FILL, peak)
             top = jnp.maximum(top, peak)
         m_ref[:, cols] = top
-    vt = jnp.concatenate([jnp.concatenate([kv[:, HEAD:].T, ones], axis=0) for kv in units], axis=1)
+    vt = [jnp.concatenate([load(refs, rows, u, HEAD).T, ones], axis=0) for u in range(count)]
+    vt = jnp.concatenate(vt, axis=1) if count > 1 else vt[0]
     for c in range(0, big, pair):
         cols = slice(c, c + pair)
-        for u in range(len(units)):
+        for u in range(count):
             base = m_ref[:, cols]
-            if u > 0 and bias is not None:
-                base = jnp.where(bias[u - 1] < 0.0, -NEG_FILL, base)
+            if u == 0 and hidden is not None:
+                base = jnp.where(hidden < 0.0, -NEG_FILL, base)
             w_ref[u * keys : (u + 1) * keys, cols] = jnp.exp2(s_ref[u, :, cols] - base).astype(BF16)
-        summed = dot(vt, w_ref[:, cols])
+        summed = dot(vt, w_ref[: count * keys, cols])
         finish(cols, summed[:HEAD], summed[HEAD : HEAD + 1])
 
 
-def near_kernel(rows, half, blk_count, span_ref, qs, so, sm, sf, o_ref, m_ref, l_ref, w_ref, s_ref):
-    idx = lax.rem(lax.axis_index("grp"), half)
+def attend_block(which, rows, half, blk_count, span_ref, qs, refs, before, o_run, m_run, l_run, w_ref, s_ref):
+    late = is_late(half)
+    o_in, m_in, l_in = before or (None, None, None)
 
     def finish(cols, summed, total):
-        o_ref[:, cols] = summed
-        l_ref[:, cols] = total
-
-    mask = own_mask(so.shape[0], rows, idx)
-    bias = biases(half, blk_count, span_ref)
-    attend_group((so, sm, sf), bias, mask, qs, None, m_ref, w_ref, s_ref, finish)
-
-
-def far_kernel(
-    half, qs, gs, eo, em, ef, o_in, m_in, l_in,
-    out_ref, w_ref, near_ref, far_ref, delta_ref, o_run, m_run, l_run, s_ref,
-):
-    late = is_late(half)
-    rows = out_ref.shape[0]
+        if before:
+            alpha = jnp.exp2(m_in[:, cols] - m_run[:, cols])
+            summed = o_in[:, cols] * alpha + summed
+            total = l_in[:, cols] * alpha + total
+        o_run[:, cols] = summed
+        l_run[:, cols] = total
+
+    hidden = mask = None
+    if which == 0:
+        mask = own_mask(half * rows, rows, lax.rem(lax.axis_index("grp"), half))
+    else:
+        hidden = biases(half, blk_count, span_ref)[which - 1]
+    for count, on in ((2, late), (1, jnp.logical_not(late))):
+        pl.when(on)(
+            functools.partial(attend_group, refs, rows, count, hidden, mask, qs, m_in, m_run, w_ref, s_ref, finish)
+        )
+
+
+def forward_kernel(which, rows, half, blk_count, span_ref, qs, *refs):
+    refs = list(refs)
+    o_run, m_run, l_run, w_ref, s_ref = refs[-5:]
+    before = refs[-8:-5] if which else None
+    attend_block(
+        which, rows, half, blk_count, span_ref, qs, refs[: -8 if which else -5], before, o_run, m_run, l_run, w_ref, s_ref
+    )
+
+
+def finish_kernel(rows, half, blk_count, span_ref, qs, gs, *refs):
+    refs = list(refs)
+    m_first, o_in, m_in, l_in, out_ref, w_ref, a_ref, b_ref, c_ref, delta_ref, o_run, m_run, l_run, s_ref = refs[-14:]
+    attend_block(
+        2, rows, half, blk_count, span_ref, qs, refs[:-14], (o_in, m_in, l_in), o_run, m_run, l_run, w_ref, s_ref
+    )
     big = qs.shape[0]
     pair = 2 * rows
-
-    @pl.when(late)
-    def _():
-        def finish(cols, summed, total):
-            alpha = jnp.exp2(m_in[:, cols] - m_run[:, cols])
-            o_run[:, cols] = o_in[:, cols] * alpha + summed
-            l_run[:, cols] = l_in[:, cols] * alpha + total
-
-        attend_group((eo, em, ef), None, None, qs, m_in, m_run, w_ref, s_ref, finish)
-
-    @pl.when(jnp.logical_not(late))
-    def _():
-        o_run[...] = o_in[...]
-        m_run[...] = m_in[...]
-        l_run[...] = l_in[...]
-
     ones = jnp.ones((8, HEAD), BF16)
     for p in range(big // pair):
         cols = slice(p * pair, (p + 1) * pair)
         inv = 1.0 / l_run[:, cols]
-        far_ref[:, cols] = inv
-        near_ref[:, cols] = inv * jnp.exp2(m_in[:, cols] - m_run[:, cols])
+        a_ref[:, cols] = inv * jnp.exp2(m_first[:, cols] - m_run[:, cols])
+        b_ref[:, cols] = inv * jnp.exp2(m_in[:, cols] - m_run[:, cols])
+        c_ref[:, cols] = inv
         o16 = (o_run[:, cols] * inv).astype(BF16).T
         out_ref[:, 2 * p * HEAD : (2 * p + 1) * HEAD] = o16[:rows]
         out_ref[:, (2 * p + 1) * HEAD : (2 * p + 2) * HEAD] = o16[rows:]
@@ -132,15 +147,16 @@
         delta_ref[:, cols] = (dot_nt(ones, high) + dot_nt(ones, low))[:1]
 
 
-def backward_unit(qs, gs, w_ref, slot, scale_ref, delta_ref, kv, gkv, gq_run, first, p_ref, d_ref):
-    keys = kv.shape[0]
+def backward_unit(qs, gs, w_ref, far, scale_ref, delta_ref, refs, rows, gkv, gq_run, first, p_ref, d_ref):
+    k, v = load(refs, rows, far, 0), load(refs, rows, far, HEAD)
+    keys = k.shape[0]
     big = qs.shape[0]
     pair = min(big, 2 * HEAD)
-    kt = kv[:, :HEAD].T
+    kt = k.T
     for c in range(0, big, pair):
         cols = slice(c, c + pair)
-        prob = w_ref[slot * keys : (slot + 1) * keys, cols].astype(F32) * scale_ref[:, cols]
-        dp = dot_nt(kv[:, HEAD:], gs[cols, :])
+        prob = w_ref[far * keys : (far + 1) * keys, cols].astype(F32) * scale_ref[:, cols]
+        dp = dot_nt(v, gs[cols, :])
         p_ref[:, cols] = prob.astype(BF16)
         d_ref[:, cols] = (prob * (dp - delta_ref[:, cols])).astype(BF16)
     gkv[:, :HEAD] = (dot(d_ref[...], qs[...]) * FACTOR).astype(BF16)
@@ -149,11 +165,11 @@
     gq_run[...] = more if first is None else first[...] + more
 
 
-def back_kernel(half, parts, blanks, carried, new, last, qs, gs, delta_ref, *refs):
+def back_kernel(half, rows, parts, pieces, blanks, carried, new, last, qs, gs, delta_ref, *refs):
     late = is_late(half)
     refs = list(refs)
     take = lambda n: [refs.pop(0) for _ in range(n)]
-    ins = [take(3) for _ in parts]
+    blocks = [(take(2), take(n)) for n in pieces]
     kept = take(1)[0] if last else None
     first = take(carried)[-1] if carried else None
     outs = take(new)
@@ -162,10 +178,10 @@
     if last:
         copy = pltpu.make_async_copy(kept, out_ref, refs.pop())
         copy.start()
-    keys = ins[0][2].shape[0]
+    keys = half * rows
     block = lambda out, row: outs[out].at[row * keys : (row + 1) * keys, :]
     for when in ("late", "early", "all"):
-        chosen = [i for i, p in enumerate(parts) if p[0] == when]
+        chosen = [p for p in parts if p[0] == when]
         empty = [block(out, row) for w, out, row in blanks if w == when]
         if not chosen and not empty:
             continue
@@ -173,11 +189,10 @@
         def run(chosen=chosen, empty=empty):
             for ref in empty:
                 ref[...] = jnp.zeros_like(ref)
-            for n, i in enumerate(chosen):
-                _, slot, out, row = parts[i][1:]
-                w_ref, scale_ref, kv = ins[i]
+            for n, (_, far, out, row, which) in enumerate(chosen):
+                (w_ref, scale_ref), kv = blocks[which]
                 backward_unit(
-                    qs, gs, w_ref, slot, scale_ref, delta_ref, kv, block(out, row), gq_run,
+                    qs, gs, w_ref, far, scale_ref, delta_ref, kv, rows, block(out, row), gq_run,
                     first if n == 0 else gq_run, refs[2 * n], refs[2 * n + 1],
                 )
 
@@ -186,7 +201,6 @@
         else:
             pl.when(late if when == "late" else jnp.logical_not(late))(run)
     if last:
-        rows = gq_ref.shape[0]
         for h in range(qs.shape[0] // rows):
             g16 = (gq_run[:, h * rows : (h + 1) * rows] * FACTOR).astype(BF16)
             gq_ref[:, h * HEAD : (h + 1) * HEAD] = g16.T
@@ -238,12 +252,6 @@
     ring_down = lambda block: send(block, lambda g: g // half * half + (g - 1) % half, same)
     across = lambda block: send(block, lambda g: (g + half) % grp_count, same)
 
-    def gathered(block):
-        parts = [block]
-        for _ in range(half - 1):
-            parts.append(ring_up(parts[-1]))
-        return jnp.concatenate(parts, axis=0)
-
     def scattered(block):
         slots = [block[s * rows : (s + 1) * rows] for s in range(half)]
         total = slots[-1]
@@ -261,29 +269,40 @@
 
     qs, gs = stacked(queries), stacked(out_grad)
 
+    def block_of(mine):
+        theirs = across(mine)
+        parts = [jnp.concatenate([mine, theirs], axis=0)]
+        for _ in range(half - 1):
+            parts.append(ring_up(parts[-1]))
+        return parts
+
     off = off_chip(own)
-    so = gathered(own)
-    sf = gathered(off)
-    sm = on_chip(so)
-    eo = across(so)
-    ef = across(sf)
-    em = on_chip(eo)
-
-    weights = like((3 * unit, big), BF16)
-    scores = pltpu.VMEM((3, unit, big), F32)
-    o_run, m_run, l_run, nw = call(
-        functools.partial(near_kernel, rows, half, blk_count), [wide, line, line, weights], [scores],
-        3 * unit, [span_order.reshape(1, blk_count), qs, so, sm, sf],
-    )
-    kept, fw, near, far, delta = call(
-        functools.partial(far_kernel, half), [full, weights, line, line, line], [wide_s, line_s, line_s, scores],
-        3 * unit, [qs, gs, eo, em, ef, o_run, m_run, l_run],
-    )
+    own_parts = block_of(own)
+    off_parts = block_of(off)
+    mate_parts = [on_chip(jnp.concatenate(own_parts, axis=0))]
+
+    weights = like((2 * unit, big), BF16)
+    scores = pltpu.VMEM((2, unit, big), F32)
+    span = span_order.reshape(1, blk_count)
+    forward = lambda which: functools.partial(forward_kernel, which, rows, half, blk_count)
+    state = [wide, line, line, weights]
+    o_run, m_own, l_run, w_own = call(forward(0), state, [scores], 2 * unit, [span, qs, *own_parts])
+    o_run, m_mate, l_run, w_mate = call(
+        forward(1), state, [scores], 2 * unit, [span, qs, *mate_parts, o_run, m_own, l_run]
+    )
+    kept, w_off, scale_own, scale_mate, scale_off, delta = call(
+        functools.partial(finish_kernel, rows, half, blk_count), [full, weights, line, line, line, line],
+        [wide_s, line_s, line_s, scores], 2 * unit, [span, qs, gs, *off_parts, m_own, o_run, m_mate, l_run],
+    )
+    saved = {
+        "own": ([w_own, scale_own], own_parts), "mate": ([w_mate, scale_mate], mate_parts), "off": ([w_off, scale_off], off_parts)
+    }
 
     def back(parts, blanks, carry, sizes, gq, last=False):
+        used = list(dict.fromkeys(p[4] for p in parts))
         args = [qs, gs, delta]
-        for _, far_part, slot, _, _, kv in parts:
-            args += [fw, far, kv] if far_part else [nw, near, kv]
+        for key in used:
+            args += saved[key][0] + saved[key][1]
         if last:
             args.append(kept)
         carried = list(carry) + ([] if gq is None else [gq])
@@ -302,19 +321,18 @@
             outs.append(wide)
             if gq is not None:
                 aliases[base + len(carry)] = len(outs) - 1
-        shape = tuple(p[:5] for p in parts)
-        kernel = functools.partial(back_kernel, half, shape, blanks, len(carried), new, last)
+        shape = tuple((when, far, out, row, used.index(key)) for when, far, out, row, key in parts)
+        pieces = tuple(len(saved[key][1]) for key in used)
+        kernel = functools.partial(back_kernel, half, rows, shape, pieces, blanks, len(carried), new, last)
         return call(kernel, outs, temp, unit * len(parts), args, specs, aliases)
 
     gef, gsf, gm, gq = back(
-        [("late", True, 2, 0, 0, ef), ("early", False, 2, 1, 0, sf), ("early", False, 1, 2, 0, sm)],
+        [("late", 1, 0, 0, "off"), ("early", 0, 1, 0, "off"), ("early", 0, 2, 0, "mate")],
         (("early", 0, 0), ("early", 2, 1)), [], [unit, unit, 2 * unit], None,
     )
-    gm, gq = back([("late", True, 1, 0, 1, em), ("late", False, 1, 0, 0, sm)], (), [gm], [], gq)
-    gsf, geo, gq = back(
-        [("late", True, 0, 1, 0, eo), ("late", False, 2, 0, 0, sf)], (("early", 1, 0),), [gsf], [unit], gq
-    )
-    gso, gq, out = back([("all", False, 0, 0, 0, so)], (), [], [unit], gq, last=True)
+    gm, gq = back([("late", 1, 0, 1, "mate"), ("late", 0, 0, 0, "mate")], (), [gm], [], gq)
+    gsf, geo, gq = back([("late", 1, 1, 0, "own"), ("late", 0, 0, 0, "off")], (("early", 1, 0),), [gsf], [unit], gq)
+    gso, gq, out = back([("all", 0, 0, 0, "own")], (), [], [unit], gq, last=True)
 
     back_f = across(gef)
     gsf = add(gsf, back_f)

time: 39.8 us -> 38.9 us (0.977)
  starting transfers between devices: 15 us -> 12.9 us
  Pallas kernels: 4.57 us -> 5.29 us
  waiting for transfers between devices: 16.6 us -> 17.3 us
    ppermute x13 -> x12, starting transfers between devices: 15 us -> 12.9 us  [send(): return lax.ppermute(block, ('grp', 'blk'), route)]
    reshape x2, local copies, waits for them, and re-layouts: 1.04 us -> 0.09 us  [stacked(): x = jnp.transpose(x.reshape(rows, width // HEAD, HEAD), (1, 0, 2))]
    ppermute x13 -> x12, waiting for transfers between devices: 16.6 us -> 17.3 us  [send(): return lax.ppermute(block, ('grp', 'blk'), route)]
    pallas_call x6 -> x7, Pallas kernels: 4.57 us -> 5.29 us  [call(): pl.pallas_call(kernel, out_shape=outs, in_specs=[VMEM] * len(args), out_s...]
    unnamed x5 -> x7, local copies, waits for them, and re-layouts: 0.02 us -> 0.67 us
  transfers between devices with their start and end apart: 13 -> 12, of which waited for: 8 -> 9; matrix products, arithmetic and copies ran while one was open for 3% -> 1% of each run, Pallas kernels for 8% -> 8%
where the time goes in v4:
time: 38.9 us; the launch traced here: 38.8 us
  waiting for transfers between devices  17.3 us (44%)
  starting transfers between devices  12.9 us (33%)
  Pallas kernels  5.29 us (14%)
  local copies, waits for them, and re-layouts  1.41 us (4%)
  other arithmetic  1.02 us (3%)
  between operations  0.8 us (2%)
    ppermute x12, waiting for transfers between devices, send(): return lax.ppermute(block, ('grp', 'blk'), route)  17.3 us
    ppermute x12, starting transfers between devices, send(): return lax.ppermute(block, ('grp', 'blk'), route)  12.9 us
    pallas_call x7, Pallas kernels, call(): pl.pallas_call(kernel, out_shape=outs, in_specs=[VMEM] * len(args), out_s...  5.29 us
    concatenate x1, other arithmetic, step(): own = lax.optimization_barrier(jnp.concatenate([key_rows, values], axis=1))  0.83 us
  transfers between devices with their start and end apart: 12, of which 9 were waited for; matrix products, arithmetic and copies ran while one was open for 1% of the time, Pallas kernels for 8%

profile of v4, /device:TPU:0, one launch (start us, length us, event | category | flops | bytes accessed | tf_op | source)
XLA Modules:
  0.0 38.8 jit_solution(13350199387051495787)
XLA Ops:
  0.6 0.8 %pad_maximum_fusion.2 = bf16[128,256]{1,0:T(8,128)(2,1)S(1)} fusion(bf16[128,128]{1,0:T(8,128)(2,1)} %param.7, bf16[128,128]{1,0:T(8,128)(2,1)} %param.6), kind=kLoop, calls=%fused_computation.10 | loop fusion | flops 131072 | bytes 131072 | tf_op jit(solution)/shard_map/concatenate | solution.py:264
  1.5 3.1 %collective-permute-start.3 = (bf16[128,256]{1,0:T(8,128)(2,1)S(1)}, bf16[128,256]{1,0:T(8,128)(2,1)S(1)}, u32[]{:S(2)}, u32[]{:S(2)}) collective-permute-start(bf16[128,256]{1,0:T(8,128)(2,1)S(1)} %pad_maximum_fusion.2), channel_id=1, source_target_pairs={{0,16},{1,17},{2,18},{3,19},{4,20},{5,21},{6,22},{7,23},{8,24},{9,... | collective-permute-start | bytes 196616 | tf_op jit(solution)/shard_map/ppermute | solution.py:246
  4.5 2.8 %collective-permute-start = (bf16[128,256]{1,0:T(8,128)(2,1)S(1)}, bf16[128,256]{1,0:T(8,128)(2,1)S(1)}, u32[]{:S(2)}, u32[]{:S(2)}) collective-permute-start(bf16[128,256]{1,0:T(8,128)(2,1)S(1)} %pad_maximum_fusion.2), channel_id=1, source_target_pairs={{0,7},{1,2},{2,1},{3,4},{4,3},{5,6},{6,5},{7,0},{8,15},{9,10},{10,... | collective-permute-start | bytes 196616 | tf_op jit(solution)/shard_map/ppermute | solution.py:246
  7.4 1.6 %collective-permute-start.4 = (bf16[256,256]{1,0:T(8,128)(2,1)S(1)}, bf16[256,256]{1,0:T(8,128)(2,1)S(1)}, u32[]{:S(2)}, u32[]{:S(2)}) collective-permute-start(bf16[256,256]{1,0:T(8,128)(2,1)S(1)} %pad_maximum_fusion.1.refs_0_.refs_2_), channel_id=1, source_target_pairs={{0,8},{1,9},{2,10},{3,11},{4,12},{5,13},{6,14},{7,15},{8,0},{9,1},... | collective-permute-start | bytes 393224 | tf_op jit(solution)/shard_map/ppermute | solution.py:246
  8.9 1.4 %collective-permute-done = bf16[128,256]{1,0:T(8,128)(2,1)S(1)} collective-permute-done((bf16[128,256]{1,0:T(8,128)(2,1)S(1)}, bf16[128,256]{1,0:T(8,128)(2,1)S(1)}, u32[]{:S(2)}, u32[]{:S(2)}) %collective-permute-start) | collective-permute-done | bytes 65568 | tf_op jit(solution)/shard_map/ppermute | solution.py:246
  10.4 4.3 %collective-permute-done.1 = bf16[128,256]{1,0:T(8,128)(2,1)S(1)} collective-permute-done((bf16[128,256]{1,0:T(8,128)(2,1)S(1)}, bf16[128,256]{1,0:T(8,128)(2,1)S(1)}, u32[]{:S(2)}, u32[]{:S(2)}) %collective-permute-start.1) | collective-permute-done | bytes 65568 | tf_op jit(solution)/shard_map/ppermute | solution.py:246
  14.6 1.6 %collective-permute-start.2 = (bf16[256,256]{1,0:T(8,128)(2,1)S(1)}, bf16[256,256]{1,0:T(8,128)(2,1)S(1)}, u32[]{:S(2)}, u32[]{:S(2)}) collective-permute-start(bf16[256,256]{1,0:T(8,128)(2,1)S(1)} %constant_dynamic-update-slice_fusion.refs_0_.refs_2_.refs_6_), channel_id=1, source_target_pairs={{0,8},{1,9},{2,10},{3,11},{4,12},{5,13},{6,14},{7,15},{8,0},{9,1},... | collective-permute-start | bytes 393224 | tf_op jit(solution)/shard_map/ppermute | solution.py:246
  16.4 0.6 %copy-done.1 = s32[8]{0:T(128)S(1)} copy-done((s32[8]{0:T(128)S(1)}, s32[8]{0:T(128)}, u32[]{:S(2)}) %copy-start.1) | copy-done | bytes 56
  17.0 0.7 %shard_map.84 = (f32[128,1024]{1,0:T(8,128)S(1)}, f32[1,1024]{1,0:T(1,128)S(1)}, f32[1,1024]{1,0:T(1,128)S(1)}, bf16[512,1024]{1,0:T(8,128)(2,1)S(1)}) custom-call(s32[1,8]{1,0:T(1,128)S(1)} %bitcast.29, bf16[1024,128]{1,0:T(8,128)(2,1)S(1)} %bitcast.17, bf16[256,256]{1,0:T(8,128)(2,1)S(1)} %pad_maximum_fusion.1.refs_0_.refs_2_, ...), custom_call_target="tpu_custom_call" | custom-call | flops 536870912 | bytes 1048576 | tf_op jit(solution)/shard_map/pallas_call | solution.py:216
  17.8 0.7 %shard_map.85 = (f32[128,1024]{1,0:T(8,128)S(1)}, f32[1,1024]{1,0:T(1,128)S(1)}, f32[1,1024]{1,0:T(1,128)S(1)}, bf16[512,1024]{1,0:T(8,128)(2,1)S(1)}) custom-call(s32[1,8]{1,0:T(1,128)S(1)} %bitcast.30, bf16[1024,128]{1,0:T(8,128)(2,1)S(1)} %bitcast.18, bf16[512,256]{1,0:T(8,128)(2,1)S(1)} %collective-permute-done.5.refs_0_.refs_6_.refs_2_, ...), custom_call_target="tpu_custom_call" | custom-call | flops 536870912 | bytes 1048576 | tf_op jit(solution)/shard_map/pallas_call | solution.py:216
  18.6 1.1 %collective-permute-done.2.refs_1_.refs_3_.refs_7_ = bf16[256,256]{1,0:T(8,128)(2,1)S(1)} collective-permute-done((bf16[256,256]{1,0:T(8,128)(2,1)S(1)}, bf16[256,256]{1,0:T(8,128)(2,1)S(1)}, u32[]{:S(2)}, u32[]{:S(2)}) %collective-permute-start.2) | collective-permute-done | bytes 131104 | tf_op jit(solution)/shard_map/ppermute | solution.py:246
  19.7 1.1 %shard_map.86 = (bf16[128,1024]{1,0:T(8,128)(2,1)S(1)}, bf16[512,1024]{1,0:T(8,128)(2,1)S(1)}, f32[1,1024]{1,0:T(1,128)S(1)}, f32[1,1024]{1,0:T(1,128)S(1)}, f32...) custom-call(s32[1,8]{1,0:T(1,128)S(1)} %bitcast.31, bf16[1024,128]{1,0:T(8,128)(2,1)S(1)} %bitcast.19, ...), custom_call_target="tpu_custom_call" | custom-call | flops 536870912 | bytes 1048576 | tf_op jit(solution)/shard_map/pallas_call | solution.py:216
  20.8 1.2 %shard_map.87 = (bf16[256,256]{1,0:T(8,128)(2,1)S(1)}, bf16[256,256]{1,0:T(8,128)(2,1)S(1)}, bf16[512,256]{1,0:T(8,128)(2,1)S(1)}, f32[128,1024]{1,0:T(8,128)S(1)}) custom-call(bf16[1024,128]{1,0:T(8,128)(2,1)S(1)} %bitcast.20, bf16[1024,128]{1,0:T(8,128)(2,1)S(1)} %bitcast.25, f32[1,1024]{1,0:T(1,128)S(1)} %get-tuple-element.36.delta_ref, ...), custom_call_target="tpu_custom_call" | custom-call | flops 805306368 | bytes 1048576 | tf_op jit(solution)/shard_map/pallas_call | solution.py:216
  22.2 1.5 %shard_map.90 = (bf16[256,256]{1,0:T(8,128)(2,1)S(1)}, bf16[128,1024]{1,0:T(8,128)(2,1)}, bf16[128,1024]{1,0:T(8,128)(2,1)}) custom-call(bf16[1024,128]{1,0:T(8,128)(2,1)S(1)} %bitcast.23, bf16[1024,128]{1,0:T(8,128)(2,1)S(1)} %bitcast.28, f32[1,1024]{1,0:T(1,128)S(1)} %get-tuple-element.36.delta_ref, bf16[512,1024]{1,0:T(8,128)(2,1)S(1)} %get-tuple-element.37.refs_0_, ...), custom_call_target="tpu_custom_call" | custom-call | flops 268435456 | bytes 1048576 | tf_op jit(solution)/shard_map/pallas_call | solution.py:216
  23.7 3.3 %collective-permute-done.9 = bf16[256,256]{1,0:T(8,128)(2,1)S(1)} collective-permute-done((bf16[256,256]{1,0:T(8,128)(2,1)S(1)}, bf16[256,256]{1,0:T(8,128)(2,1)S(1)}, u32[]{:S(2)}, u32[]{:S(2)}) %collective-permute-start.9) | collective-permute-done | bytes 131104 | tf_op jit(solution)/shard_map/ppermute | solution.py:246
  27.1 1.6 %collective-permute-start.10 = (bf16[128,256]{1,0:T(8,128)(2,1)S(1)}, bf16[128,256]{1,0:T(8,128)(2,1)S(1)}, u32[]{:S(2)}, u32[]{:S(2)}) collective-permute-start(bf16[128,256]{1,0:T(8,128)(2,1)S(1)} %slice.36), channel_id=1, source_target_pairs={{0,8},{1,9},{2,10},{3,11},{4,12},{5,13},{6,14},{7,15},{8,0},{9,1},... | collective-permute-start | bytes 196616 | tf_op jit(solution)/shard_map/ppermute | solution.py:246
  28.7 1.2 %collective-permute-start.7 = (bf16[256,256]{1,0:T(8,128)(2,1)S(1)}, bf16[256,256]{1,0:T(8,128)(2,1)S(1)}, u32[]{:S(2)}, u32[]{:S(2)}) collective-permute-start(bf16[256,256]{1,0:T(8,128)(2,1)S(1)} %add_convert_fusion.2), channel_id=1, source_target_pairs={{0,16},{1,17},{2,18},{3,19},{4,20},{5,21},{6,22},{7,23},{8,24},{9,... | collective-permute-start | bytes 393224 | tf_op jit(solution)/shard_map/ppermute | solution.py:246
  29.8 1.6 %collective-permute-done.10 = bf16[128,256]{1,0:T(8,128)(2,1)S(1)} collective-permute-done((bf16[128,256]{1,0:T(8,128)(2,1)S(1)}, bf16[128,256]{1,0:T(8,128)(2,1)S(1)}, u32[]{:S(2)}, u32[]{:S(2)}) %collective-permute-start.10) | collective-permute-done | bytes 65568 | tf_op jit(solution)/shard_map/ppermute | solution.py:246
  31.4 0.4 %collective-permute-start.11 = (bf16[128,256]{1,0:T(8,128)(2,1)S(1)}, bf16[128,256]{1,0:T(8,128)(2,1)S(1)}, u32[]{:S(2)}, u32[]{:S(2)}) collective-permute-start(bf16[128,256]{1,0:T(8,128)(2,1)S(1)} %add_convert_fusion.4), channel_id=1, source_target_pairs={{0,7},{1,2},{2,1},{3,4},{4,3},{5,6},{6,5},{7,0},{8,15},{9,10},{10,... | collective-permute-start | bytes 196616 | tf_op jit(solution)/shard_map/ppermute | solution.py:246
  31.9 1.8 %collective-permute-done.7 = bf16[256,256]{1,0:T(8,128)(2,1)S(1)} collective-permute-done((bf16[256,256]{1,0:T(8,128)(2,1)S(1)}, bf16[256,256]{1,0:T(8,128)(2,1)S(1)}, u32[]{:S(2)}, u32[]{:S(2)}) %collective-permute-start.7) | collective-permute-done | bytes 131104 | tf_op jit(solution)/shard_map/ppermute | solution.py:246
  33.8 0.6 %collective-permute-start.8 = (bf16[128,256]{1,0:T(8,128)(2,1)S(1)}, bf16[128,256]{1,0:T(8,128)(2,1)S(1)}, u32[]{:S(2)}, u32[]{:S(2)}) collective-permute-start(bf16[128,256]{1,0:T(8,128)(2,1)S(1)} %slice.34), channel_id=1, source_target_pairs={{0,8},{1,9},{2,10},{3,11},{4,12},{5,13},{6,14},{7,15},{8,0},{9,1},... | collective-permute-start | bytes 196616 | tf_op jit(solution)/shard_map/ppermute | solution.py:246
  34.4 2.9 %collective-permute-done.11 = bf16[128,256]{1,0:T(8,128)(2,1)S(1)} collective-permute-done((bf16[128,256]{1,0:T(8,128)(2,1)S(1)}, bf16[128,256]{1,0:T(8,128)(2,1)S(1)}, u32[]{:S(2)}, u32[]{:S(2)}) %collective-permute-start.11) | collective-permute-done | bytes 65568 | tf_op jit(solution)/shard_map/ppermute | solution.py:246
  37.3 0.8 %collective-permute-done.8 = bf16[128,256]{1,0:T(8,128)(2,1)S(1)} collective-permute-done((bf16[128,256]{1,0:T(8,128)(2,1)S(1)}, bf16[128,256]{1,0:T(8,128)(2,1)S(1)}, u32[]{:S(2)}, u32[]{:S(2)}) %collective-permute-start.8) | collective-permute-done | bytes 65568 | tf_op jit(solution)/shard_map/ppermute | solution.py:246
  38.1 0.6 %fusion = (bf16[128,128]{1,0:T(8,128)(2,1)}, bf16[128,128]{1,0:T(8,128)(2,1)}) fusion(bf16[128,256]{1,0:T(8,128)(2,1)S(1)} %add_convert_fusion.3), kind=kLoop, calls=%fused_computation.13 | loop fusion | bytes 131072 | tf_op jit(solution)/shard_map/slice | solution.py:347
  (28 shorter events, 0.7 us)
Async XLA Ops:
  0.6 6.7 %copy-start = (bf16[128,1024]{1,0:T(8,128)(2,1)S(1)}, bf16[128,1024]{1,0:T(8,128)(2,1)}, u32[]{:S(2)}) copy-start(bf16[128,1024]{1,0:T(8,128)(2,1)} %param.5) | copy-start | bytes 786436
  1.5 5.9 %collective-permute-start.3 = (bf16[128,256]{1,0:T(8,128)(2,1)S(1)}, bf16[128,256]{1,0:T(8,128)(2,1)S(1)}, u32[]{:S(2)}, u32[]{:S(2)}) collective-permute-start(bf16[128,256]{1,0:T(8,128)(2,1)S(1)} %pad_maximum_fusion.2), channel_id=1, source_target_pairs={{0,16},{1,17},{2,18},{3,19},{4,20},{5,21},{6,22},{7,23},{8,24},{9,... | collective-permute-start | bytes 196616 | tf_op jit(solution)/shard_map/ppermute | solution.py:246
  4.5 5.8 %collective-permute-start = (bf16[128,256]{1,0:T(8,128)(2,1)S(1)}, bf16[128,256]{1,0:T(8,128)(2,1)S(1)}, u32[]{:S(2)}, u32[]{:S(2)}) collective-permute-start(bf16[128,256]{1,0:T(8,128)(2,1)S(1)} %pad_maximum_fusion.2), channel_id=1, source_target_pairs={{0,7},{1,2},{2,1},{3,4},{4,3},{5,6},{6,5},{7,0},{8,15},{9,10},{10,... | collective-permute-start | bytes 196616 | tf_op jit(solution)/shard_map/ppermute | solution.py:246
  7.4 8.8 %collective-permute-start.4 = (bf16[256,256]{1,0:T(8,128)(2,1)S(1)}, bf16[256,256]{1,0:T(8,128)(2,1)S(1)}, u32[]{:S(2)}, u32[]{:S(2)}) collective-permute-start(bf16[256,256]{1,0:T(8,128)(2,1)S(1)} %pad_maximum_fusion.1.refs_0_.refs_2_), channel_id=1, source_target_pairs={{0,8},{1,9},{2,10},{3,11},{4,12},{5,13},{6,14},{7,15},{8,0},{9,1},... | collective-permute-start | bytes 393224 | tf_op jit(solution)/shard_map/ppermute | solution.py:246
  10.4 4.3 %collective-permute-start.1 = (bf16[128,256]{1,0:T(8,128)(2,1)S(1)}, bf16[128,256]{1,0:T(8,128)(2,1)S(1)}, u32[]{:S(2)}, u32[]{:S(2)}) collective-permute-start(bf16[128,256]{1,0:T(8,128)(2,1)S(1)} %collective-permute-done), channel_id=1, source_target_pairs={{0,16},{1,17},{2,18},{3,19},{4,20},{5,21},{6,22},{7,23},{8,24},{9,... | collective-permute-start | bytes 196616 | tf_op jit(solution)/shard_map/ppermute | solution.py:246
  14.6 1.7 %copy-start.2 = (bf16[128,1024]{1,0:T(8,128)(2,1)S(1)}, bf16[128,1024]{1,0:T(8,128)(2,1)}, u32[]{:S(2)}) copy-start(bf16[128,1024]{1,0:T(8,128)(2,1)} %param.8) | copy-start | bytes 786436
  14.6 5.0 %collective-permute-start.2 = (bf16[256,256]{1,0:T(8,128)(2,1)S(1)}, bf16[256,256]{1,0:T(8,128)(2,1)S(1)}, u32[]{:S(2)}, u32[]{:S(2)}) collective-permute-start(bf16[256,256]{1,0:T(8,128)(2,1)S(1)} %constant_dynamic-update-slice_fusion.refs_0_.refs_2_.refs_6_), channel_id=1, source_target_pairs={{0,8},{1,9},{2,10},{3,11},{4,12},{5,13},{6,14},{7,15},{8,0},{9,1},... | collective-permute-start | bytes 393224 | tf_op jit(solution)/shard_map/ppermute | solution.py:246
  16.2 1.6 %collective-permute-start.5 = (bf16[512,256]{1,0:T(8,128)(2,1)S(1)}, bf16[512,256]{1,0:T(8,128)(2,1)S(1)}, u32[]{:S(2)}, u32[]{:S(2)}) collective-permute-start(bf16[512,256]{1,0:T(8,128)(2,1)S(1)} %pad_maximum_fusion), channel_id=1, source_target_pairs={{0,1},{1,0},{2,3},{3,2},{4,5},{5,4},{6,7},{7,6},{8,9},{9,8},{10,11... | collective-permute-start | bytes 786440 | tf_op jit(solution)/shard_map/ppermute | solution.py:246
  16.4 0.7 %copy-start.1 = (s32[8]{0:T(128)S(1)}, s32[8]{0:T(128)}, u32[]{:S(2)}) copy-start(s32[8]{0:T(128)} %param.9) | copy-start | bytes 100
  22.0 5.0 %collective-permute-start.9 = (bf16[256,256]{1,0:T(8,128)(2,1)S(1)}, bf16[256,256]{1,0:T(8,128)(2,1)S(1)}, u32[]{:S(2)}, u32[]{:S(2)}) collective-permute-start(bf16[256,256]{1,0:T(8,128)(2,1)S(1)} %get-tuple-element.55), channel_id=1, source_target_pairs={{0,16},{1,17},{2,18},{3,19},{4,20},{5,21},{6,22},{7,23},{8,24},{9,... | collective-permute-start | bytes 393224 | tf_op jit(solution)/shard_map/ppermute | solution.py:246
  22.1 6.5 %collective-permute-start.6 = (bf16[512,256]{1,0:T(8,128)(2,1)S(1)}, bf16[512,256]{1,0:T(8,128)(2,1)S(1)}, u32[]{:S(2)}, u32[]{:S(2)}) collective-permute-start(bf16[512,256]{1,0:T(8,128)(2,1)S(1)} %get-tuple-element.52), channel_id=1, source_target_pairs={{0,1},{1,0},{2,3},{3,2},{4,5},{5,4},{6,7},{7,6},{8,9},{9,8},{10,11... | collective-permute-start | bytes 786440 | tf_op jit(solution)/shard_map/ppermute | solution.py:246
  27.1 4.3 %collective-permute-start.10 = (bf16[128,256]{1,0:T(8,128)(2,1)S(1)}, bf16[128,256]{1,0:T(8,128)(2,1)S(1)}, u32[]{:S(2)}, u32[]{:S(2)}) collective-permute-start(bf16[128,256]{1,0:T(8,128)(2,1)S(1)} %slice.36), channel_id=1, source_target_pairs={{0,8},{1,9},{2,10},{3,11},{4,12},{5,13},{6,14},{7,15},{8,0},{9,1},... | collective-permute-start | bytes 196616 | tf_op jit(solution)/shard_map/ppermute | solution.py:246
  28.7 5.0 %collective-permute-start.7 = (bf16[256,256]{1,0:T(8,128)(2,1)S(1)}, bf16[256,256]{1,0:T(8,128)(2,1)S(1)}, u32[]{:S(2)}, u32[]{:S(2)}) collective-permute-start(bf16[256,256]{1,0:T(8,128)(2,1)S(1)} %add_convert_fusion.2), channel_id=1, source_target_pairs={{0,16},{1,17},{2,18},{3,19},{4,20},{5,21},{6,22},{7,23},{8,24},{9,... | collective-permute-start | bytes 393224 | tf_op jit(solution)/shard_map/ppermute | solution.py:246
  31.4 5.9 %collective-permute-start.11 = (bf16[128,256]{1,0:T(8,128)(2,1)S(1)}, bf16[128,256]{1,0:T(8,128)(2,1)S(1)}, u32[]{:S(2)}, u32[]{:S(2)}) collective-permute-start(bf16[128,256]{1,0:T(8,128)(2,1)S(1)} %add_convert_fusion.4), channel_id=1, source_target_pairs={{0,7},{1,2},{2,1},{3,4},{4,3},{5,6},{6,5},{7,0},{8,15},{9,10},{10,... | collective-permute-start | bytes 196616 | tf_op jit(solution)/shard_map/ppermute | solution.py:246
  33.8 4.3 %collective-permute-start.8 = (bf16[128,256]{1,0:T(8,128)(2,1)S(1)}, bf16[128,256]{1,0:T(8,128)(2,1)S(1)}, u32[]{:S(2)}, u32[]{:S(2)}) collective-permute-start(bf16[128,256]{1,0:T(8,128)(2,1)S(1)} %slice.34), channel_id=1, source_target_pairs={{0,8},{1,9},{2,10},{3,11},{4,12},{5,13},{6,14},{7,15},{8,0},{9,1},... | collective-permute-start | bytes 196616 | tf_op jit(solution)/shard_map/ppermute | solution.py:246

commit v5 on v4

--- a/solution.py
+++ b/solution.py
@@ -31,7 +31,7 @@
     blk = lax.axis_index("blk")
     late = lax.axis_index("grp") >= half
     step = jnp.where(lax.rem(blk, 2) == 0, 1, -1)
-    span = span_ref[...]
+    span = span_ref[:1, :]
     ids = lax.broadcasted_iota(jnp.int32, span.shape, 1)
     pick = lambda b: jnp.sum(jnp.where(ids == lax.rem(b + blk_count, blk_count), span, 0), axis=1, keepdims=True)
     mine = pick(blk)
@@ -252,11 +252,13 @@
     ring_down = lambda block: send(block, lambda g: g // half * half + (g - 1) % half, same)
     across = lambda block: send(block, lambda g: (g + half) % grp_count, same)
 
-    def scattered(block):
+    def scattered(block, apart=False):
         slots = [block[s * rows : (s + 1) * rows] for s in range(half)]
         total = slots[-1]
         for s in range(half - 2, -1, -1):
             moved = ring_down(total)
+            if s == 0 and apart:
+                return slots[0], moved
             total = add(moved, slots[s])
         return total
 
@@ -268,6 +270,7 @@
         return lax.optimization_barrier(x.reshape(big, HEAD))
 
     qs, gs = stacked(queries), stacked(out_grad)
+    span = lax.optimization_barrier(jnp.maximum(jnp.broadcast_to(span_order[None, :], (8, blk_count)), 0))
 
     def block_of(mine):
         theirs = across(mine)
@@ -283,7 +286,6 @@
 
     weights = like((2 * unit, big), BF16)
     scores = pltpu.VMEM((2, unit, big), F32)
-    span = span_order.reshape(1, blk_count)
     forward = lambda which: functools.partial(forward_kernel, which, rows, half, blk_count)
     state = [wide, line, line, weights]
     o_run, m_own, l_run, w_own = call(forward(0), state, [scores], 2 * unit, [span, qs, *own_parts])
@@ -343,8 +345,12 @@
     back_o = across(geo)
     gso = gso.astype(F32) + mate[:unit].astype(F32)
     gso = (gso + back_o.astype(F32)).astype(BF16)
-    final = add(scattered(gso), ret_f)
-    return (out, gq, final[:, :HEAD], final[:, HEAD:])
+    mine, moved = scattered(gso, True)
+
+    def final(part):
+        return (mine[:, part].astype(F32) + moved[:, part].astype(F32) + ret_f[:, part].astype(F32)).astype(BF16)
+
+    return (out, gq, final(slice(0, HEAD)), final(slice(HEAD, 2 * HEAD)))
 
 
 def solution(mesh):

time: 38.9 us -> 38.9 us (level)
  local copies, waits for them, and re-layouts: 1.41 us -> 0.14 us
  other arithmetic: 1.02 us -> 1.65 us
  waiting for transfers between devices: 17.3 us -> 17.9 us
    convert_element_type x0 -> x1, other arithmetic: none -> 0.66 us  [final(): (mine[:, part].astype(F32) + moved[:, part].astype(F32) + ret_f[:, part]....]
    unnamed x7, local copies, waits for them, and re-layouts: 0.67 us -> 0.02 us
    slice x1 -> x0, local copies, waits for them, and re-layouts: 0.63 us -> none  [step(): return (out, gq, final[:, :HEAD], final[:, HEAD:])]
    ppermute x12, waiting for transfers between devices: 17.3 us -> 17.9 us  [send(): return lax.ppermute(block, ('grp', 'blk'), route)]
where the time goes in v5:
time: 38.9 us; the launch traced here: 38.8 us
  waiting for transfers between devices  17.9 us (46%)
  starting transfers between devices  12.9 us (33%)
  Pallas kernels  5.29 us (14%)
  other arithmetic  1.65 us (4%)
  between operations  0.82 us (2%)
    ppermute x12, waiting for transfers between devices, send(): return lax.ppermute(block, ('grp', 'blk'), route)  17.9 us
    ppermute x12, starting transfers between devices, send(): return lax.ppermute(block, ('grp', 'blk'), route)  12.9 us
    pallas_call x7, Pallas kernels, call(): pl.pallas_call(kernel, out_shape=outs, in_specs=[VMEM] * len(args), out_s...  5.29 us
    concatenate x1, other arithmetic, step(): own = lax.optimization_barrier(jnp.concatenate([key_rows, values], axis=1))  0.83 us
  transfers between devices with their start and end apart: 12, of which 9 were waited for; matrix products, arithmetic and copies ran while one was open for 1% of the time, Pallas kernels for 8%

profile of v5, /device:TPU:0, one launch (start us, length us, event | category | flops | bytes accessed | tf_op | source)
XLA Modules:
  0.0 38.8 jit_solution(11223396033507683783)
XLA Ops:
  0.6 0.8 %pad_maximum_fusion.2 = bf16[128,256]{1,0:T(8,128)(2,1)S(1)} fusion(bf16[128,128]{1,0:T(8,128)(2,1)} %param.7, bf16[128,128]{1,0:T(8,128)(2,1)} %param.6), kind=kLoop, calls=%fused_computation.8 | loop fusion | flops 131072 | bytes 131072 | tf_op jit(solution)/shard_map/concatenate | solution.py:266
  1.5 3.1 %collective-permute-start.3 = (bf16[128,256]{1,0:T(8,128)(2,1)S(1)}, bf16[128,256]{1,0:T(8,128)(2,1)S(1)}, u32[]{:S(2)}, u32[]{:S(2)}) collective-permute-start(bf16[128,256]{1,0:T(8,128)(2,1)S(1)} %pad_maximum_fusion.2), channel_id=1, source_target_pairs={{0,16},{1,17},{2,18},{3,19},{4,20},{5,21},{6,22},{7,23},{8,24},{9,... | collective-permute-start | bytes 196616 | tf_op jit(solution)/shard_map/ppermute | solution.py:246
  4.5 2.8 %collective-permute-start = (bf16[128,256]{1,0:T(8,128)(2,1)S(1)}, bf16[128,256]{1,0:T(8,128)(2,1)S(1)}, u32[]{:S(2)}, u32[]{:S(2)}) collective-permute-start(bf16[128,256]{1,0:T(8,128)(2,1)S(1)} %pad_maximum_fusion.2), channel_id=1, source_target_pairs={{0,7},{1,2},{2,1},{3,4},{4,3},{5,6},{6,5},{7,0},{8,15},{9,10},{10,... | collective-permute-start | bytes 196616 | tf_op jit(solution)/shard_map/ppermute | solution.py:246
  7.5 1.6 %collective-permute-start.4 = (bf16[256,256]{1,0:T(8,128)(2,1)S(1)}, bf16[256,256]{1,0:T(8,128)(2,1)S(1)}, u32[]{:S(2)}, u32[]{:S(2)}) collective-permute-start(bf16[256,256]{1,0:T(8,128)(2,1)S(1)} %pad_maximum_fusion.1.refs_0_.refs_2_), channel_id=1, source_target_pairs={{0,8},{1,9},{2,10},{3,11},{4,12},{5,13},{6,14},{7,15},{8,0},{9,1},... | collective-permute-start | bytes 393224 | tf_op jit(solution)/shard_map/ppermute | solution.py:246
  9.0 1.4 %collective-permute-done = bf16[128,256]{1,0:T(8,128)(2,1)S(1)} collective-permute-done((bf16[128,256]{1,0:T(8,128)(2,1)S(1)}, bf16[128,256]{1,0:T(8,128)(2,1)S(1)}, u32[]{:S(2)}, u32[]{:S(2)}) %collective-permute-start) | collective-permute-done | bytes 65568 | tf_op jit(solution)/shard_map/ppermute | solution.py:246
  10.4 4.3 %collective-permute-done.1 = bf16[128,256]{1,0:T(8,128)(2,1)S(1)} collective-permute-done((bf16[128,256]{1,0:T(8,128)(2,1)S(1)}, bf16[128,256]{1,0:T(8,128)(2,1)S(1)}, u32[]{:S(2)}, u32[]{:S(2)}) %collective-permute-start.1) | collective-permute-done | bytes 65568 | tf_op jit(solution)/shard_map/ppermute | solution.py:246
  14.7 1.6 %collective-permute-start.2 = (bf16[256,256]{1,0:T(8,128)(2,1)S(1)}, bf16[256,256]{1,0:T(8,128)(2,1)S(1)}, u32[]{:S(2)}, u32[]{:S(2)}) collective-permute-start(bf16[256,256]{1,0:T(8,128)(2,1)S(1)} %constant_dynamic-update-slice_fusion.refs_0_.refs_2_.refs_6_), channel_id=1, source_target_pairs={{0,8},{1,9},{2,10},{3,11},{4,12},{5,13},{6,14},{7,15},{8,0},{9,1},... | collective-permute-start | bytes 393224 | tf_op jit(solution)/shard_map/ppermute | solution.py:246
  16.3 0.7 %shard_map.84 = (f32[128,1024]{1,0:T(8,128)S(1)}, f32[1,1024]{1,0:T(1,128)S(1)}, f32[1,1024]{1,0:T(1,128)S(1)}, bf16[512,1024]{1,0:T(8,128)(2,1)S(1)}) custom-call(s32[8,8]{1,0:T(8,128)S(1)} %broadcast_in_dim.2.span_ref, bf16[1024,128]{1,0:T(8,128)(2,1)S(1)} %bitcast.16, bf16[256,256]{1,0:T(8,128)(2,1)S(1)} %pad_maximum_fusion.1.refs_0_.refs_2_, ...), custom_call_target="tpu_custom_call" | custom-call | flops 536870912 | bytes 1048576 | tf_op jit(solution)/shard_map/pallas_call | solution.py:216
  17.0 0.8 %collective-permute-done.5.refs_0_.refs_6_.refs_2_ = bf16[512,256]{1,0:T(8,128)(2,1)S(1)} collective-permute-done((bf16[512,256]{1,0:T(8,128)(2,1)S(1)}, bf16[512,256]{1,0:T(8,128)(2,1)S(1)}, u32[]{:S(2)}, u32[]{:S(2)}) %collective-permute-start.5) | collective-permute-done | bytes 262176 | tf_op jit(solution)/shard_map/ppermute | solution.py:246
  17.8 0.7 %shard_map.85 = (f32[128,1024]{1,0:T(8,128)S(1)}, f32[1,1024]{1,0:T(1,128)S(1)}, f32[1,1024]{1,0:T(1,128)S(1)}, bf16[512,1024]{1,0:T(8,128)(2,1)S(1)}) custom-call(s32[8,8]{1,0:T(8,128)S(1)} %broadcast_in_dim.2.span_ref, bf16[1024,128]{1,0:T(8,128)(2,1)S(1)} %bitcast.17, bf16[512,256]{1,0:T(8,128)(2,1)S(1)} %collective-permute-done.5.refs_0_.refs_6_.refs_2_, ...), custom_call_target="tpu_custom_call" | custom-call | flops 536870912 | bytes 1048576 | tf_op jit(solution)/shard_map/pallas_call | solution.py:216
  18.6 1.1 %collective-permute-done.2.refs_1_.refs_3_.refs_7_ = bf16[256,256]{1,0:T(8,128)(2,1)S(1)} collective-permute-done((bf16[256,256]{1,0:T(8,128)(2,1)S(1)}, bf16[256,256]{1,0:T(8,128)(2,1)S(1)}, u32[]{:S(2)}, u32[]{:S(2)}) %collective-permute-start.2) | collective-permute-done | bytes 131104 | tf_op jit(solution)/shard_map/ppermute | solution.py:246
  19.7 1.1 %shard_map.86 = (bf16[128,1024]{1,0:T(8,128)(2,1)S(1)}, bf16[512,1024]{1,0:T(8,128)(2,1)S(1)}, f32[1,1024]{1,0:T(1,128)S(1)}, f32[1,1024]{1,0:T(1,128)S(1)}, f32...) custom-call(s32[8,8]{1,0:T(8,128)S(1)} %broadcast_in_dim.2.span_ref, bf16[1024,128]{1,0:T(8,128)(2,1)S(1)} %bitcast.18, ...), custom_call_target="tpu_custom_call" | custom-call | flops 536870912 | bytes 1048576 | tf_op jit(solution)/shard_map/pallas_call | solution.py:216
  20.8 1.2 %shard_map.87 = (bf16[256,256]{1,0:T(8,128)(2,1)S(1)}, bf16[256,256]{1,0:T(8,128)(2,1)S(1)}, bf16[512,256]{1,0:T(8,128)(2,1)S(1)}, f32[128,1024]{1,0:T(8,128)S(1)}) custom-call(bf16[1024,128]{1,0:T(8,128)(2,1)S(1)} %bitcast.19, bf16[1024,128]{1,0:T(8,128)(2,1)S(1)} %bitcast.24, f32[1,1024]{1,0:T(1,128)S(1)} %get-tuple-element.36.delta_ref, ...), custom_call_target="tpu_custom_call" | custom-call | flops 805306368 | bytes 1048576 | tf_op jit(solution)/shard_map/pallas_call | solution.py:216
  22.2 1.5 %shard_map.90 = (bf16[256,256]{1,0:T(8,128)(2,1)S(1)}, bf16[128,1024]{1,0:T(8,128)(2,1)}, bf16[128,1024]{1,0:T(8,128)(2,1)}) custom-call(bf16[1024,128]{1,0:T(8,128)(2,1)S(1)} %bitcast.22, bf16[1024,128]{1,0:T(8,128)(2,1)S(1)} %bitcast.27, f32[1,1024]{1,0:T(1,128)S(1)} %get-tuple-element.36.delta_ref, bf16[512,1024]{1,0:T(8,128)(2,1)S(1)} %get-tuple-element.37.refs_0_, ...), custom_call_target="tpu_custom_call" | custom-call | flops 268435456 | bytes 1048576 | tf_op jit(solution)/shard_map/pallas_call | solution.py:216
  23.8 3.3 %collective-permute-done.9 = bf16[256,256]{1,0:T(8,128)(2,1)S(1)} collective-permute-done((bf16[256,256]{1,0:T(8,128)(2,1)S(1)}, bf16[256,256]{1,0:T(8,128)(2,1)S(1)}, u32[]{:S(2)}, u32[]{:S(2)}) %collective-permute-start.9) | collective-permute-done | bytes 131104 | tf_op jit(solution)/shard_map/ppermute | solution.py:246
  27.1 1.6 %collective-permute-start.10 = (bf16[128,256]{1,0:T(8,128)(2,1)S(1)}, bf16[128,256]{1,0:T(8,128)(2,1)S(1)}, u32[]{:S(2)}, u32[]{:S(2)}) collective-permute-start(bf16[128,256]{1,0:T(8,128)(2,1)S(1)} %slice.52), channel_id=1, source_target_pairs={{0,8},{1,9},{2,10},{3,11},{4,12},{5,13},{6,14},{7,15},{8,0},{9,1},... | collective-permute-start | bytes 196616 | tf_op jit(solution)/shard_map/ppermute | solution.py:246
  28.7 1.2 %collective-permute-start.7 = (bf16[256,256]{1,0:T(8,128)(2,1)S(1)}, bf16[256,256]{1,0:T(8,128)(2,1)S(1)}, u32[]{:S(2)}, u32[]{:S(2)}) collective-permute-start(bf16[256,256]{1,0:T(8,128)(2,1)S(1)} %add_convert_fusion.2), channel_id=1, source_target_pairs={{0,16},{1,17},{2,18},{3,19},{4,20},{5,21},{6,22},{7,23},{8,24},{9,... | collective-permute-start | bytes 393224 | tf_op jit(solution)/shard_map/ppermute | solution.py:246
  29.8 1.6 %collective-permute-done.10 = bf16[128,256]{1,0:T(8,128)(2,1)S(1)} collective-permute-done((bf16[128,256]{1,0:T(8,128)(2,1)S(1)}, bf16[128,256]{1,0:T(8,128)(2,1)S(1)}, u32[]{:S(2)}, u32[]{:S(2)}) %collective-permute-start.10) | collective-permute-done | bytes 65568 | tf_op jit(solution)/shard_map/ppermute | solution.py:246
  31.4 0.4 %collective-permute-start.11 = (bf16[128,256]{1,0:T(8,128)(2,1)S(1)}, bf16[128,256]{1,0:T(8,128)(2,1)S(1)}, u32[]{:S(2)}, u32[]{:S(2)}) collective-permute-start(bf16[128,256]{1,0:T(8,128)(2,1)S(1)} %add_convert_fusion.3), channel_id=1, source_target_pairs={{0,7},{1,2},{2,1},{3,4},{4,3},{5,6},{6,5},{7,0},{8,15},{9,10},{10,... | collective-permute-start | bytes 196616 | tf_op jit(solution)/shard_map/ppermute | solution.py:246
  31.9 1.8 %collective-permute-done.7 = bf16[256,256]{1,0:T(8,128)(2,1)S(1)} collective-permute-done((bf16[256,256]{1,0:T(8,128)(2,1)S(1)}, bf16[256,256]{1,0:T(8,128)(2,1)S(1)}, u32[]{:S(2)}, u32[]{:S(2)}) %collective-permute-start.7) | collective-permute-done | bytes 131104 | tf_op jit(solution)/shard_map/ppermute | solution.py:246
  33.8 0.6 %collective-permute-start.8 = (bf16[128,256]{1,0:T(8,128)(2,1)S(1)}, bf16[128,256]{1,0:T(8,128)(2,1)S(1)}, u32[]{:S(2)}, u32[]{:S(2)}) collective-permute-start(bf16[128,256]{1,0:T(8,128)(2,1)S(1)} %slice.50), channel_id=1, source_target_pairs={{0,8},{1,9},{2,10},{3,11},{4,12},{5,13},{6,14},{7,15},{8,0},{9,1},... | collective-permute-start | bytes 196616 | tf_op jit(solution)/shard_map/ppermute | solution.py:246
  34.4 2.9 %collective-permute-done.11 = bf16[128,256]{1,0:T(8,128)(2,1)S(1)} collective-permute-done((bf16[128,256]{1,0:T(8,128)(2,1)S(1)}, bf16[128,256]{1,0:T(8,128)(2,1)S(1)}, u32[]{:S(2)}, u32[]{:S(2)}) %collective-permute-start.11) | collective-permute-done | bytes 65568 | tf_op jit(solution)/shard_map/ppermute | solution.py:246
  37.3 0.8 %collective-permute-done.8 = bf16[128,256]{1,0:T(8,128)(2,1)S(1)} collective-permute-done((bf16[128,256]{1,0:T(8,128)(2,1)S(1)}, bf16[128,256]{1,0:T(8,128)(2,1)S(1)}, u32[]{:S(2)}, u32[]{:S(2)}) %collective-permute-start.8) | collective-permute-done | bytes 65568 | tf_op jit(solution)/shard_map/ppermute | solution.py:246
  38.1 0.7 %add_convert_fusion.4 = (bf16[128,128]{1,0:T(8,128)(2,1)}, bf16[128,128]{1,0:T(8,128)(2,1)}) fusion(bf16[128,256]{1,0:T(8,128)(2,1)S(1)} %collective-permute-done.11, bf16[128,256]{1,0:T(8,128)(2,1)S(1)} %collective-permute-done.8, bf16[256,256]{1,0:T(8,128)(2,1)S(1)} %add_convert_fusion.1), kind=kLoop, calls=%fused_computation.9 | loop fusion | flops 196608 | bytes 262144 | tf_op jit(solution)/shard_map/convert_element_type | solution.py:351
  (29 shorter events, 0.6 us)
Async XLA Ops:
  0.6 6.7 %copy-start = (bf16[128,1024]{1,0:T(8,128)(2,1)S(1)}, bf16[128,1024]{1,0:T(8,128)(2,1)}, u32[]{:S(2)}) copy-start(bf16[128,1024]{1,0:T(8,128)(2,1)} %param.5) | copy-start | bytes 786436
  1.5 5.9 %copy-start.1 = (bf16[128,1024]{1,0:T(8,128)(2,1)S(1)}, bf16[128,1024]{1,0:T(8,128)(2,1)}, u32[]{:S(2)}) copy-start(bf16[128,1024]{1,0:T(8,128)(2,1)} %param.8) | copy-start | bytes 786436
  1.5 5.9 %collective-permute-start.3 = (bf16[128,256]{1,0:T(8,128)(2,1)S(1)}, bf16[128,256]{1,0:T(8,128)(2,1)S(1)}, u32[]{:S(2)}, u32[]{:S(2)}) collective-permute-start(bf16[128,256]{1,0:T(8,128)(2,1)S(1)} %pad_maximum_fusion.2), channel_id=1, source_target_pairs={{0,16},{1,17},{2,18},{3,19},{4,20},{5,21},{6,22},{7,23},{8,24},{9,... | collective-permute-start | bytes 196616 | tf_op jit(solution)/shard_map/ppermute | solution.py:246
  4.5 5.8 %collective-permute-start = (bf16[128,256]{1,0:T(8,128)(2,1)S(1)}, bf16[128,256]{1,0:T(8,128)(2,1)S(1)}, u32[]{:S(2)}, u32[]{:S(2)}) collective-permute-start(bf16[128,256]{1,0:T(8,128)(2,1)S(1)} %pad_maximum_fusion.2), channel_id=1, source_target_pairs={{0,7},{1,2},{2,1},{3,4},{4,3},{5,6},{6,5},{7,0},{8,15},{9,10},{10,... | collective-permute-start | bytes 196616 | tf_op jit(solution)/shard_map/ppermute | solution.py:246
  7.5 8.8 %collective-permute-start.4 = (bf16[256,256]{1,0:T(8,128)(2,1)S(1)}, bf16[256,256]{1,0:T(8,128)(2,1)S(1)}, u32[]{:S(2)}, u32[]{:S(2)}) collective-permute-start(bf16[256,256]{1,0:T(8,128)(2,1)S(1)} %pad_maximum_fusion.1.refs_0_.refs_2_), channel_id=1, source_target_pairs={{0,8},{1,9},{2,10},{3,11},{4,12},{5,13},{6,14},{7,15},{8,0},{9,1},... | collective-permute-start | bytes 393224 | tf_op jit(solution)/shard_map/ppermute | solution.py:246
  10.4 4.3 %collective-permute-start.1 = (bf16[128,256]{1,0:T(8,128)(2,1)S(1)}, bf16[128,256]{1,0:T(8,128)(2,1)S(1)}, u32[]{:S(2)}, u32[]{:S(2)}) collective-permute-start(bf16[128,256]{1,0:T(8,128)(2,1)S(1)} %collective-permute-done), channel_id=1, source_target_pairs={{0,16},{1,17},{2,18},{3,19},{4,20},{5,21},{6,22},{7,23},{8,24},{9,... | collective-permute-start | bytes 196616 | tf_op jit(solution)/shard_map/ppermute | solution.py:246
  14.6 1.7 %copy-start.2 = (s32[8]{0:T(128)S(1)}, s32[8]{0:T(128)}, u32[]{:S(2)}) copy-start(s32[8]{0:T(128)} %param.9) | copy-start | bytes 100
  14.7 5.0 %collective-permute-start.2 = (bf16[256,256]{1,0:T(8,128)(2,1)S(1)}, bf16[256,256]{1,0:T(8,128)(2,1)S(1)}, u32[]{:S(2)}, u32[]{:S(2)}) collective-permute-start(bf16[256,256]{1,0:T(8,128)(2,1)S(1)} %constant_dynamic-update-slice_fusion.refs_0_.refs_2_.refs_6_), channel_id=1, source_target_pairs={{0,8},{1,9},{2,10},{3,11},{4,12},{5,13},{6,14},{7,15},{8,0},{9,1},... | collective-permute-start | bytes 393224 | tf_op jit(solution)/shard_map/ppermute | solution.py:246
  16.2 1.6 %collective-permute-start.5 = (bf16[512,256]{1,0:T(8,128)(2,1)S(1)}, bf16[512,256]{1,0:T(8,128)(2,1)S(1)}, u32[]{:S(2)}, u32[]{:S(2)}) collective-permute-start(bf16[512,256]{1,0:T(8,128)(2,1)S(1)} %pad_maximum_fusion), channel_id=1, source_target_pairs={{0,1},{1,0},{2,3},{3,2},{4,5},{5,4},{6,7},{7,6},{8,9},{9,8},{10,11... | collective-permute-start | bytes 786440 | tf_op jit(solution)/shard_map/ppermute | solution.py:246
  22.0 5.0 %collective-permute-start.9 = (bf16[256,256]{1,0:T(8,128)(2,1)S(1)}, bf16[256,256]{1,0:T(8,128)(2,1)S(1)}, u32[]{:S(2)}, u32[]{:S(2)}) collective-permute-start(bf16[256,256]{1,0:T(8,128)(2,1)S(1)} %get-tuple-element.55), channel_id=1, source_target_pairs={{0,16},{1,17},{2,18},{3,19},{4,20},{5,21},{6,22},{7,23},{8,24},{9,... | collective-permute-start | bytes 393224 | tf_op jit(solution)/shard_map/ppermute | solution.py:246
  22.1 6.5 %collective-permute-start.6 = (bf16[512,256]{1,0:T(8,128)(2,1)S(1)}, bf16[512,256]{1,0:T(8,128)(2,1)S(1)}, u32[]{:S(2)}, u32[]{:S(2)}) collective-permute-start(bf16[512,256]{1,0:T(8,128)(2,1)S(1)} %get-tuple-element.52), channel_id=1, source_target_pairs={{0,1},{1,0},{2,3},{3,2},{4,5},{5,4},{6,7},{7,6},{8,9},{9,8},{10,11... | collective-permute-start | bytes 786440 | tf_op jit(solution)/shard_map/ppermute | solution.py:246
  27.1 4.3 %collective-permute-start.10 = (bf16[128,256]{1,0:T(8,128)(2,1)S(1)}, bf16[128,256]{1,0:T(8,128)(2,1)S(1)}, u32[]{:S(2)}, u32[]{:S(2)}) collective-permute-start(bf16[128,256]{1,0:T(8,128)(2,1)S(1)} %slice.52), channel_id=1, source_target_pairs={{0,8},{1,9},{2,10},{3,11},{4,12},{5,13},{6,14},{7,15},{8,0},{9,1},... | collective-permute-start | bytes 196616 | tf_op jit(solution)/shard_map/ppermute | solution.py:246
  28.7 5.0 %collective-permute-start.7 = (bf16[256,256]{1,0:T(8,128)(2,1)S(1)}, bf16[256,256]{1,0:T(8,128)(2,1)S(1)}, u32[]{:S(2)}, u32[]{:S(2)}) collective-permute-start(bf16[256,256]{1,0:T(8,128)(2,1)S(1)} %add_convert_fusion.2), channel_id=1, source_target_pairs={{0,16},{1,17},{2,18},{3,19},{4,20},{5,21},{6,22},{7,23},{8,24},{9,... | collective-permute-start | bytes 393224 | tf_op jit(solution)/shard_map/ppermute | solution.py:246
  31.4 5.9 %collective-permute-start.11 = (bf16[128,256]{1,0:T(8,128)(2,1)S(1)}, bf16[128,256]{1,0:T(8,128)(2,1)S(1)}, u32[]{:S(2)}, u32[]{:S(2)}) collective-permute-start(bf16[128,256]{1,0:T(8,128)(2,1)S(1)} %add_convert_fusion.3), channel_id=1, source_target_pairs={{0,7},{1,2},{2,1},{3,4},{4,3},{5,6},{6,5},{7,0},{8,15},{9,10},{10,... | collective-permute-start | bytes 196616 | tf_op jit(solution)/shard_map/ppermute | solution.py:246
  33.8 4.3 %collective-permute-start.8 = (bf16[128,256]{1,0:T(8,128)(2,1)S(1)}, bf16[128,256]{1,0:T(8,128)(2,1)S(1)}, u32[]{:S(2)}, u32[]{:S(2)}) collective-permute-start(bf16[128,256]{1,0:T(8,128)(2,1)S(1)} %slice.50), channel_id=1, source_target_pairs={{0,8},{1,9},{2,10},{3,11},{4,12},{5,13},{6,14},{7,15},{8,0},{9,1},... | collective-permute-start | bytes 196616 | tf_op jit(solution)/shard_map/ppermute | solution.py:246

commit v6 on v5

--- a/solution.py
+++ b/solution.py
@@ -171,7 +171,8 @@
     take = lambda n: [refs.pop(0) for _ in range(n)]
     blocks = [(take(2), take(n)) for n in pieces]
     kept = take(1)[0] if last else None
-    first = take(carried)[-1] if carried else None
+    held = take(carried)
+    first = held[-1] if held else None
     outs = take(new)
     gq_ref, out_ref = take(2) if last else (None, None)
     gq_run = take(1)[0]
@@ -183,10 +184,13 @@
     for when in ("late", "early", "all"):
         chosen = [p for p in parts if p[0] == when]
         empty = [block(out, row) for w, out, row in blanks if w == when]
-        if not chosen and not empty:
+        kept_on = list(zip(held, outs[: len(held) - 1] + [gq_run])) if when == "early" and not last and held else []
+        if not chosen and not empty and not kept_on:
             continue
 
-        def run(chosen=chosen, empty=empty):
+        def run(chosen=chosen, empty=empty, kept_on=kept_on):
+            for old, ref in kept_on:
+                ref[...] = old[...]
             for ref in empty:
                 ref[...] = jnp.zeros_like(ref)
             for n, (_, far, out, row, which) in enumerate(chosen):

time: 38.9 us -> 38.9 us (level)
  no operation moved by 1% of the time
where the time goes in v6:
time: 38.9 us; the launch traced here: 38.8 us
  waiting for transfers between devices  17.7 us (46%)
  starting transfers between devices  12.9 us (33%)
  Pallas kernels  5.48 us (14%)
  other arithmetic  1.65 us (4%)
  between operations  0.82 us (2%)
    ppermute x12, waiting for transfers between devices, send(): return lax.ppermute(block, ('grp', 'blk'), route)  17.7 us
    ppermute x12, starting transfers between devices, send(): return lax.ppermute(block, ('grp', 'blk'), route)  12.9 us
    pallas_call x7, Pallas kernels, call(): pl.pallas_call(kernel, out_shape=outs, in_specs=[VMEM] * len(args), out_s...  5.48 us
    concatenate x1, other arithmetic, step(): own = lax.optimization_barrier(jnp.concatenate([key_rows, values], axis=1))  0.83 us
  transfers between devices with their start and end apart: 12, of which 9 were waited for; matrix products, arithmetic and copies ran while one was open for 1% of the time, Pallas kernels for 8%

profile of v6, /device:TPU:0, one launch (start us, length us, event | category | flops | bytes accessed | tf_op | source)
XLA Modules:
  0.0 38.8 jit_solution(7522920708097997603)
XLA Ops:
  0.6 0.8 %pad_maximum_fusion.2 = bf16[128,256]{1,0:T(8,128)(2,1)S(1)} fusion(bf16[128,128]{1,0:T(8,128)(2,1)} %param.7, bf16[128,128]{1,0:T(8,128)(2,1)} %param.6), kind=kLoop, calls=%fused_computation.8 | loop fusion | flops 131072 | bytes 131072 | tf_op jit(solution)/shard_map/concatenate | solution.py:270
  1.5 3.1 %collective-permute-start.3 = (bf16[128,256]{1,0:T(8,128)(2,1)S(1)}, bf16[128,256]{1,0:T(8,128)(2,1)S(1)}, u32[]{:S(2)}, u32[]{:S(2)}) collective-permute-start(bf16[128,256]{1,0:T(8,128)(2,1)S(1)} %pad_maximum_fusion.2), channel_id=1, source_target_pairs={{0,16},{1,17},{2,18},{3,19},{4,20},{5,21},{6,22},{7,23},{8,24},{9,... | collective-permute-start | bytes 196616 | tf_op jit(solution)/shard_map/ppermute | solution.py:250
  4.5 2.8 %collective-permute-start = (bf16[128,256]{1,0:T(8,128)(2,1)S(1)}, bf16[128,256]{1,0:T(8,128)(2,1)S(1)}, u32[]{:S(2)}, u32[]{:S(2)}) collective-permute-start(bf16[128,256]{1,0:T(8,128)(2,1)S(1)} %pad_maximum_fusion.2), channel_id=1, source_target_pairs={{0,7},{1,2},{2,1},{3,4},{4,3},{5,6},{6,5},{7,0},{8,15},{9,10},{10,... | collective-permute-start | bytes 196616 | tf_op jit(solution)/shard_map/ppermute | solution.py:250
  7.5 1.6 %collective-permute-start.4 = (bf16[256,256]{1,0:T(8,128)(2,1)S(1)}, bf16[256,256]{1,0:T(8,128)(2,1)S(1)}, u32[]{:S(2)}, u32[]{:S(2)}) collective-permute-start(bf16[256,256]{1,0:T(8,128)(2,1)S(1)} %pad_maximum_fusion.1.refs_0_.refs_2_), channel_id=1, source_target_pairs={{0,8},{1,9},{2,10},{3,11},{4,12},{5,13},{6,14},{7,15},{8,0},{9,1},... | collective-permute-start | bytes 393224 | tf_op jit(solution)/shard_map/ppermute | solution.py:250
  9.0 1.4 %collective-permute-done = bf16[128,256]{1,0:T(8,128)(2,1)S(1)} collective-permute-done((bf16[128,256]{1,0:T(8,128)(2,1)S(1)}, bf16[128,256]{1,0:T(8,128)(2,1)S(1)}, u32[]{:S(2)}, u32[]{:S(2)}) %collective-permute-start) | collective-permute-done | bytes 65568 | tf_op jit(solution)/shard_map/ppermute | solution.py:250
  10.4 4.3 %collective-permute-done.1 = bf16[128,256]{1,0:T(8,128)(2,1)S(1)} collective-permute-done((bf16[128,256]{1,0:T(8,128)(2,1)S(1)}, bf16[128,256]{1,0:T(8,128)(2,1)S(1)}, u32[]{:S(2)}, u32[]{:S(2)}) %collective-permute-start.1) | collective-permute-done | bytes 65568 | tf_op jit(solution)/shard_map/ppermute | solution.py:250
  14.7 1.6 %collective-permute-start.2 = (bf16[256,256]{1,0:T(8,128)(2,1)S(1)}, bf16[256,256]{1,0:T(8,128)(2,1)S(1)}, u32[]{:S(2)}, u32[]{:S(2)}) collective-permute-start(bf16[256,256]{1,0:T(8,128)(2,1)S(1)} %constant_dynamic-update-slice_fusion.refs_0_.refs_2_.refs_6_), channel_id=1, source_target_pairs={{0,8},{1,9},{2,10},{3,11},{4,12},{5,13},{6,14},{7,15},{8,0},{9,1},... | collective-permute-start | bytes 393224 | tf_op jit(solution)/shard_map/ppermute | solution.py:250
  16.3 0.7 %shard_map.84 = (f32[128,1024]{1,0:T(8,128)S(1)}, f32[1,1024]{1,0:T(1,128)S(1)}, f32[1,1024]{1,0:T(1,128)S(1)}, bf16[512,1024]{1,0:T(8,128)(2,1)S(1)}) custom-call(s32[8,8]{1,0:T(8,128)S(1)} %broadcast_in_dim.2.span_ref, bf16[1024,128]{1,0:T(8,128)(2,1)S(1)} %bitcast.16, bf16[256,256]{1,0:T(8,128)(2,1)S(1)} %pad_maximum_fusion.1.refs_0_.refs_2_, ...), custom_call_target="tpu_custom_call" | custom-call | flops 536870912 | bytes 1048576 | tf_op jit(solution)/shard_map/pallas_call | solution.py:220
  17.0 0.8 %collective-permute-done.5.refs_0_.refs_6_.refs_2_ = bf16[512,256]{1,0:T(8,128)(2,1)S(1)} collective-permute-done((bf16[512,256]{1,0:T(8,128)(2,1)S(1)}, bf16[512,256]{1,0:T(8,128)(2,1)S(1)}, u32[]{:S(2)}, u32[]{:S(2)}) %collective-permute-start.5) | collective-permute-done | bytes 262176 | tf_op jit(solution)/shard_map/ppermute | solution.py:250
  17.8 0.7 %shard_map.85 = (f32[128,1024]{1,0:T(8,128)S(1)}, f32[1,1024]{1,0:T(1,128)S(1)}, f32[1,1024]{1,0:T(1,128)S(1)}, bf16[512,1024]{1,0:T(8,128)(2,1)S(1)}) custom-call(s32[8,8]{1,0:T(8,128)S(1)} %broadcast_in_dim.2.span_ref, bf16[1024,128]{1,0:T(8,128)(2,1)S(1)} %bitcast.17, bf16[512,256]{1,0:T(8,128)(2,1)S(1)} %collective-permute-done.5.refs_0_.refs_6_.refs_2_, ...), custom_call_target="tpu_custom_call" | custom-call | flops 536870912 | bytes 1048576 | tf_op jit(solution)/shard_map/pallas_call | solution.py:220
  18.6 1.1 %collective-permute-done.2.refs_1_.refs_3_.refs_7_ = bf16[256,256]{1,0:T(8,128)(2,1)S(1)} collective-permute-done((bf16[256,256]{1,0:T(8,128)(2,1)S(1)}, bf16[256,256]{1,0:T(8,128)(2,1)S(1)}, u32[]{:S(2)}, u32[]{:S(2)}) %collective-permute-start.2) | collective-permute-done | bytes 131104 | tf_op jit(solution)/shard_map/ppermute | solution.py:250
  19.7 1.1 %shard_map.86 = (bf16[128,1024]{1,0:T(8,128)(2,1)S(1)}, bf16[512,1024]{1,0:T(8,128)(2,1)S(1)}, f32[1,1024]{1,0:T(1,128)S(1)}, f32[1,1024]{1,0:T(1,128)S(1)}, f32...) custom-call(s32[8,8]{1,0:T(8,128)S(1)} %broadcast_in_dim.2.span_ref, bf16[1024,128]{1,0:T(8,128)(2,1)S(1)} %bitcast.18, ...), custom_call_target="tpu_custom_call" | custom-call | flops 536870912 | bytes 1048576 | tf_op jit(solution)/shard_map/pallas_call | solution.py:220
  20.8 1.2 %shard_map.87 = (bf16[256,256]{1,0:T(8,128)(2,1)S(1)}, bf16[256,256]{1,0:T(8,128)(2,1)S(1)}, bf16[512,256]{1,0:T(8,128)(2,1)S(1)}, f32[128,1024]{1,0:T(8,128)S(1)}) custom-call(bf16[1024,128]{1,0:T(8,128)(2,1)S(1)} %bitcast.19, bf16[1024,128]{1,0:T(8,128)(2,1)S(1)} %bitcast.24, f32[1,1024]{1,0:T(1,128)S(1)} %get-tuple-element.36.delta_ref, ...), custom_call_target="tpu_custom_call" | custom-call | flops 805306368 | bytes 1048576 | tf_op jit(solution)/shard_map/pallas_call | solution.py:220
  22.4 1.5 %shard_map.90 = (bf16[256,256]{1,0:T(8,128)(2,1)S(1)}, bf16[128,1024]{1,0:T(8,128)(2,1)}, bf16[128,1024]{1,0:T(8,128)(2,1)}) custom-call(bf16[1024,128]{1,0:T(8,128)(2,1)S(1)} %bitcast.22, bf16[1024,128]{1,0:T(8,128)(2,1)S(1)} %bitcast.27, f32[1,1024]{1,0:T(1,128)S(1)} %get-tuple-element.36.delta_ref, bf16[512,1024]{1,0:T(8,128)(2,1)S(1)} %get-tuple-element.37.refs_0_, ...), custom_call_target="tpu_custom_call" | custom-call | flops 268435456 | bytes 1048576 | tf_op jit(solution)/shard_map/pallas_call | solution.py:220
  23.9 3.1 %collective-permute-done.9 = bf16[256,256]{1,0:T(8,128)(2,1)S(1)} collective-permute-done((bf16[256,256]{1,0:T(8,128)(2,1)S(1)}, bf16[256,256]{1,0:T(8,128)(2,1)S(1)}, u32[]{:S(2)}, u32[]{:S(2)}) %collective-permute-start.9) | collective-permute-done | bytes 131104 | tf_op jit(solution)/shard_map/ppermute | solution.py:250
  27.1 1.6 %collective-permute-start.10 = (bf16[128,256]{1,0:T(8,128)(2,1)S(1)}, bf16[128,256]{1,0:T(8,128)(2,1)S(1)}, u32[]{:S(2)}, u32[]{:S(2)}) collective-permute-start(bf16[128,256]{1,0:T(8,128)(2,1)S(1)} %slice.52), channel_id=1, source_target_pairs={{0,8},{1,9},{2,10},{3,11},{4,12},{5,13},{6,14},{7,15},{8,0},{9,1},... | collective-permute-start | bytes 196616 | tf_op jit(solution)/shard_map/ppermute | solution.py:250
  28.7 1.2 %collective-permute-start.7 = (bf16[256,256]{1,0:T(8,128)(2,1)S(1)}, bf16[256,256]{1,0:T(8,128)(2,1)S(1)}, u32[]{:S(2)}, u32[]{:S(2)}) collective-permute-start(bf16[256,256]{1,0:T(8,128)(2,1)S(1)} %add_convert_fusion.2), channel_id=1, source_target_pairs={{0,16},{1,17},{2,18},{3,19},{4,20},{5,21},{6,22},{7,23},{8,24},{9,... | collective-permute-start | bytes 393224 | tf_op jit(solution)/shard_map/ppermute | solution.py:250
  29.8 1.6 %collective-permute-done.10 = bf16[128,256]{1,0:T(8,128)(2,1)S(1)} collective-permute-done((bf16[128,256]{1,0:T(8,128)(2,1)S(1)}, bf16[128,256]{1,0:T(8,128)(2,1)S(1)}, u32[]{:S(2)}, u32[]{:S(2)}) %collective-permute-start.10) | collective-permute-done | bytes 65568 | tf_op jit(solution)/shard_map/ppermute | solution.py:250
  31.4 0.4 %collective-permute-start.11 = (bf16[128,256]{1,0:T(8,128)(2,1)S(1)}, bf16[128,256]{1,0:T(8,128)(2,1)S(1)}, u32[]{:S(2)}, u32[]{:S(2)}) collective-permute-start(bf16[128,256]{1,0:T(8,128)(2,1)S(1)} %add_convert_fusion.3), channel_id=1, source_target_pairs={{0,7},{1,2},{2,1},{3,4},{4,3},{5,6},{6,5},{7,0},{8,15},{9,10},{10,... | collective-permute-start | bytes 196616 | tf_op jit(solution)/shard_map/ppermute | solution.py:250
  31.9 1.8 %collective-permute-done.7 = bf16[256,256]{1,0:T(8,128)(2,1)S(1)} collective-permute-done((bf16[256,256]{1,0:T(8,128)(2,1)S(1)}, bf16[256,256]{1,0:T(8,128)(2,1)S(1)}, u32[]{:S(2)}, u32[]{:S(2)}) %collective-permute-start.7) | collective-permute-done | bytes 131104 | tf_op jit(solution)/shard_map/ppermute | solution.py:250
  33.8 0.6 %collective-permute-start.8 = (bf16[128,256]{1,0:T(8,128)(2,1)S(1)}, bf16[128,256]{1,0:T(8,128)(2,1)S(1)}, u32[]{:S(2)}, u32[]{:S(2)}) collective-permute-start(bf16[128,256]{1,0:T(8,128)(2,1)S(1)} %slice.50), channel_id=1, source_target_pairs={{0,8},{1,9},{2,10},{3,11},{4,12},{5,13},{6,14},{7,15},{8,0},{9,1},... | collective-permute-start | bytes 196616 | tf_op jit(solution)/shard_map/ppermute | solution.py:250
  34.4 2.9 %collective-permute-done.11 = bf16[128,256]{1,0:T(8,128)(2,1)S(1)} collective-permute-done((bf16[128,256]{1,0:T(8,128)(2,1)S(1)}, bf16[128,256]{1,0:T(8,128)(2,1)S(1)}, u32[]{:S(2)}, u32[]{:S(2)}) %collective-permute-start.11) | collective-permute-done | bytes 65568 | tf_op jit(solution)/shard_map/ppermute | solution.py:250
  37.3 0.8 %collective-permute-done.8 = bf16[128,256]{1,0:T(8,128)(2,1)S(1)} collective-permute-done((bf16[128,256]{1,0:T(8,128)(2,1)S(1)}, bf16[128,256]{1,0:T(8,128)(2,1)S(1)}, u32[]{:S(2)}, u32[]{:S(2)}) %collective-permute-start.8) | collective-permute-done | bytes 65568 | tf_op jit(solution)/shard_map/ppermute | solution.py:250
  38.1 0.7 %add_convert_fusion.4 = (bf16[128,128]{1,0:T(8,128)(2,1)}, bf16[128,128]{1,0:T(8,128)(2,1)}) fusion(bf16[128,256]{1,0:T(8,128)(2,1)S(1)} %collective-permute-done.11, bf16[128,256]{1,0:T(8,128)(2,1)S(1)} %collective-permute-done.8, bf16[256,256]{1,0:T(8,128)(2,1)S(1)} %add_convert_fusion.1), kind=kLoop, calls=%fused_computation.9 | loop fusion | flops 196608 | bytes 262144 | tf_op jit(solution)/shard_map/convert_element_type | solution.py:355
  (29 shorter events, 0.8 us)
Async XLA Ops:
  0.6 6.7 %copy-start = (bf16[128,1024]{1,0:T(8,128)(2,1)S(1)}, bf16[128,1024]{1,0:T(8,128)(2,1)}, u32[]{:S(2)}) copy-start(bf16[128,1024]{1,0:T(8,128)(2,1)} %param.5) | copy-start | bytes 786436
  1.5 5.9 %copy-start.1 = (bf16[128,1024]{1,0:T(8,128)(2,1)S(1)}, bf16[128,1024]{1,0:T(8,128)(2,1)}, u32[]{:S(2)}) copy-start(bf16[128,1024]{1,0:T(8,128)(2,1)} %param.8) | copy-start | bytes 786436
  1.5 5.9 %collective-permute-start.3 = (bf16[128,256]{1,0:T(8,128)(2,1)S(1)}, bf16[128,256]{1,0:T(8,128)(2,1)S(1)}, u32[]{:S(2)}, u32[]{:S(2)}) collective-permute-start(bf16[128,256]{1,0:T(8,128)(2,1)S(1)} %pad_maximum_fusion.2), channel_id=1, source_target_pairs={{0,16},{1,17},{2,18},{3,19},{4,20},{5,21},{6,22},{7,23},{8,24},{9,... | collective-permute-start | bytes 196616 | tf_op jit(solution)/shard_map/ppermute | solution.py:250
  4.5 5.8 %collective-permute-start = (bf16[128,256]{1,0:T(8,128)(2,1)S(1)}, bf16[128,256]{1,0:T(8,128)(2,1)S(1)}, u32[]{:S(2)}, u32[]{:S(2)}) collective-permute-start(bf16[128,256]{1,0:T(8,128)(2,1)S(1)} %pad_maximum_fusion.2), channel_id=1, source_target_pairs={{0,7},{1,2},{2,1},{3,4},{4,3},{5,6},{6,5},{7,0},{8,15},{9,10},{10,... | collective-permute-start | bytes 196616 | tf_op jit(solution)/shard_map/ppermute | solution.py:250
  7.5 8.8 %collective-permute-start.4 = (bf16[256,256]{1,0:T(8,128)(2,1)S(1)}, bf16[256,256]{1,0:T(8,128)(2,1)S(1)}, u32[]{:S(2)}, u32[]{:S(2)}) collective-permute-start(bf16[256,256]{1,0:T(8,128)(2,1)S(1)} %pad_maximum_fusion.1.refs_0_.refs_2_), channel_id=1, source_target_pairs={{0,8},{1,9},{2,10},{3,11},{4,12},{5,13},{6,14},{7,15},{8,0},{9,1},... | collective-permute-start | bytes 393224 | tf_op jit(solution)/shard_map/ppermute | solution.py:250
  10.4 4.3 %collective-permute-start.1 = (bf16[128,256]{1,0:T(8,128)(2,1)S(1)}, bf16[128,256]{1,0:T(8,128)(2,1)S(1)}, u32[]{:S(2)}, u32[]{:S(2)}) collective-permute-start(bf16[128,256]{1,0:T(8,128)(2,1)S(1)} %collective-permute-done), channel_id=1, source_target_pairs={{0,16},{1,17},{2,18},{3,19},{4,20},{5,21},{6,22},{7,23},{8,24},{9,... | collective-permute-start | bytes 196616 | tf_op jit(solution)/shard_map/ppermute | solution.py:250
  14.6 1.7 %copy-start.2 = (s32[8]{0:T(128)S(1)}, s32[8]{0:T(128)}, u32[]{:S(2)}) copy-start(s32[8]{0:T(128)} %param.9) | copy-start | bytes 100
  14.7 5.0 %collective-permute-start.2 = (bf16[256,256]{1,0:T(8,128)(2,1)S(1)}, bf16[256,256]{1,0:T(8,128)(2,1)S(1)}, u32[]{:S(2)}, u32[]{:S(2)}) collective-permute-start(bf16[256,256]{1,0:T(8,128)(2,1)S(1)} %constant_dynamic-update-slice_fusion.refs_0_.refs_2_.refs_6_), channel_id=1, source_target_pairs={{0,8},{1,9},{2,10},{3,11},{4,12},{5,13},{6,14},{7,15},{8,0},{9,1},... | collective-permute-start | bytes 393224 | tf_op jit(solution)/shard_map/ppermute | solution.py:250
  16.2 1.6 %collective-permute-start.5 = (bf16[512,256]{1,0:T(8,128)(2,1)S(1)}, bf16[512,256]{1,0:T(8,128)(2,1)S(1)}, u32[]{:S(2)}, u32[]{:S(2)}) collective-permute-start(bf16[512,256]{1,0:T(8,128)(2,1)S(1)} %pad_maximum_fusion), channel_id=1, source_target_pairs={{0,1},{1,0},{2,3},{3,2},{4,5},{5,4},{6,7},{7,6},{8,9},{9,8},{10,11... | collective-permute-start | bytes 786440 | tf_op jit(solution)/shard_map/ppermute | solution.py:250
  22.0 5.0 %collective-permute-start.9 = (bf16[256,256]{1,0:T(8,128)(2,1)S(1)}, bf16[256,256]{1,0:T(8,128)(2,1)S(1)}, u32[]{:S(2)}, u32[]{:S(2)}) collective-permute-start(bf16[256,256]{1,0:T(8,128)(2,1)S(1)} %get-tuple-element.55), channel_id=1, source_target_pairs={{0,16},{1,17},{2,18},{3,19},{4,20},{5,21},{6,22},{7,23},{8,24},{9,... | collective-permute-start | bytes 393224 | tf_op jit(solution)/shard_map/ppermute | solution.py:250
  22.2 6.4 %collective-permute-start.6 = (bf16[512,256]{1,0:T(8,128)(2,1)S(1)}, bf16[512,256]{1,0:T(8,128)(2,1)S(1)}, u32[]{:S(2)}, u32[]{:S(2)}) collective-permute-start(bf16[512,256]{1,0:T(8,128)(2,1)S(1)} %get-tuple-element.52), channel_id=1, source_target_pairs={{0,1},{1,0},{2,3},{3,2},{4,5},{5,4},{6,7},{7,6},{8,9},{9,8},{10,11... | collective-permute-start | bytes 786440 | tf_op jit(solution)/shard_map/ppermute | solution.py:250
  27.1 4.3 %collective-permute-start.10 = (bf16[128,256]{1,0:T(8,128)(2,1)S(1)}, bf16[128,256]{1,0:T(8,128)(2,1)S(1)}, u32[]{:S(2)}, u32[]{:S(2)}) collective-permute-start(bf16[128,256]{1,0:T(8,128)(2,1)S(1)} %slice.52), channel_id=1, source_target_pairs={{0,8},{1,9},{2,10},{3,11},{4,12},{5,13},{6,14},{7,15},{8,0},{9,1},... | collective-permute-start | bytes 196616 | tf_op jit(solution)/shard_map/ppermute | solution.py:250
  28.7 5.0 %collective-permute-start.7 = (bf16[256,256]{1,0:T(8,128)(2,1)S(1)}, bf16[256,256]{1,0:T(8,128)(2,1)S(1)}, u32[]{:S(2)}, u32[]{:S(2)}) collective-permute-start(bf16[256,256]{1,0:T(8,128)(2,1)S(1)} %add_convert_fusion.2), channel_id=1, source_target_pairs={{0,16},{1,17},{2,18},{3,19},{4,20},{5,21},{6,22},{7,23},{8,24},{9,... | collective-permute-start | bytes 393224 | tf_op jit(solution)/shard_map/ppermute | solution.py:250
  31.4 5.9 %collective-permute-start.11 = (bf16[128,256]{1,0:T(8,128)(2,1)S(1)}, bf16[128,256]{1,0:T(8,128)(2,1)S(1)}, u32[]{:S(2)}, u32[]{:S(2)}) collective-permute-start(bf16[128,256]{1,0:T(8,128)(2,1)S(1)} %add_convert_fusion.3), channel_id=1, source_target_pairs={{0,7},{1,2},{2,1},{3,4},{4,3},{5,6},{6,5},{7,0},{8,15},{9,10},{10,... | collective-permute-start | bytes 196616 | tf_op jit(solution)/shard_map/ppermute | solution.py:250
  33.8 4.3 %collective-permute-start.8 = (bf16[128,256]{1,0:T(8,128)(2,1)S(1)}, bf16[128,256]{1,0:T(8,128)(2,1)S(1)}, u32[]{:S(2)}, u32[]{:S(2)}) collective-permute-start(bf16[128,256]{1,0:T(8,128)(2,1)S(1)} %slice.50), channel_id=1, source_target_pairs={{0,8},{1,9},{2,10},{3,11},{4,12},{5,13},{6,14},{7,15},{8,0},{9,1},... | collective-permute-start | bytes 196616 | tf_op jit(solution)/shard_map/ppermute | solution.py:250

commit v7 on v6

--- a/solution.py
+++ b/solution.py
@@ -184,7 +184,7 @@
     for when in ("late", "early", "all"):
         chosen = [p for p in parts if p[0] == when]
         empty = [block(out, row) for w, out, row in blanks if w == when]
-        kept_on = list(zip(held, outs[: len(held) - 1] + [gq_run])) if when == "early" and not last and held else []
+        kept_on = list(zip(held, outs[: len(held) - 1] + [gq_run])) if when == "early" and held else []
         if not chosen and not empty and not kept_on:
             continue
 
@@ -336,13 +336,21 @@
         [("late", 1, 0, 0, "off"), ("early", 0, 1, 0, "off"), ("early", 0, 2, 0, "mate")],
         (("early", 0, 0), ("early", 2, 1)), [], [unit, unit, 2 * unit], None,
     )
-    gm, gq = back([("late", 1, 0, 1, "mate"), ("late", 0, 0, 0, "mate")], (), [gm], [], gq)
-    gsf, geo, gq = back([("late", 1, 1, 0, "own"), ("late", 0, 0, 0, "off")], (("early", 1, 0),), [gsf], [unit], gq)
-    gso, gq, out = back([("all", 0, 0, 0, "own")], (), [], [unit], gq, last=True)
-
-    back_f = across(gef)
-    gsf = add(gsf, back_f)
-    total_f = scattered(gsf)
+    gsf, gm, gso, gq = back(
+        [("late", 0, 0, 0, "off"), ("late", 1, 1, 1, "mate"), ("late", 0, 1, 0, "mate"), ("early", 0, 2, 0, "own")],
+        (), [gsf, gm], [unit], gq,
+    )
+    geo, gq = back([("late", 1, 0, 0, "own")], (("early", 0, 0),), [], [unit], gq)
+    gso, gq, out = back([("late", 0, 0, 0, "own")], (), [gso], [], gq, last=True)
+
+    back_1 = across(gef[rows:])
+    back_0 = across(gef[:rows])
+    total_f = gsf[unit - rows :].astype(F32) + back_1[unit - 2 * rows :].astype(F32)
+    for s in range(half - 2, -1, -1):
+        moved = ring_down(total_f.astype(BF16))
+        more = back_1[(s - 1) * rows : s * rows] if s > 0 else back_0
+        total_f = moved.astype(F32) + gsf[s * rows : (s + 1) * rows].astype(F32) + more.astype(F32)
+    total_f = total_f.astype(BF16)
     ret_f = off_chip(total_f)
     mate = on_chip(gm)
     geo = add(geo, mate[unit:])

time: 38.9 us -> 39.1 us (level)
  waiting for transfers between devices: 17.7 us -> 13.1 us
  starting transfers between devices: 12.9 us -> 17.2 us
  Pallas kernels: 5.48 us -> 5.96 us
    ppermute x12 -> x13, waiting for transfers between devices: 17.7 us -> 13.1 us  [send(): return lax.ppermute(block, ('grp', 'blk'), route)]
    ppermute x12 -> x13, starting transfers between devices: 12.9 us -> 17.2 us  [send(): return lax.ppermute(block, ('grp', 'blk'), route)]
    pallas_call x7, Pallas kernels: 5.48 us -> 5.96 us  [call(): pl.pallas_call(kernel, out_shape=outs, in_specs=[VMEM] * len(args), out_s...]
  transfers between devices with their start and end apart: 12 -> 13, of which waited for: 9 -> 8; matrix products, arithmetic and copies ran while one was open for 1% -> 1% of each run, Pallas kernels for 8% -> 9%
where the time goes in v7:
time: 39.1 us; the launch traced here: 39 us
  starting transfers between devices  17.2 us (44%)
  waiting for transfers between devices  13.1 us (34%)
  Pallas kernels  5.96 us (15%)
  other arithmetic  1.65 us (4%)
  between operations  0.83 us (2%)
    ppermute x13, starting transfers between devices, send(): return lax.ppermute(block, ('grp', 'blk'), route)  17.2 us
    ppermute x13, waiting for transfers between devices, send(): return lax.ppermute(block, ('grp', 'blk'), route)  13.1 us
    pallas_call x7, Pallas kernels, call(): pl.pallas_call(kernel, out_shape=outs, in_specs=[VMEM] * len(args), out_s...  5.96 us
    concatenate x1, other arithmetic, step(): own = lax.optimization_barrier(jnp.concatenate([key_rows, values], axis=1))  0.83 us
  transfers between devices with their start and end apart: 13, of which 8 were waited for; matrix products, arithmetic and copies ran while one was open for 1% of the time, Pallas kernels for 9%

profile of v7, /device:TPU:0, one launch (start us, length us, event | category | flops | bytes accessed | tf_op | source)
XLA Modules:
  0.0 39.0 jit_solution(6652369413151257848)
XLA Ops:
  0.6 0.8 %pad_maximum_fusion.2 = bf16[128,256]{1,0:T(8,128)(2,1)S(1)} fusion(bf16[128,128]{1,0:T(8,128)(2,1)} %param.7, bf16[128,128]{1,0:T(8,128)(2,1)} %param.6), kind=kLoop, calls=%fused_computation.8 | loop fusion | flops 131072 | bytes 131072 | tf_op jit(solution)/shard_map/concatenate | solution.py:270
  1.5 3.1 %collective-permute-start.3 = (bf16[128,256]{1,0:T(8,128)(2,1)S(1)}, bf16[128,256]{1,0:T(8,128)(2,1)S(1)}, u32[]{:S(2)}, u32[]{:S(2)}) collective-permute-start(bf16[128,256]{1,0:T(8,128)(2,1)S(1)} %pad_maximum_fusion.2), channel_id=1, source_target_pairs={{0,16},{1,17},{2,18},{3,19},{4,20},{5,21},{6,22},{7,23},{8,24},{9,... | collective-permute-start | bytes 196616 | tf_op jit(solution)/shard_map/ppermute | solution.py:250
  4.5 2.8 %collective-permute-start = (bf16[128,256]{1,0:T(8,128)(2,1)S(1)}, bf16[128,256]{1,0:T(8,128)(2,1)S(1)}, u32[]{:S(2)}, u32[]{:S(2)}) collective-permute-start(bf16[128,256]{1,0:T(8,128)(2,1)S(1)} %pad_maximum_fusion.2), channel_id=1, source_target_pairs={{0,7},{1,2},{2,1},{3,4},{4,3},{5,6},{6,5},{7,0},{8,15},{9,10},{10,... | collective-permute-start | bytes 196616 | tf_op jit(solution)/shard_map/ppermute | solution.py:250
  7.5 1.6 %collective-permute-start.4 = (bf16[256,256]{1,0:T(8,128)(2,1)S(1)}, bf16[256,256]{1,0:T(8,128)(2,1)S(1)}, u32[]{:S(2)}, u32[]{:S(2)}) collective-permute-start(bf16[256,256]{1,0:T(8,128)(2,1)S(1)} %pad_maximum_fusion.1.refs_0_.refs_9_.refs_2_), channel_id=1, source_target_pairs={{0,8},{1,9},{2,10},{3,11},{4,12},{5,13},{6,14},{7,15},{8,0},{9,1},... | collective-permute-start | bytes 393224 | tf_op jit(solution)/shard_map/ppermute | solution.py:250
  9.0 1.4 %collective-permute-done = bf16[128,256]{1,0:T(8,128)(2,1)S(1)} collective-permute-done((bf16[128,256]{1,0:T(8,128)(2,1)S(1)}, bf16[128,256]{1,0:T(8,128)(2,1)S(1)}, u32[]{:S(2)}, u32[]{:S(2)}) %collective-permute-start) | collective-permute-done | bytes 65568 | tf_op jit(solution)/shard_map/ppermute | solution.py:250
  10.4 4.3 %collective-permute-done.1 = bf16[128,256]{1,0:T(8,128)(2,1)S(1)} collective-permute-done((bf16[128,256]{1,0:T(8,128)(2,1)S(1)}, bf16[128,256]{1,0:T(8,128)(2,1)S(1)}, u32[]{:S(2)}, u32[]{:S(2)}) %collective-permute-start.1) | collective-permute-done | bytes 65568 | tf_op jit(solution)/shard_map/ppermute | solution.py:250
  14.7 1.6 %collective-permute-start.2 = (bf16[256,256]{1,0:T(8,128)(2,1)S(1)}, bf16[256,256]{1,0:T(8,128)(2,1)S(1)}, u32[]{:S(2)}, u32[]{:S(2)}) collective-permute-start(bf16[256,256]{1,0:T(8,128)(2,1)S(1)} %constant_dynamic-update-slice_fusion.refs_0_.refs_2_), channel_id=1, source_target_pairs={{0,8},{1,9},{2,10},{3,11},{4,12},{5,13},{6,14},{7,15},{8,0},{9,1},... | collective-permute-start | bytes 393224 | tf_op jit(solution)/shard_map/ppermute | solution.py:250
  16.3 0.7 %shard_map.84 = (f32[128,1024]{1,0:T(8,128)S(1)}, f32[1,1024]{1,0:T(1,128)S(1)}, f32[1,1024]{1,0:T(1,128)S(1)}, bf16[512,1024]{1,0:T(8,128)(2,1)S(1)}) custom-call(s32[8,8]{1,0:T(8,128)S(1)} %broadcast_in_dim.2.span_ref, bf16[1024,128]{1,0:T(8,128)(2,1)S(1)} %bitcast.16, bf16[256,256]{1,0:T(8,128)(2,1)S(1)} %pad_maximum_fusion.1.refs_0_.refs_9_.refs_2_, ...), custom_call_target="tpu_custom_call" | custom-call | flops 536870912 | bytes 1048576 | tf_op jit(solution)/shard_map/pallas_call | solution.py:220
  17.0 0.8 %collective-permute-done.5.refs_0_.refs_6_ = bf16[512,256]{1,0:T(8,128)(2,1)S(1)} collective-permute-done((bf16[512,256]{1,0:T(8,128)(2,1)S(1)}, bf16[512,256]{1,0:T(8,128)(2,1)S(1)}, u32[]{:S(2)}, u32[]{:S(2)}) %collective-permute-start.5) | collective-permute-done | bytes 262176 | tf_op jit(solution)/shard_map/ppermute | solution.py:250
  17.8 0.7 %shard_map.85 = (f32[128,1024]{1,0:T(8,128)S(1)}, f32[1,1024]{1,0:T(1,128)S(1)}, f32[1,1024]{1,0:T(1,128)S(1)}, bf16[512,1024]{1,0:T(8,128)(2,1)S(1)}) custom-call(s32[8,8]{1,0:T(8,128)S(1)} %broadcast_in_dim.2.span_ref, bf16[1024,128]{1,0:T(8,128)(2,1)S(1)} %bitcast.17, bf16[512,256]{1,0:T(8,128)(2,1)S(1)} %collective-permute-done.5.refs_0_.refs_6_, ...), custom_call_target="tpu_custom_call" | custom-call | flops 536870912 | bytes 1048576 | tf_op jit(solution)/shard_map/pallas_call | solution.py:220
  18.6 1.1 %collective-permute-done.2.refs_1_.refs_3_ = bf16[256,256]{1,0:T(8,128)(2,1)S(1)} collective-permute-done((bf16[256,256]{1,0:T(8,128)(2,1)S(1)}, bf16[256,256]{1,0:T(8,128)(2,1)S(1)}, u32[]{:S(2)}, u32[]{:S(2)}) %collective-permute-start.2) | collective-permute-done | bytes 131104 | tf_op jit(solution)/shard_map/ppermute | solution.py:250
  19.7 1.1 %shard_map.86 = (bf16[128,1024]{1,0:T(8,128)(2,1)S(1)}, bf16[512,1024]{1,0:T(8,128)(2,1)S(1)}, f32[1,1024]{1,0:T(1,128)S(1)}, f32[1,1024]{1,0:T(1,128)S(1)}, f32...) custom-call(s32[8,8]{1,0:T(8,128)S(1)} %broadcast_in_dim.2.span_ref, bf16[1024,128]{1,0:T(8,128)(2,1)S(1)} %bitcast.18, ...), custom_call_target="tpu_custom_call" | custom-call | flops 536870912 | bytes 1048576 | tf_op jit(solution)/shard_map/pallas_call | solution.py:220
  20.8 1.2 %shard_map.87 = (bf16[256,256]{1,0:T(8,128)(2,1)S(1)}, bf16[256,256]{1,0:T(8,128)(2,1)S(1)}, bf16[512,256]{1,0:T(8,128)(2,1)S(1)}, f32[128,1024]{1,0:T(8,128)S(1)}) custom-call(bf16[1024,128]{1,0:T(8,128)(2,1)S(1)} %bitcast.19, bf16[1024,128]{1,0:T(8,128)(2,1)S(1)} %bitcast.24, f32[1,1024]{1,0:T(1,128)S(1)} %get-tuple-element.37.delta_ref, ...), custom_call_target="tpu_custom_call" | custom-call | flops 805306368 | bytes 1048576 | tf_op jit(solution)/shard_map/pallas_call | solution.py:220
  22.1 2.0 %collective-permute-start.11 = (bf16[128,256]{1,0:T(8,128)(2,1)S(1)}, bf16[128,256]{1,0:T(8,128)(2,1)S(1)}, u32[]{:S(2)}, u32[]{:S(2)}) collective-permute-start(bf16[128,256]{1,0:T(8,128)(2,1)S(1)} %get-tuple-element.61), channel_id=1, source_target_pairs={{0,16},{1,17},{2,18},{3,19},{4,20},{5,21},{6,22},{7,23},{8,24},{9,... | collective-permute-start | bytes 196616 | tf_op jit(solution)/shard_map/ppermute | solution.py:250
  24.1 0.8 %shard_map.88 = (bf16[256,256]{1,0:T(8,128)(2,1)S(1)}, bf16[512,256]{1,0:T(8,128)(2,1)S(1)}, bf16[256,256]{1,0:T(8,128)(2,1)S(1)}, f32[128,1024]{1,0:T(8,128)S(1)}) custom-call(bf16[1024,128]{1,0:T(8,128)(2,1)S(1)} %bitcast.20, bf16[1024,128]{1,0:T(8,128)(2,1)S(1)} %bitcast.25, ...), custom_call_target="tpu_custom_call", output_to_operand_aliasing={{0}: (14, {}), {1}: (15, {}), {3}: (16, {})} | custom-call | flops 1073741824 | bytes 1048576 | tf_op jit(solution)/shard_map/pallas_call | solution.py:220
  25.0 1.4 %shard_map.90 = (bf16[256,256]{1,0:T(8,128)(2,1)S(1)}, bf16[128,1024]{1,0:T(8,128)(2,1)}, bf16[128,1024]{1,0:T(8,128)(2,1)}) custom-call(bf16[1024,128]{1,0:T(8,128)(2,1)S(1)} %bitcast.22, bf16[1024,128]{1,0:T(8,128)(2,1)S(1)} %bitcast.27, f32[1,1024]{1,0:T(1,128)S(1)} %get-tuple-element.37.delta_ref, ...), custom_call_target="tpu_custom_call", output_to_operand_aliasing={{0}: (8, {})} | custom-call | flops 268435456 | bytes 1048576 | tf_op jit(solution)/shard_map/pallas_call | solution.py:220
  26.5 1.5 %collective-permute-start.10 = (bf16[128,256]{1,0:T(8,128)(2,1)S(1)}, bf16[128,256]{1,0:T(8,128)(2,1)S(1)}, u32[]{:S(2)}, u32[]{:S(2)}) collective-permute-start(bf16[128,256]{1,0:T(8,128)(2,1)S(1)} %add_convert_fusion.3), channel_id=1, source_target_pairs={{0,8},{1,9},{2,10},{3,11},{4,12},{5,13},{6,14},{7,15},{8,0},{9,1},... | collective-permute-start | bytes 196616 | tf_op jit(solution)/shard_map/ppermute | solution.py:250
  28.1 2.0 %collective-permute-start.7 = (bf16[256,256]{1,0:T(8,128)(2,1)S(1)}, bf16[256,256]{1,0:T(8,128)(2,1)S(1)}, u32[]{:S(2)}, u32[]{:S(2)}) collective-permute-start(bf16[256,256]{1,0:T(8,128)(2,1)S(1)} %add_convert_fusion.1), channel_id=1, source_target_pairs={{0,16},{1,17},{2,18},{3,19},{4,20},{5,21},{6,22},{7,23},{8,24},{9,... | collective-permute-start | bytes 393224 | tf_op jit(solution)/shard_map/ppermute | solution.py:250
  30.0 1.0 %collective-permute-done.10 = bf16[128,256]{1,0:T(8,128)(2,1)S(1)} collective-permute-done((bf16[128,256]{1,0:T(8,128)(2,1)S(1)}, bf16[128,256]{1,0:T(8,128)(2,1)S(1)}, u32[]{:S(2)}, u32[]{:S(2)}) %collective-permute-start.10) | collective-permute-done | bytes 65568 | tf_op jit(solution)/shard_map/ppermute | solution.py:250
  31.1 2.1 %collective-permute-start.12 = (bf16[128,256]{1,0:T(8,128)(2,1)S(1)}, bf16[128,256]{1,0:T(8,128)(2,1)S(1)}, u32[]{:S(2)}, u32[]{:S(2)}) collective-permute-start(bf16[128,256]{1,0:T(8,128)(2,1)S(1)} %add_convert_fusion.2), channel_id=1, source_target_pairs={{0,7},{1,2},{2,1},{3,4},{4,3},{5,6},{6,5},{7,0},{8,15},{9,10},{10,... | collective-permute-start | bytes 196616 | tf_op jit(solution)/shard_map/ppermute | solution.py:250
  33.2 0.7 %collective-permute-done.7 = bf16[256,256]{1,0:T(8,128)(2,1)S(1)} collective-permute-done((bf16[256,256]{1,0:T(8,128)(2,1)S(1)}, bf16[256,256]{1,0:T(8,128)(2,1)S(1)}, u32[]{:S(2)}, u32[]{:S(2)}) %collective-permute-start.7) | collective-permute-done | bytes 131104 | tf_op jit(solution)/shard_map/ppermute | solution.py:250
  34.4 2.5 %collective-permute-done.12 = bf16[128,256]{1,0:T(8,128)(2,1)S(1)} collective-permute-done((bf16[128,256]{1,0:T(8,128)(2,1)S(1)}, bf16[128,256]{1,0:T(8,128)(2,1)S(1)}, u32[]{:S(2)}, u32[]{:S(2)}) %collective-permute-start.12) | collective-permute-done | bytes 65568 | tf_op jit(solution)/shard_map/ppermute | solution.py:250
  36.9 1.4 %collective-permute-done.8 = bf16[128,256]{1,0:T(8,128)(2,1)S(1)} collective-permute-done((bf16[128,256]{1,0:T(8,128)(2,1)S(1)}, bf16[128,256]{1,0:T(8,128)(2,1)S(1)}, u32[]{:S(2)}, u32[]{:S(2)}) %collective-permute-start.8) | collective-permute-done | bytes 65568 | tf_op jit(solution)/shard_map/ppermute | solution.py:250
  38.3 0.7 %add_convert_fusion.4 = (bf16[128,128]{1,0:T(8,128)(2,1)}, bf16[128,128]{1,0:T(8,128)(2,1)}) fusion(bf16[128,256]{1,0:T(8,128)(2,1)S(1)} %collective-permute-done.12, bf16[128,256]{1,0:T(8,128)(2,1)S(1)} %collective-permute-done.8, bf16[256,256]{1,0:T(8,128)(2,1)S(1)} %add_convert_fusion), kind=kLoop, calls=%fused_computation.9 | loop fusion | flops 196608 | bytes 262144 | tf_op jit(solution)/shard_map/convert_element_type | solution.py:363
  (31 shorter events, 1.1 us)
Async XLA Ops:
  0.6 6.7 %copy-start = (bf16[128,1024]{1,0:T(8,128)(2,1)S(1)}, bf16[128,1024]{1,0:T(8,128)(2,1)}, u32[]{:S(2)}) copy-start(bf16[128,1024]{1,0:T(8,128)(2,1)} %param.5) | copy-start | bytes 786436
  1.5 5.9 %copy-start.1 = (bf16[128,1024]{1,0:T(8,128)(2,1)S(1)}, bf16[128,1024]{1,0:T(8,128)(2,1)}, u32[]{:S(2)}) copy-start(bf16[128,1024]{1,0:T(8,128)(2,1)} %param.8) | copy-start | bytes 786436
  1.5 5.9 %collective-permute-start.3 = (bf16[128,256]{1,0:T(8,128)(2,1)S(1)}, bf16[128,256]{1,0:T(8,128)(2,1)S(1)}, u32[]{:S(2)}, u32[]{:S(2)}) collective-permute-start(bf16[128,256]{1,0:T(8,128)(2,1)S(1)} %pad_maximum_fusion.2), channel_id=1, source_target_pairs={{0,16},{1,17},{2,18},{3,19},{4,20},{5,21},{6,22},{7,23},{8,24},{9,... | collective-permute-start | bytes 196616 | tf_op jit(solution)/shard_map/ppermute | solution.py:250
  4.5 5.8 %collective-permute-start = (bf16[128,256]{1,0:T(8,128)(2,1)S(1)}, bf16[128,256]{1,0:T(8,128)(2,1)S(1)}, u32[]{:S(2)}, u32[]{:S(2)}) collective-permute-start(bf16[128,256]{1,0:T(8,128)(2,1)S(1)} %pad_maximum_fusion.2), channel_id=1, source_target_pairs={{0,7},{1,2},{2,1},{3,4},{4,3},{5,6},{6,5},{7,0},{8,15},{9,10},{10,... | collective-permute-start | bytes 196616 | tf_op jit(solution)/shard_map/ppermute | solution.py:250
  7.5 8.8 %collective-permute-start.4 = (bf16[256,256]{1,0:T(8,128)(2,1)S(1)}, bf16[256,256]{1,0:T(8,128)(2,1)S(1)}, u32[]{:S(2)}, u32[]{:S(2)}) collective-permute-start(bf16[256,256]{1,0:T(8,128)(2,1)S(1)} %pad_maximum_fusion.1.refs_0_.refs_9_.refs_2_), channel_id=1, source_target_pairs={{0,8},{1,9},{2,10},{3,11},{4,12},{5,13},{6,14},{7,15},{8,0},{9,1},... | collective-permute-start | bytes 393224 | tf_op jit(solution)/shard_map/ppermute | solution.py:250
  10.4 4.3 %collective-permute-start.1 = (bf16[128,256]{1,0:T(8,128)(2,1)S(1)}, bf16[128,256]{1,0:T(8,128)(2,1)S(1)}, u32[]{:S(2)}, u32[]{:S(2)}) collective-permute-start(bf16[128,256]{1,0:T(8,128)(2,1)S(1)} %collective-permute-done), channel_id=1, source_target_pairs={{0,16},{1,17},{2,18},{3,19},{4,20},{5,21},{6,22},{7,23},{8,24},{9,... | collective-permute-start | bytes 196616 | tf_op jit(solution)/shard_map/ppermute | solution.py:250
  14.6 1.7 %copy-start.2 = (s32[8]{0:T(128)S(1)}, s32[8]{0:T(128)}, u32[]{:S(2)}) copy-start(s32[8]{0:T(128)} %param.9) | copy-start | bytes 100
  14.7 5.0 %collective-permute-start.2 = (bf16[256,256]{1,0:T(8,128)(2,1)S(1)}, bf16[256,256]{1,0:T(8,128)(2,1)S(1)}, u32[]{:S(2)}, u32[]{:S(2)}) collective-permute-start(bf16[256,256]{1,0:T(8,128)(2,1)S(1)} %constant_dynamic-update-slice_fusion.refs_0_.refs_2_), channel_id=1, source_target_pairs={{0,8},{1,9},{2,10},{3,11},{4,12},{5,13},{6,14},{7,15},{8,0},{9,1},... | collective-permute-start | bytes 393224 | tf_op jit(solution)/shard_map/ppermute | solution.py:250
  16.2 1.6 %collective-permute-start.5 = (bf16[512,256]{1,0:T(8,128)(2,1)S(1)}, bf16[512,256]{1,0:T(8,128)(2,1)S(1)}, u32[]{:S(2)}, u32[]{:S(2)}) collective-permute-start(bf16[512,256]{1,0:T(8,128)(2,1)S(1)} %pad_maximum_fusion), channel_id=1, source_target_pairs={{0,1},{1,0},{2,3},{3,2},{4,5},{5,4},{6,7},{7,6},{8,9},{9,8},{10,11... | collective-permute-start | bytes 786440 | tf_op jit(solution)/shard_map/ppermute | solution.py:250
  22.0 4.5 %collective-permute-start.9 = (bf16[128,256]{1,0:T(8,128)(2,1)S(1)}, bf16[128,256]{1,0:T(8,128)(2,1)S(1)}, u32[]{:S(2)}, u32[]{:S(2)}) collective-permute-start(bf16[128,256]{1,0:T(8,128)(2,1)S(1)} %get-tuple-element.60), channel_id=1, source_target_pairs={{0,16},{1,17},{2,18},{3,19},{4,20},{5,21},{6,22},{7,23},{8,24},{9,... | collective-permute-start | bytes 196616 | tf_op jit(solution)/shard_map/ppermute | solution.py:250
  22.1 8.0 %collective-permute-start.11 = (bf16[128,256]{1,0:T(8,128)(2,1)S(1)}, bf16[128,256]{1,0:T(8,128)(2,1)S(1)}, u32[]{:S(2)}, u32[]{:S(2)}) collective-permute-start(bf16[128,256]{1,0:T(8,128)(2,1)S(1)} %get-tuple-element.61), channel_id=1, source_target_pairs={{0,16},{1,17},{2,18},{3,19},{4,20},{5,21},{6,22},{7,23},{8,24},{9,... | collective-permute-start | bytes 196616 | tf_op jit(solution)/shard_map/ppermute | solution.py:250
  24.8 3.2 %collective-permute-start.6 = (bf16[512,256]{1,0:T(8,128)(2,1)S(1)}, bf16[512,256]{1,0:T(8,128)(2,1)S(1)}, u32[]{:S(2)}, u32[]{:S(2)}) collective-permute-start(bf16[512,256]{1,0:T(8,128)(2,1)S(1)} %get-tuple-element.54), channel_id=1, source_target_pairs={{0,1},{1,0},{2,3},{3,2},{4,5},{5,4},{6,7},{7,6},{8,9},{9,8},{10,11... | collective-permute-start | bytes 786440 | tf_op jit(solution)/shard_map/ppermute | solution.py:250
  26.5 4.5 %collective-permute-start.10 = (bf16[128,256]{1,0:T(8,128)(2,1)S(1)}, bf16[128,256]{1,0:T(8,128)(2,1)S(1)}, u32[]{:S(2)}, u32[]{:S(2)}) collective-permute-start(bf16[128,256]{1,0:T(8,128)(2,1)S(1)} %add_convert_fusion.3), channel_id=1, source_target_pairs={{0,8},{1,9},{2,10},{3,11},{4,12},{5,13},{6,14},{7,15},{8,0},{9,1},... | collective-permute-start | bytes 196616 | tf_op jit(solution)/shard_map/ppermute | solution.py:250
  28.1 5.8 %collective-permute-start.7 = (bf16[256,256]{1,0:T(8,128)(2,1)S(1)}, bf16[256,256]{1,0:T(8,128)(2,1)S(1)}, u32[]{:S(2)}, u32[]{:S(2)}) collective-permute-start(bf16[256,256]{1,0:T(8,128)(2,1)S(1)} %add_convert_fusion.1), channel_id=1, source_target_pairs={{0,16},{1,17},{2,18},{3,19},{4,20},{5,21},{6,22},{7,23},{8,24},{9,... | collective-permute-start | bytes 393224 | tf_op jit(solution)/shard_map/ppermute | solution.py:250
  31.1 5.9 %collective-permute-start.12 = (bf16[128,256]{1,0:T(8,128)(2,1)S(1)}, bf16[128,256]{1,0:T(8,128)(2,1)S(1)}, u32[]{:S(2)}, u32[]{:S(2)}) collective-permute-start(bf16[128,256]{1,0:T(8,128)(2,1)S(1)} %add_convert_fusion.2), channel_id=1, source_target_pairs={{0,7},{1,2},{2,1},{3,4},{4,3},{5,6},{6,5},{7,0},{8,15},{9,10},{10,... | collective-permute-start | bytes 196616 | tf_op jit(solution)/shard_map/ppermute | solution.py:250
  34.0 4.3 %collective-permute-start.8 = (bf16[128,256]{1,0:T(8,128)(2,1)S(1)}, bf16[128,256]{1,0:T(8,128)(2,1)S(1)}, u32[]{:S(2)}, u32[]{:S(2)}) collective-permute-start(bf16[128,256]{1,0:T(8,128)(2,1)S(1)} %slice.58), channel_id=1, source_target_pairs={{0,8},{1,9},{2,10},{3,11},{4,12},{5,13},{6,14},{7,15},{8,0},{9,1},... | collective-permute-start | bytes 196616 | tf_op jit(solution)/shard_map/ppermute | solution.py:250

commit v8 on v7

--- a/solution.py
+++ b/solution.py
@@ -62,14 +62,19 @@
 def attend_group(refs, rows, count, hidden, mask, qs, m_in, m_ref, w_ref, s_ref, finish):
     big = qs.shape[0]
     pair = min(big, 2 * HEAD)
-    ks = [load(refs, rows, u, 0) for u in range(count)]
+    ks = []
+    for u in range(count):
+        scaled = load(refs, rows, u, 0).astype(F32) * C2
+        high = scaled.astype(BF16)
+        ks.append(jnp.concatenate([high, (scaled - high.astype(F32)).astype(BF16)], axis=1))
     keys = ks[0].shape[0]
     ones = jnp.ones((16, keys), BF16)
     for c in range(0, big, pair):
         cols = slice(c, c + pair)
         top = m_in[:, cols] if m_in is not None else jnp.full((1, pair), NEG_FILL, F32)
+        q2 = jnp.concatenate([qs[cols, :], qs[cols, :]], axis=1)
         for u, k in enumerate(ks):
-            s = dot_nt(k, qs[cols, :]) * C2
+            s = dot_nt(k, q2)
             if u == 0 and mask is not None:
                 s = jnp.where(mask, s, NEG_FILL)
             s_ref[u, :, cols] = s

time: 39.1 us -> 39.1 us (level)
  no operation moved by 1% of the time
where the time goes in v8:
time: 39.1 us; the launch traced here: 38.9 us
  starting transfers between devices  17.2 us (44%)
  waiting for transfers between devices  13.1 us (34%)
  Pallas kernels  5.94 us (15%)
  other arithmetic  1.65 us (4%)
  between operations  0.83 us (2%)
    ppermute x13, starting transfers between devices, send(): return lax.ppermute(block, ('grp', 'blk'), route)  17.2 us
    ppermute x13, waiting for transfers between devices, send(): return lax.ppermute(block, ('grp', 'blk'), route)  13.1 us
    pallas_call x7, Pallas kernels, call(): pl.pallas_call(kernel, out_shape=outs, in_specs=[VMEM] * len(args), out_s...  5.94 us
    concatenate x1, other arithmetic, step(): own = lax.optimization_barrier(jnp.concatenate([key_rows, values], axis=1))  0.83 us
  transfers between devices with their start and end apart: 13, of which 8 were waited for; matrix products, arithmetic and copies ran while one was open for 1% of the time, Pallas kernels for 9%

profile of v8, /device:TPU:0, one launch (start us, length us, event | category | flops | bytes accessed | tf_op | source)
XLA Modules:
  0.0 38.9 jit_solution(2687527831048450493)
XLA Ops:
  0.6 0.8 %pad_maximum_fusion.2 = bf16[128,256]{1,0:T(8,128)(2,1)S(1)} fusion(bf16[128,128]{1,0:T(8,128)(2,1)} %param.7, bf16[128,128]{1,0:T(8,128)(2,1)} %param.6), kind=kLoop, calls=%fused_computation.8 | loop fusion | flops 131072 | bytes 131072 | tf_op jit(solution)/shard_map/concatenate | solution.py:275
  1.5 3.1 %collective-permute-start.3 = (bf16[128,256]{1,0:T(8,128)(2,1)S(1)}, bf16[128,256]{1,0:T(8,128)(2,1)S(1)}, u32[]{:S(2)}, u32[]{:S(2)}) collective-permute-start(bf16[128,256]{1,0:T(8,128)(2,1)S(1)} %pad_maximum_fusion.2), channel_id=1, source_target_pairs={{0,16},{1,17},{2,18},{3,19},{4,20},{5,21},{6,22},{7,23},{8,24},{9,... | collective-permute-start | bytes 196616 | tf_op jit(solution)/shard_map/ppermute | solution.py:255
  4.5 2.8 %collective-permute-start = (bf16[128,256]{1,0:T(8,128)(2,1)S(1)}, bf16[128,256]{1,0:T(8,128)(2,1)S(1)}, u32[]{:S(2)}, u32[]{:S(2)}) collective-permute-start(bf16[128,256]{1,0:T(8,128)(2,1)S(1)} %pad_maximum_fusion.2), channel_id=1, source_target_pairs={{0,7},{1,2},{2,1},{3,4},{4,3},{5,6},{6,5},{7,0},{8,15},{9,10},{10,... | collective-permute-start | bytes 196616 | tf_op jit(solution)/shard_map/ppermute | solution.py:255
  7.5 1.6 %collective-permute-start.4 = (bf16[256,256]{1,0:T(8,128)(2,1)S(1)}, bf16[256,256]{1,0:T(8,128)(2,1)S(1)}, u32[]{:S(2)}, u32[]{:S(2)}) collective-permute-start(bf16[256,256]{1,0:T(8,128)(2,1)S(1)} %pad_maximum_fusion.1.refs_0_.refs_9_.refs_2_), channel_id=1, source_target_pairs={{0,8},{1,9},{2,10},{3,11},{4,12},{5,13},{6,14},{7,15},{8,0},{9,1},... | collective-permute-start | bytes 393224 | tf_op jit(solution)/shard_map/ppermute | solution.py:255
  9.0 1.4 %collective-permute-done = bf16[128,256]{1,0:T(8,128)(2,1)S(1)} collective-permute-done((bf16[128,256]{1,0:T(8,128)(2,1)S(1)}, bf16[128,256]{1,0:T(8,128)(2,1)S(1)}, u32[]{:S(2)}, u32[]{:S(2)}) %collective-permute-start) | collective-permute-done | bytes 65568 | tf_op jit(solution)/shard_map/ppermute | solution.py:255
  10.4 4.3 %collective-permute-done.1 = bf16[128,256]{1,0:T(8,128)(2,1)S(1)} collective-permute-done((bf16[128,256]{1,0:T(8,128)(2,1)S(1)}, bf16[128,256]{1,0:T(8,128)(2,1)S(1)}, u32[]{:S(2)}, u32[]{:S(2)}) %collective-permute-start.1) | collective-permute-done | bytes 65568 | tf_op jit(solution)/shard_map/ppermute | solution.py:255
  14.7 1.6 %collective-permute-start.2 = (bf16[256,256]{1,0:T(8,128)(2,1)S(1)}, bf16[256,256]{1,0:T(8,128)(2,1)S(1)}, u32[]{:S(2)}, u32[]{:S(2)}) collective-permute-start(bf16[256,256]{1,0:T(8,128)(2,1)S(1)} %constant_dynamic-update-slice_fusion.refs_0_.refs_2_), channel_id=1, source_target_pairs={{0,8},{1,9},{2,10},{3,11},{4,12},{5,13},{6,14},{7,15},{8,0},{9,1},... | collective-permute-start | bytes 393224 | tf_op jit(solution)/shard_map/ppermute | solution.py:255
  16.3 0.7 %shard_map.84 = (f32[128,1024]{1,0:T(8,128)S(1)}, f32[1,1024]{1,0:T(1,128)S(1)}, f32[1,1024]{1,0:T(1,128)S(1)}, bf16[512,1024]{1,0:T(8,128)(2,1)S(1)}) custom-call(s32[8,8]{1,0:T(8,128)S(1)} %broadcast_in_dim.2.span_ref, bf16[1024,128]{1,0:T(8,128)(2,1)S(1)} %bitcast.16, bf16[256,256]{1,0:T(8,128)(2,1)S(1)} %pad_maximum_fusion.1.refs_0_.refs_9_.refs_2_, ...), custom_call_target="tpu_custom_call" | custom-call | flops 536870912 | bytes 1048576 | tf_op jit(solution)/shard_map/pallas_call | solution.py:225
  17.0 0.8 %collective-permute-done.5.refs_0_.refs_6_ = bf16[512,256]{1,0:T(8,128)(2,1)S(1)} collective-permute-done((bf16[512,256]{1,0:T(8,128)(2,1)S(1)}, bf16[512,256]{1,0:T(8,128)(2,1)S(1)}, u32[]{:S(2)}, u32[]{:S(2)}) %collective-permute-start.5) | collective-permute-done | bytes 262176 | tf_op jit(solution)/shard_map/ppermute | solution.py:255
  17.8 0.7 %shard_map.85 = (f32[128,1024]{1,0:T(8,128)S(1)}, f32[1,1024]{1,0:T(1,128)S(1)}, f32[1,1024]{1,0:T(1,128)S(1)}, bf16[512,1024]{1,0:T(8,128)(2,1)S(1)}) custom-call(s32[8,8]{1,0:T(8,128)S(1)} %broadcast_in_dim.2.span_ref, bf16[1024,128]{1,0:T(8,128)(2,1)S(1)} %bitcast.17, bf16[512,256]{1,0:T(8,128)(2,1)S(1)} %collective-permute-done.5.refs_0_.refs_6_, ...), custom_call_target="tpu_custom_call" | custom-call | flops 536870912 | bytes 1048576 | tf_op jit(solution)/shard_map/pallas_call | solution.py:225
  18.6 1.1 %collective-permute-done.2.refs_1_.refs_3_ = bf16[256,256]{1,0:T(8,128)(2,1)S(1)} collective-permute-done((bf16[256,256]{1,0:T(8,128)(2,1)S(1)}, bf16[256,256]{1,0:T(8,128)(2,1)S(1)}, u32[]{:S(2)}, u32[]{:S(2)}) %collective-permute-start.2) | collective-permute-done | bytes 131104 | tf_op jit(solution)/shard_map/ppermute | solution.py:255
  19.7 1.1 %shard_map.86 = (bf16[128,1024]{1,0:T(8,128)(2,1)S(1)}, bf16[512,1024]{1,0:T(8,128)(2,1)S(1)}, f32[1,1024]{1,0:T(1,128)S(1)}, f32[1,1024]{1,0:T(1,128)S(1)}, f32...) custom-call(s32[8,8]{1,0:T(8,128)S(1)} %broadcast_in_dim.2.span_ref, bf16[1024,128]{1,0:T(8,128)(2,1)S(1)} %bitcast.18, ...), custom_call_target="tpu_custom_call" | custom-call | flops 536870912 | bytes 1048576 | tf_op jit(solution)/shard_map/pallas_call | solution.py:225
  20.8 1.2 %shard_map.87 = (bf16[256,256]{1,0:T(8,128)(2,1)S(1)}, bf16[256,256]{1,0:T(8,128)(2,1)S(1)}, bf16[512,256]{1,0:T(8,128)(2,1)S(1)}, f32[128,1024]{1,0:T(8,128)S(1)}) custom-call(bf16[1024,128]{1,0:T(8,128)(2,1)S(1)} %bitcast.19, bf16[1024,128]{1,0:T(8,128)(2,1)S(1)} %bitcast.24, f32[1,1024]{1,0:T(1,128)S(1)} %get-tuple-element.37.delta_ref, ...), custom_call_target="tpu_custom_call" | custom-call | flops 805306368 | bytes 1048576 | tf_op jit(solution)/shard_map/pallas_call | solution.py:225
  22.0 2.0 %collective-permute-start.11 = (bf16[128,256]{1,0:T(8,128)(2,1)S(1)}, bf16[128,256]{1,0:T(8,128)(2,1)S(1)}, u32[]{:S(2)}, u32[]{:S(2)}) collective-permute-start(bf16[128,256]{1,0:T(8,128)(2,1)S(1)} %get-tuple-element.61), channel_id=1, source_target_pairs={{0,16},{1,17},{2,18},{3,19},{4,20},{5,21},{6,22},{7,23},{8,24},{9,... | collective-permute-start | bytes 196616 | tf_op jit(solution)/shard_map/ppermute | solution.py:255
  24.1 0.8 %shard_map.88 = (bf16[256,256]{1,0:T(8,128)(2,1)S(1)}, bf16[512,256]{1,0:T(8,128)(2,1)S(1)}, bf16[256,256]{1,0:T(8,128)(2,1)S(1)}, f32[128,1024]{1,0:T(8,128)S(1)}) custom-call(bf16[1024,128]{1,0:T(8,128)(2,1)S(1)} %bitcast.20, bf16[1024,128]{1,0:T(8,128)(2,1)S(1)} %bitcast.25, ...), custom_call_target="tpu_custom_call", output_to_operand_aliasing={{0}: (14, {}), {1}: (15, {}), {3}: (16, {})} | custom-call | flops 1073741824 | bytes 1048576 | tf_op jit(solution)/shard_map/pallas_call | solution.py:225
  25.0 1.4 %shard_map.90 = (bf16[256,256]{1,0:T(8,128)(2,1)S(1)}, bf16[128,1024]{1,0:T(8,128)(2,1)}, bf16[128,1024]{1,0:T(8,128)(2,1)}) custom-call(bf16[1024,128]{1,0:T(8,128)(2,1)S(1)} %bitcast.22, bf16[1024,128]{1,0:T(8,128)(2,1)S(1)} %bitcast.27, f32[1,1024]{1,0:T(1,128)S(1)} %get-tuple-element.37.delta_ref, ...), custom_call_target="tpu_custom_call", output_to_operand_aliasing={{0}: (8, {})} | custom-call | flops 268435456 | bytes 1048576 | tf_op jit(solution)/shard_map/pallas_call | solution.py:225
  26.5 1.6 %collective-permute-start.10 = (bf16[128,256]{1,0:T(8,128)(2,1)S(1)}, bf16[128,256]{1,0:T(8,128)(2,1)S(1)}, u32[]{:S(2)}, u32[]{:S(2)}) collective-permute-start(bf16[128,256]{1,0:T(8,128)(2,1)S(1)} %add_convert_fusion.3), channel_id=1, source_target_pairs={{0,8},{1,9},{2,10},{3,11},{4,12},{5,13},{6,14},{7,15},{8,0},{9,1},... | collective-permute-start | bytes 196616 | tf_op jit(solution)/shard_map/ppermute | solution.py:255
  28.1 1.9 %collective-permute-start.7 = (bf16[256,256]{1,0:T(8,128)(2,1)S(1)}, bf16[256,256]{1,0:T(8,128)(2,1)S(1)}, u32[]{:S(2)}, u32[]{:S(2)}) collective-permute-start(bf16[256,256]{1,0:T(8,128)(2,1)S(1)} %add_convert_fusion.1), channel_id=1, source_target_pairs={{0,16},{1,17},{2,18},{3,19},{4,20},{5,21},{6,22},{7,23},{8,24},{9,... | collective-permute-start | bytes 393224 | tf_op jit(solution)/shard_map/ppermute | solution.py:255
  30.0 1.0 %collective-permute-done.10 = bf16[128,256]{1,0:T(8,128)(2,1)S(1)} collective-permute-done((bf16[128,256]{1,0:T(8,128)(2,1)S(1)}, bf16[128,256]{1,0:T(8,128)(2,1)S(1)}, u32[]{:S(2)}, u32[]{:S(2)}) %collective-permute-start.10) | collective-permute-done | bytes 65568 | tf_op jit(solution)/shard_map/ppermute | solution.py:255
  31.0 2.1 %collective-permute-start.12 = (bf16[128,256]{1,0:T(8,128)(2,1)S(1)}, bf16[128,256]{1,0:T(8,128)(2,1)S(1)}, u32[]{:S(2)}, u32[]{:S(2)}) collective-permute-start(bf16[128,256]{1,0:T(8,128)(2,1)S(1)} %add_convert_fusion.2), channel_id=1, source_target_pairs={{0,7},{1,2},{2,1},{3,4},{4,3},{5,6},{6,5},{7,0},{8,15},{9,10},{10,... | collective-permute-start | bytes 196616 | tf_op jit(solution)/shard_map/ppermute | solution.py:255
  33.2 0.7 %collective-permute-done.7 = bf16[256,256]{1,0:T(8,128)(2,1)S(1)} collective-permute-done((bf16[256,256]{1,0:T(8,128)(2,1)S(1)}, bf16[256,256]{1,0:T(8,128)(2,1)S(1)}, u32[]{:S(2)}, u32[]{:S(2)}) %collective-permute-start.7) | collective-permute-done | bytes 131104 | tf_op jit(solution)/shard_map/ppermute | solution.py:255
  34.4 2.5 %collective-permute-done.12 = bf16[128,256]{1,0:T(8,128)(2,1)S(1)} collective-permute-done((bf16[128,256]{1,0:T(8,128)(2,1)S(1)}, bf16[128,256]{1,0:T(8,128)(2,1)S(1)}, u32[]{:S(2)}, u32[]{:S(2)}) %collective-permute-start.12) | collective-permute-done | bytes 65568 | tf_op jit(solution)/shard_map/ppermute | solution.py:255
  36.9 1.4 %collective-permute-done.8 = bf16[128,256]{1,0:T(8,128)(2,1)S(1)} collective-permute-done((bf16[128,256]{1,0:T(8,128)(2,1)S(1)}, bf16[128,256]{1,0:T(8,128)(2,1)S(1)}, u32[]{:S(2)}, u32[]{:S(2)}) %collective-permute-start.8) | collective-permute-done | bytes 65568 | tf_op jit(solution)/shard_map/ppermute | solution.py:255
  38.3 0.7 %add_convert_fusion.4 = (bf16[128,128]{1,0:T(8,128)(2,1)}, bf16[128,128]{1,0:T(8,128)(2,1)}) fusion(bf16[128,256]{1,0:T(8,128)(2,1)S(1)} %collective-permute-done.12, bf16[128,256]{1,0:T(8,128)(2,1)S(1)} %collective-permute-done.8, bf16[256,256]{1,0:T(8,128)(2,1)S(1)} %add_convert_fusion), kind=kLoop, calls=%fused_computation.9 | loop fusion | flops 196608 | bytes 262144 | tf_op jit(solution)/shard_map/convert_element_type | solution.py:368
  (31 shorter events, 1.1 us)
Async XLA Ops:
  0.6 6.7 %copy-start = (bf16[128,1024]{1,0:T(8,128)(2,1)S(1)}, bf16[128,1024]{1,0:T(8,128)(2,1)}, u32[]{:S(2)}) copy-start(bf16[128,1024]{1,0:T(8,128)(2,1)} %param.5) | copy-start | bytes 786436
  1.5 5.9 %copy-start.1 = (bf16[128,1024]{1,0:T(8,128)(2,1)S(1)}, bf16[128,1024]{1,0:T(8,128)(2,1)}, u32[]{:S(2)}) copy-start(bf16[128,1024]{1,0:T(8,128)(2,1)} %param.8) | copy-start | bytes 786436
  1.5 5.9 %collective-permute-start.3 = (bf16[128,256]{1,0:T(8,128)(2,1)S(1)}, bf16[128,256]{1,0:T(8,128)(2,1)S(1)}, u32[]{:S(2)}, u32[]{:S(2)}) collective-permute-start(bf16[128,256]{1,0:T(8,128)(2,1)S(1)} %pad_maximum_fusion.2), channel_id=1, source_target_pairs={{0,16},{1,17},{2,18},{3,19},{4,20},{5,21},{6,22},{7,23},{8,24},{9,... | collective-permute-start | bytes 196616 | tf_op jit(solution)/shard_map/ppermute | solution.py:255
  4.5 5.8 %collective-permute-start = (bf16[128,256]{1,0:T(8,128)(2,1)S(1)}, bf16[128,256]{1,0:T(8,128)(2,1)S(1)}, u32[]{:S(2)}, u32[]{:S(2)}) collective-permute-start(bf16[128,256]{1,0:T(8,128)(2,1)S(1)} %pad_maximum_fusion.2), channel_id=1, source_target_pairs={{0,7},{1,2},{2,1},{3,4},{4,3},{5,6},{6,5},{7,0},{8,15},{9,10},{10,... | collective-permute-start | bytes 196616 | tf_op jit(solution)/shard_map/ppermute | solution.py:255
  7.5 8.8 %collective-permute-start.4 = (bf16[256,256]{1,0:T(8,128)(2,1)S(1)}, bf16[256,256]{1,0:T(8,128)(2,1)S(1)}, u32[]{:S(2)}, u32[]{:S(2)}) collective-permute-start(bf16[256,256]{1,0:T(8,128)(2,1)S(1)} %pad_maximum_fusion.1.refs_0_.refs_9_.refs_2_), channel_id=1, source_target_pairs={{0,8},{1,9},{2,10},{3,11},{4,12},{5,13},{6,14},{7,15},{8,0},{9,1},... | collective-permute-start | bytes 393224 | tf_op jit(solution)/shard_map/ppermute | solution.py:255
  10.4 4.3 %collective-permute-start.1 = (bf16[128,256]{1,0:T(8,128)(2,1)S(1)}, bf16[128,256]{1,0:T(8,128)(2,1)S(1)}, u32[]{:S(2)}, u32[]{:S(2)}) collective-permute-start(bf16[128,256]{1,0:T(8,128)(2,1)S(1)} %collective-permute-done), channel_id=1, source_target_pairs={{0,16},{1,17},{2,18},{3,19},{4,20},{5,21},{6,22},{7,23},{8,24},{9,... | collective-permute-start | bytes 196616 | tf_op jit(solution)/shard_map/ppermute | solution.py:255
  14.6 1.7 %copy-start.2 = (s32[8]{0:T(128)S(1)}, s32[8]{0:T(128)}, u32[]{:S(2)}) copy-start(s32[8]{0:T(128)} %param.9) | copy-start | bytes 100
  14.7 5.0 %collective-permute-start.2 = (bf16[256,256]{1,0:T(8,128)(2,1)S(1)}, bf16[256,256]{1,0:T(8,128)(2,1)S(1)}, u32[]{:S(2)}, u32[]{:S(2)}) collective-permute-start(bf16[256,256]{1,0:T(8,128)(2,1)S(1)} %constant_dynamic-update-slice_fusion.refs_0_.refs_2_), channel_id=1, source_target_pairs={{0,8},{1,9},{2,10},{3,11},{4,12},{5,13},{6,14},{7,15},{8,0},{9,1},... | collective-permute-start | bytes 393224 | tf_op jit(solution)/shard_map/ppermute | solution.py:255
  16.2 1.6 %collective-permute-start.5 = (bf16[512,256]{1,0:T(8,128)(2,1)S(1)}, bf16[512,256]{1,0:T(8,128)(2,1)S(1)}, u32[]{:S(2)}, u32[]{:S(2)}) collective-permute-start(bf16[512,256]{1,0:T(8,128)(2,1)S(1)} %pad_maximum_fusion), channel_id=1, source_target_pairs={{0,1},{1,0},{2,3},{3,2},{4,5},{5,4},{6,7},{7,6},{8,9},{9,8},{10,11... | collective-permute-start | bytes 786440 | tf_op jit(solution)/shard_map/ppermute | solution.py:255
  22.0 4.5 %collective-permute-start.9 = (bf16[128,256]{1,0:T(8,128)(2,1)S(1)}, bf16[128,256]{1,0:T(8,128)(2,1)S(1)}, u32[]{:S(2)}, u32[]{:S(2)}) collective-permute-start(bf16[128,256]{1,0:T(8,128)(2,1)S(1)} %get-tuple-element.60), channel_id=1, source_target_pairs={{0,16},{1,17},{2,18},{3,19},{4,20},{5,21},{6,22},{7,23},{8,24},{9,... | collective-permute-start | bytes 196616 | tf_op jit(solution)/shard_map/ppermute | solution.py:255
  22.0 8.0 %collective-permute-start.11 = (bf16[128,256]{1,0:T(8,128)(2,1)S(1)}, bf16[128,256]{1,0:T(8,128)(2,1)S(1)}, u32[]{:S(2)}, u32[]{:S(2)}) collective-permute-start(bf16[128,256]{1,0:T(8,128)(2,1)S(1)} %get-tuple-element.61), channel_id=1, source_target_pairs={{0,16},{1,17},{2,18},{3,19},{4,20},{5,21},{6,22},{7,23},{8,24},{9,... | collective-permute-start | bytes 196616 | tf_op jit(solution)/shard_map/ppermute | solution.py:255
  24.8 3.2 %collective-permute-start.6 = (bf16[512,256]{1,0:T(8,128)(2,1)S(1)}, bf16[512,256]{1,0:T(8,128)(2,1)S(1)}, u32[]{:S(2)}, u32[]{:S(2)}) collective-permute-start(bf16[512,256]{1,0:T(8,128)(2,1)S(1)} %get-tuple-element.54), channel_id=1, source_target_pairs={{0,1},{1,0},{2,3},{3,2},{4,5},{5,4},{6,7},{7,6},{8,9},{9,8},{10,11... | collective-permute-start | bytes 786440 | tf_op jit(solution)/shard_map/ppermute | solution.py:255
  26.5 4.5 %collective-permute-start.10 = (bf16[128,256]{1,0:T(8,128)(2,1)S(1)}, bf16[128,256]{1,0:T(8,128)(2,1)S(1)}, u32[]{:S(2)}, u32[]{:S(2)}) collective-permute-start(bf16[128,256]{1,0:T(8,128)(2,1)S(1)} %add_convert_fusion.3), channel_id=1, source_target_pairs={{0,8},{1,9},{2,10},{3,11},{4,12},{5,13},{6,14},{7,15},{8,0},{9,1},... | collective-permute-start | bytes 196616 | tf_op jit(solution)/shard_map/ppermute | solution.py:255
  28.1 5.8 %collective-permute-start.7 = (bf16[256,256]{1,0:T(8,128)(2,1)S(1)}, bf16[256,256]{1,0:T(8,128)(2,1)S(1)}, u32[]{:S(2)}, u32[]{:S(2)}) collective-permute-start(bf16[256,256]{1,0:T(8,128)(2,1)S(1)} %add_convert_fusion.1), channel_id=1, source_target_pairs={{0,16},{1,17},{2,18},{3,19},{4,20},{5,21},{6,22},{7,23},{8,24},{9,... | collective-permute-start | bytes 393224 | tf_op jit(solution)/shard_map/ppermute | solution.py:255
  31.0 5.9 %collective-permute-start.12 = (bf16[128,256]{1,0:T(8,128)(2,1)S(1)}, bf16[128,256]{1,0:T(8,128)(2,1)S(1)}, u32[]{:S(2)}, u32[]{:S(2)}) collective-permute-start(bf16[128,256]{1,0:T(8,128)(2,1)S(1)} %add_convert_fusion.2), channel_id=1, source_target_pairs={{0,7},{1,2},{2,1},{3,4},{4,3},{5,6},{6,5},{7,0},{8,15},{9,10},{10,... | collective-permute-start | bytes 196616 | tf_op jit(solution)/shard_map/ppermute | solution.py:255
  34.0 4.3 %collective-permute-start.8 = (bf16[128,256]{1,0:T(8,128)(2,1)S(1)}, bf16[128,256]{1,0:T(8,128)(2,1)S(1)}, u32[]{:S(2)}, u32[]{:S(2)}) collective-permute-start(bf16[128,256]{1,0:T(8,128)(2,1)S(1)} %slice.58), channel_id=1, source_target_pairs={{0,8},{1,9},{2,10},{3,11},{4,12},{5,13},{6,14},{7,15},{8,0},{9,1},... | collective-permute-start | bytes 196616 | tf_op jit(solution)/shard_map/ppermute | solution.py:255
